TPU v7x, 32 devices: a whole 2x2x4 slice. The times are simulated.
32 devices in a mesh: dp: 8 (over z, y), tensor: 4 (over x, core).
Axes of the slice: x: 2, y: 2, z: 4, core: 2. Of those that a mesh axis runs over, the one named last changes fastest.
Arguments:
- tokens: bfloat16 [16384, 1024], P(('dp', 'tensor')), may hold values from -6 to 6
- grad_out: bfloat16 [16384, 1024], P(('dp', 'tensor')), may hold values from -6 to 6
- lengths: int32 [8, 10], P('dp'), may hold values from 0 to 1568, as said below
- coords: int32 [3, 16384], P(None, 'dp'), may hold values from 0 to 20, as said below
- w_qkv: bfloat16 [3, 1024, 1024], P(None, None, 'tensor'), may hold values from -0.1875 to 0.1875
- b_qkv: bfloat16 [3, 1024], P(None, 'tensor'), may hold values from -1.796875 to 1.796875
- w_proj: bfloat16 [1024, 1024], P('tensor'), may hold values from -1.5 to 1.5
- w_fc1: bfloat16 [1024, 4096], P(None, 'tensor'), may hold values from -0.1875 to 0.1875
- b_fc1: bfloat16 [4096], P('tensor'), may hold values from -1.796875 to 1.796875
- w_fc2: bfloat16 [4096, 1024], P('tensor'), may hold values from -0.09375 to 0.09375
- norm_gains: bfloat16 [2, 1024], replicated, may hold values from 0.5 to 1.5
- shift_biases: bfloat16 [4, 1024], replicated, may hold values from -1.796875 to 1.796875
Outputs:
- output: bfloat16 [16384, 1024], P(('dp', 'tensor'))
- grad_tokens: bfloat16 [16384, 1024], P(('dp', 'tensor'))
- grad_w_qkv: float32 [3, 1024, 1024], P(None, None, 'tensor')
- grad_b_qkv: float32 [3, 1024], P(None, 'tensor')
- grad_w_proj: float32 [1024, 1024], P('tensor')
- grad_w_fc1: float32 [1024, 4096], P(None, 'tensor')
- grad_b_fc1: float32 [4096], P('tensor')
- grad_w_fc2: float32 [4096, 1024], P('tensor')
- grad_norm_gains: float32 [2, 1024], replicated
- grad_shift_biases: float32 [4, 1024], replicated
Inputs may be any that keep to these rules, and one draw needn't show every extreme that they name: `lengths`: each row lists one group's sequences: at most one video of 1568 tokens in slot 0, then images of 196 tokens, then empty slots of 0; a row sums to at most 2048; row 0 holds a video. `coords`: A token's coordinates are its tubelet's frame pair, row and column within its sequence on a 14 x 14 grid, each plus an offset of 0 to 7 drawn for the sequence and axis; padding tokens have 0.
All inputs are finite; a program needn't handle non-finite values.
Results may differ from a plain program's by a relative error of at most 0.018.
Values may be sent and summed in bfloat16 or wider, within the bound.
No kernel may reach another device: no remote copies, remote signals or barrier semaphores. Data moves between devices by JAX's collectives and lax.ppermute only.
A program may use at most 192 MiB of HBM per device.

v0:
```python
from functools import partial

import jax
import jax.numpy as jnp
from jax import lax
from jax.sharding import PartitionSpec as P

HDIM = 64


def norm_rows(values_in, gain_row, shift_row):
    row_mean = jnp.mean(values_in, axis=-1, keepdims=True)
    centred = values_in - row_mean
    variance = jnp.mean(centred * centred, axis=-1, keepdims=True)
    return centred * lax.rsqrt(variance + 1e-06) * gain_row + shift_row


def segment_of(lengths_row, count):
    seq_ends = jnp.cumsum(lengths_row)
    places = jnp.arange(count, dtype=jnp.int32)
    seg_ids = jnp.sum((places[:, None] >= seq_ends[None, :]).astype(jnp.int32), axis=1)
    return (seg_ids, places < seq_ends[-1])


def angle_table(coords_grp, half_dim):
    pair_ids = jnp.arange(half_dim)
    frequency = 100.0 ** (-(pair_ids // 3).astype(jnp.float32) / (half_dim // 3 + 1))
    angles = jnp.zeros((coords_grp.shape[1], half_dim), jnp.float32)
    for axis_id in range(3):
        chosen = jnp.where(pair_ids % 3 == axis_id, frequency, 0.0)
        angles = angles + coords_grp[axis_id].astype(jnp.float32)[:, None] * chosen[None, :]
    return (jnp.cos(angles), jnp.sin(angles))


def rotate(heads_in, cosine, sine):
    half_dim = heads_in.shape[-1] // 2
    first_half = heads_in[..., :half_dim]
    second_half = heads_in[..., half_dim:]
    return jnp.concatenate(
        [first_half * cosine - second_half * sine, first_half * sine + second_half * cosine],
        axis=-1,
    )


def rounded(values_in):
    return values_in.astype(jnp.bfloat16).astype(jnp.float32)


def shards(
    tokens,
    grad_out,
    lengths,
    coords,
    w_qkv,
    b_qkv,
    w_proj,
    w_fc1,
    b_fc1,
    w_fc2,
    norm_gains,
    shift_biases,
):
    f32 = jnp.float32
    bf16 = jnp.bfloat16
    tok_dev = tokens.shape[0]
    group_rows = tok_dev * lax.axis_size("tensor")
    head_cols = w_qkv.shape[2]
    heads_dev = head_cols // HDIM
    score_scale = HDIM ** (-0.5)
    block_rows = min(512, group_rows)
    nblocks = group_rows // block_rows
    seg_ids, live_grp = segment_of(lengths[0], group_rows)
    own_start = lax.axis_index("tensor") * tok_dev
    live_mine = lax.dynamic_slice_in_dim(live_grp, own_start, tok_dev, 0).astype(f32)
    cosine, sine = angle_table(coords, HDIM // 2)
    cosine = cosine[:, None, :]
    sine = sine[:, None, :]
    gains = norm_gains.astype(f32)
    shifts = shift_biases.astype(f32)
    x_rows = tokens.astype(f32)
    normed_one, norm_one_back = jax.vjp(norm_rows, x_rows, gains[0], shifts[0])
    all_one = lax.all_gather(normed_one.astype(bf16), "tensor", axis=0, tiled=True)
    projected = (
        jnp.einsum("td,cde->cte", all_one, w_qkv, preferred_element_type=f32)
        + b_qkv.astype(f32)[:, None, :]
    )
    shaped = projected.reshape(3, group_rows, heads_dev, HDIM)

    def rope_pair(query_in, key_in):
        return (rotate(query_in, cosine, sine), rotate(key_in, cosine, sine))

    (query_rot, key_rot), rope_back = jax.vjp(rope_pair, shaped[0], shaped[1])
    query_low = query_rot.astype(bf16)
    key_low = key_rot.astype(bf16)
    value_low = shaped[2].astype(bf16)

    def block_scores(query_blk, seg_blk):
        scores = (
            jnp.einsum("qhd,khd->hqk", query_blk, key_low, preferred_element_type=f32) * score_scale
        )
        allowed = seg_blk[:, None] == seg_ids[None, :]
        return jnp.where(allowed[None], scores, -1e30)

    def attend_block(block_id):
        start_row = block_id * block_rows
        query_blk = lax.dynamic_slice_in_dim(query_low, start_row, block_rows, 0)
        seg_blk = lax.dynamic_slice_in_dim(seg_ids, start_row, block_rows, 0)
        scores = block_scores(query_blk, seg_blk)
        top_score = jnp.max(scores, axis=-1, keepdims=True)
        expd = jnp.exp(scores - top_score)
        total = jnp.sum(expd, axis=-1, keepdims=True)
        probs_low = (expd / total).astype(bf16)
        out_blk = jnp.einsum("hqk,khd->qhd", probs_low, value_low, preferred_element_type=f32)
        return (out_blk, (top_score + jnp.log(total))[..., 0])

    attended, log_sums = lax.map(attend_block, jnp.arange(nblocks))
    attn_low = attended.reshape(group_rows, head_cols).astype(bf16)
    picked = attn_low
    attn_part = lax.psum_scatter(
        rounded(jnp.dot(picked, w_proj, preferred_element_type=f32)).astype(jnp.bfloat16),
        "tensor",
        scatter_dimension=0,
        tiled=True,
    ).astype(jnp.float32)
    resid_one = x_rows + attn_part + shifts[2]
    normed_two, norm_two_back = jax.vjp(norm_rows, resid_one, gains[1], shifts[1])
    all_two = lax.all_gather(normed_two.astype(bf16), "tensor", axis=0, tiled=True)
    hidden_pre = jnp.dot(all_two, w_fc1, preferred_element_type=f32) + b_fc1.astype(f32)
    hidden_act, gelu_back = jax.vjp(partial(jax.nn.gelu, approximate=False), hidden_pre)
    hidden_low = hidden_act.astype(bf16)
    picked = lax.slice_in_dim(hidden_low, 0, tok_dev * lax.axis_size("tensor"), axis=0)
    mlp_part = lax.psum_scatter(
        rounded(jnp.dot(picked, w_fc2, preferred_element_type=f32)).astype(jnp.bfloat16),
        "tensor",
        scatter_dimension=0,
        tiled=True,
    ).astype(jnp.float32)
    output = (resid_one + mlp_part + shifts[3]).astype(bf16)
    grad_y = grad_out.astype(f32) * live_mine[:, None]
    grad_mlp = grad_y.astype(bf16)
    all_grad_mlp = lax.all_gather(grad_mlp, "tensor", axis=0, tiled=True)
    grad_w2 = jnp.einsum("tf,td->fd", hidden_low, all_grad_mlp, preferred_element_type=f32)
    grad_hidden = jnp.einsum("td,fd->tf", all_grad_mlp, w_fc2, preferred_element_type=f32)
    grad_pre = gelu_back(grad_hidden)[0].astype(bf16)
    grad_w1 = jnp.einsum("td,tf->df", all_two, grad_pre, preferred_element_type=f32)
    grad_b1 = jnp.sum(grad_pre, axis=0, dtype=f32)
    picked = grad_pre
    grad_normed_two = lax.psum_scatter(
        rounded(jnp.einsum("tf,df->td", picked, w_fc1, preferred_element_type=f32)).astype(
            jnp.bfloat16
        ),
        "tensor",
        scatter_dimension=0,
        tiled=True,
    ).astype(jnp.float32)
    grad_resid_two, grad_gain_two, grad_shift_two = norm_two_back(grad_normed_two)
    grad_resid_one = grad_y + grad_resid_two
    grad_attn = grad_resid_one.astype(bf16)
    all_grad_attn = lax.all_gather(grad_attn, "tensor", axis=0, tiled=True)
    grad_wproj = jnp.einsum("tc,td->cd", attn_low, all_grad_attn, preferred_element_type=f32)
    grad_heads = jnp.einsum("td,cd->tc", all_grad_attn, w_proj, preferred_element_type=f32).astype(
        bf16
    )
    grad_heads = grad_heads.reshape(group_rows, heads_dev, HDIM)

    def back_block(carry, items):
        grad_key, grad_value = carry
        block_id, lse_blk = items
        start_row = block_id * block_rows
        query_blk = lax.dynamic_slice_in_dim(query_low, start_row, block_rows, 0)
        seg_blk = lax.dynamic_slice_in_dim(seg_ids, start_row, block_rows, 0)
        grad_out_blk = lax.dynamic_slice_in_dim(grad_heads, start_row, block_rows, 0)
        scores = block_scores(query_blk, seg_blk)
        probs = jnp.exp(scores - lse_blk[..., None])
        grad_probs = jnp.einsum("qhd,khd->hqk", grad_out_blk, value_low, preferred_element_type=f32)
        inner = jnp.sum(grad_probs * probs, axis=-1, keepdims=True)
        grad_scores = (probs * (grad_probs - inner)).astype(bf16)
        grad_query_blk = (
            jnp.einsum("hqk,khd->qhd", grad_scores, key_low, preferred_element_type=f32)
            * score_scale
        )
        grad_key = (
            grad_key
            + jnp.einsum("hqk,qhd->khd", grad_scores, query_blk, preferred_element_type=f32)
            * score_scale
        )
        grad_value = grad_value + jnp.einsum(
            "hqk,qhd->khd", probs.astype(bf16), grad_out_blk, preferred_element_type=f32
        )
        return ((grad_key, grad_value), grad_query_blk)

    zeros_kv = jnp.zeros((group_rows, heads_dev, HDIM), f32)
    (grad_key, grad_value), grad_query = lax.scan(
        back_block, (zeros_kv, zeros_kv), (jnp.arange(nblocks), log_sums)
    )
    grad_query = grad_query.reshape(group_rows, heads_dev, HDIM)
    grad_q_pre, grad_k_pre = rope_back((grad_query, grad_key))
    grad_proj = (
        jnp.stack([grad_q_pre, grad_k_pre, grad_value])
        .reshape(3, group_rows, head_cols)
        .astype(bf16)
    )
    grad_wqkv = jnp.einsum("td,cte->cde", all_one, grad_proj, preferred_element_type=f32)
    grad_bqkv = jnp.sum(grad_proj, axis=1, dtype=f32)
    grad_wqkv, grad_bqkv, grad_wproj, grad_w1, grad_b1, grad_w2 = lax.psum(
        (grad_wqkv, grad_bqkv, grad_wproj, grad_w1, grad_b1, grad_w2), "dp"
    )
    picked = grad_proj
    grad_normed_one = lax.psum_scatter(
        rounded(jnp.einsum("cte,cde->td", picked, w_qkv, preferred_element_type=f32)).astype(
            jnp.bfloat16
        ),
        "tensor",
        scatter_dimension=0,
        tiled=True,
    ).astype(jnp.float32)
    grad_x_norm, grad_gain_one, grad_shift_one = norm_one_back(grad_normed_one)
    grad_tokens = (grad_resid_one + grad_x_norm).astype(bf16)
    gain_terms = jnp.stack([grad_gain_one, grad_gain_two])
    shift_terms = jnp.stack(
        [
            grad_shift_one,
            grad_shift_two,
            jnp.sum(grad_attn, axis=0, dtype=f32),
            jnp.sum(grad_mlp, axis=0, dtype=f32),
        ]
    )
    grad_gains, grad_shifts = lax.psum((gain_terms, shift_terms), ("dp", "tensor"))
    return (
        output,
        grad_tokens,
        grad_wqkv,
        grad_bqkv,
        grad_wproj,
        grad_w1,
        grad_b1,
        grad_w2,
        grad_gains,
        grad_shifts,
    )


def solution(mesh):
    return jax.shard_map(
        shards,
        mesh=mesh,
        in_specs=(
            P(("dp", "tensor"), None),
            P(("dp", "tensor"), None),
            P("dp", None),
            P(None, "dp"),
            P(None, None, "tensor"),
            P(None, "tensor"),
            P("tensor", None),
            P(None, "tensor"),
            P("tensor"),
            P("tensor", None),
            P(),
            P(),
        ),
        out_specs=(
            P(("dp", "tensor"), None),
            P(("dp", "tensor"), None),
            P(None, None, "tensor"),
            P(None, "tensor"),
            P("tensor", None),
            P(None, "tensor"),
            P("tensor"),
            P("tensor", None),
            P(),
            P(),
        ),
        check_vma=False,
    )
```

profile of v0, /device:TPU:0, one launch (start us, length us, event | category | flops | bytes accessed | tf_op | source)
XLA Modules:
  0.0 1154.5 jit_solution(16145208967568466152)
XLA Ops:
  18.4 35.5 %all-gather.5.cloned.1.call-done = bf16[2048,1024]{1,0:T(8,128)(2,1)} async-done(((bf16[512,1024]{1,0:T(8,128)(2,1)}), bf16[2048,1024]{1,0:T(8,128)(2,1)}) %all-gather.5.cloned.1.call-update) | async-done | bytes 4194320 | tf_op jit(solution)/shard_map/all_gather | solution.py:82
  63.2 66.5 %while.27 = (s32[]{:T(128)}, bf16[4,512,4,64]{1,3,2,0:T(8,128)(2,1)}, f32[4,4,512]{2,1,0:T(4,128)}, s32[4]{0:T(128)S(1)}, s32[2048]{0:T(1024)S(1)}, /*index=5*/b...) while((s32[]{:T(128)}, ...), condition=%wide.region_7.8_spmd, body=%wide.region_4.7_spmd.sunk | while | flops 1125120000 | bytes 70072600 | solution.py:116
  136.8 44.4 %reduce-scatter.5.cloned.1.call-done = bf16[512,1024]{1,0:T(8,128)(2,1)} async-done(((bf16[2048,1024]{1,0:T(8,128)(2,1)}), bf16[512,1024]{1,0:T(8,128)(2,1)}) %reduce-scatter.5.cloned.1.call-update) | async-done | bytes 1048592 | tf_op jit(solution)/shard_map/reduce_scatter | solution.py:119
  191.6 30.1 %all-gather.7.cloned.1.call-done = bf16[2048,1024]{1,0:T(8,128)(2,1)} async-done(((bf16[512,1024]{1,0:T(8,128)(2,1)}), bf16[2048,1024]{1,0:T(8,128)(2,1)}) %all-gather.7.cloned.1.call-update) | async-done | bytes 4194320 | tf_op jit(solution)/shard_map/all_gather | solution.py:127
  221.7 11.4 fusion.87
  233.1 25.1 %all-gather.9.cloned.1.call-done = bf16[2048,1024]{1,0:T(8,128)(2,1)} async-done(((bf16[512,1024]{1,0:T(8,128)(2,1)}), bf16[2048,1024]{1,0:T(8,128)(2,1)}) %all-gather.9.cloned.1.call-update) | async-done | bytes 4194320 | tf_op jit(solution)/shard_map/all_gather | solution.py:141
  258.2 27.5 %convert_reduce_fusion = (f32[1024]{0:T(1024)}, bf16[2048,1024]{1,0:T(8,128)(2,1)S(1)}, f32[2048,1024]{1,0:T(8,128)}) fusion(f32[2048,1024]{1,0:T(8,128)} %fusion.87, f32[1024]{0:T(1024)S(1)} %convert_element_type.183, bf16[2048,1024]{1,0:T(8,128)(2,1)} %all-gather.9.cloned.1.call-done, bf16[1024,1024]{1,0:T(8,128)(2,1)S(1)} %copy-done), kind=kOutput, calls=%fused_computation.45 | convolution fusion | flops 4452252672 | bytes 27271168 | tf_op jit(solution)/shard_map/td,fd->tf/dot_general | solution.py:143
  294.5 10.8 multiply_convert_fusion.1
  305.2 8.3 convolution_convert_fusion.2
  313.7 25.0 %reduce-scatter.9.cloned.1.call-done = bf16[512,1024]{1,0:T(8,128)(2,1)} async-done(((bf16[2048,1024]{1,0:T(8,128)(2,1)}), bf16[512,1024]{1,0:T(8,128)(2,1)}) %reduce-scatter.9.cloned.1.call-update) | async-done | bytes 1048592 | tf_op jit(solution)/shard_map/reduce_scatter | solution.py:148
  341.6 44.1 %reduce-scatter.7.cloned.1.call-done = bf16[512,1024]{1,0:T(8,128)(2,1)} async-done(((bf16[2048,1024]{1,0:T(8,128)(2,1)}), bf16[512,1024]{1,0:T(8,128)(2,1)}) %reduce-scatter.7.cloned.1.call-update) | async-done | bytes 1048592 | tf_op jit(solution)/shard_map/reduce_scatter | solution.py:132
  392.9 34.5 %all-gather.11.cloned.1.call-done = bf16[2048,1024]{1,0:T(8,128)(2,1)} async-done(((bf16[512,1024]{1,0:T(8,128)(2,1)}), bf16[2048,1024]{1,0:T(8,128)(2,1)}) %all-gather.11.cloned.1.call-update) | async-done | bytes 4194320 | tf_op jit(solution)/shard_map/all_gather | solution.py:159
  431.9 237.7 %while.28 = (s32[]{:T(128)}, f32[2048,4,64]{0,2,1:T(8,128)}, f32[2048,4,64]{0,2,1:T(8,128)}, f32[4,512,4,64]{1,0,3,2:T(4,128)}, s32[4]{0:T(128)S(1)}, /*index=5*...) while((s32[]{:T(128)}, f32[2048,4,64]{0,2,1:T(8,128)}, ...), condition=%wide.region_17.18_spmd.clone, body=%wide.region_15.17_spmd.clone.sunk | while | flops 2751068160 | bytes 183114096 | solution.py:193
  446.2 11.5 multiply_reduce_fusion.3
  457.8 11.0 multiply_convert_fusion.3
  479.5 11.1 dynamic_update_slice.19
  497.5 7.6 fusion.152
  505.1 11.5 multiply_reduce_fusion.3
  516.6 11.0 multiply_convert_fusion.3
  539.1 11.1 dynamic_update_slice.19
  557.1 7.6 fusion.152
  564.8 11.5 multiply_reduce_fusion.3
  576.3 11.0 multiply_convert_fusion.3
  598.7 11.1 dynamic_update_slice.19
  616.8 7.6 fusion.152
  624.4 11.5 multiply_reduce_fusion.3
  635.9 11.0 multiply_convert_fusion.3
  658.4 11.1 dynamic_update_slice.19
  690.1 10.3 fusion.89
  717.8 22.1 %all-reduce.5 = (f32[3,256]{1,0:T(4,128)}, f32[1024]{0:T(1024)}) all-reduce(f32[3,256]{1,0:T(4,128)S(1)} %convert_reduce_fusion.1, f32[1024]{0:T(1024)S(1)} %copy-done.53), channel_id=1, replica_groups=mesh['dp'=8,'tensor'=4] {'dp'}, use_global_device_ids=true, to_apply=%region_23.24 | all-reduce | flops 1792 | bytes 14336 | tf_op jit(solution)/shard_map/psum | solution.py:205
  744.3 42.0 %all-reduce.4 = (f32[2,1024]{1,0:T(2,128)}, f32[4,1024]{1,0:T(4,128)}) all-reduce(f32[2,1024]{1,0:T(2,128)S(1)} %pad_maximum_fusion.4, f32[4,1024]{1,0:T(4,128)S(1)} %pad_maximum_fusion.3), channel_id=1, replica_groups=mesh['dp'=8,'tensor'=4] {'dp','tensor'}, use_global_device_ids=true, to_apply=%region_31.32 | all-reduce | flops 6144 | bytes 49152 | tf_op jit(solution)/shard_map/psum | solution.py:228
  789.5 346.4 %all-reduce.9.cloned.1.call-done = (f32[3,1024,256]{1,2,0:T(8,128)}, f32[256,1024]{1,0:T(8,128)}, f32[1024,1024]{1,0:T(8,128)}, f32[1024,1024]{1,0:T(8,128)}) async-done(((f32[3,1024,256]{1,2,0:T(8,128)}, f32[256,1024]{1,0:T(8,128)}, f32[1024,1024]{1,0:T(8,128)}, f32[1024,1024]{1,0:T(8,128)}), (f32[3,1024,256]{1,2,0:T(8,128)}, f32[256,1024]{1,0:T(8,128)}, f32[1024,1024]{1,0:T(8,128)}, ...) | async-done | bytes 12582928 | tf_op jit(solution)/shard_map/psum | solution.py:205
  (320 shorter events, 258.5 us)
Async XLA Ops:
  7.2 251.0 %copy-start = (bf16[1024,1024]{1,0:T(8,128)(2,1)S(1)}, bf16[1024,1024]{1,0:T(8,128)(2,1)}, u32[]{:S(2)}) copy-start(bf16[1024,1024]{1,0:T(8,128)(2,1)} %param.25) | copy-start | bytes 6291460
  7.2 46.7 %all-gather.5.cloned.1.call-start = ((), (), s32[]{:S(2)}) async-start(), calls=%async_computation.4 | async-start | bytes 5242880 | tf_op jit(solution)/shard_map/all_gather | solution.py:82
  16.6 164.6 %reduce-scatter.5.cloned.1.call-start = ((), (), s32[]{:S(2)}) async-start(), calls=%async_computation.5 | async-start | bytes 5242880 | tf_op jit(solution)/shard_map/reduce_scatter | solution.py:119
  18.4 43.0 %copy-start.22 = (f32[2048,32]{0,1:T(8,128)}, f32[2048,32]{0,1:T(8,128)S(1)}, u32[]{:S(2)}) copy-start(f32[2048,32]{0,1:T(8,128)S(1)} %get-tuple-element.267) | copy-start | bytes 786436
  18.4 43.0 %copy-start.24 = (f32[2048,32]{0,1:T(8,128)}, f32[2048,32]{0,1:T(8,128)S(1)}, u32[]{:S(2)}) copy-start(f32[2048,32]{0,1:T(8,128)S(1)} %get-tuple-element.268) | copy-start | bytes 786436
  136.4 44.8 %copy-start.32 = (f32[1,1024]{1,0:T(1,128)S(1)}, f32[1,1024]{1,0:T(1,128)}, u32[]{:S(2)}) copy-start(f32[1,1024]{1,0:T(1,128)} %get-tuple-element.270) | copy-start | bytes 12292
  136.4 49.0 %copy-start.37 = (f32[1,1024]{1,0:T(1,128)S(1)}, f32[1,1024]{1,0:T(1,128)}, u32[]{:S(2)}) copy-start(f32[1,1024]{1,0:T(1,128)} %get-tuple-element.274) | copy-start | bytes 12292
  136.4 49.0 %copy-start.51 = (f32[1,1024]{1,0:T(1,128)S(1)}, f32[1,1024]{1,0:T(1,128)}, u32[]{:S(2)}) copy-start(f32[1,1024]{1,0:T(1,128)} %get-tuple-element.272) | copy-start | bytes 12292
  136.5 85.2 %all-gather.7.cloned.1.call-start = ((), (), s32[]{:S(2)}) async-start(), calls=%async_computation.6 | async-start | bytes 5242880 | tf_op jit(solution)/shard_map/all_gather | solution.py:127
  187.1 71.1 %all-gather.9.cloned.1.call-start = ((), (), s32[]{:S(2)}) async-start(), calls=%async_computation.8 | async-start | bytes 5242880 | tf_op jit(solution)/shard_map/all_gather | solution.py:141
  188.4 201.1 %copy-start.38 = (f32[512]{0:T(512)}, f32[512]{0:T(512)S(1)}, u32[]{:S(2)}) copy-start(f32[512]{0:T(512)S(1)} %fusion.73) | copy-start | bytes 6148
  191.5 147.2 %reduce-scatter.9.cloned.1.call-start = ((), (), s32[]{:S(2)}) async-start(), calls=%async_computation.9 | async-start | bytes 5242880 | tf_op jit(solution)/shard_map/reduce_scatter | solution.py:148
  258.2 29.5 %copy-start.61 = (bf16[1024,1024]{1,0:T(8,128)(2,1)S(1)}, bf16[1024,1024]{1,0:T(8,128)(2,1)}, u32[]{:S(2)}) copy-start(bf16[1024,1024]{1,0:T(8,128)(2,1)} %param.23) | copy-start | bytes 6291460
  294.0 91.7 %reduce-scatter.7.cloned.1.call-start = ((), (), s32[]{:S(2)}) async-start(), calls=%async_computation.7 | async-start | bytes 5242880 | tf_op jit(solution)/shard_map/reduce_scatter | solution.py:132
  313.6 25.1 %copy-start.5 = (bf16[512,1024]{1,0:T(8,128)(2,1)S(1)}, bf16[512,1024]{1,0:T(8,128)(2,1)}, u32[]{:S(2)}) copy-start(bf16[512,1024]{1,0:T(8,128)(2,1)} %param.16) | copy-start | bytes 3145732
  313.6 25.1 %copy-start.10 = (bf16[512,1024]{1,0:T(8,128)(2,1)S(1)}, bf16[512,1024]{1,0:T(8,128)(2,1)}, u32[]{:S(2)}) copy-start(bf16[512,1024]{1,0:T(8,128)(2,1)} %reduce-scatter.5.cloned.1.call-done) | copy-start | bytes 3145732
  313.6 72.1 %copy-start.49 = (f32[1,1024]{1,0:T(1,128)S(1)}, f32[1,1024]{1,0:T(1,128)}, u32[]{:S(2)}) copy-start(f32[1,1024]{1,0:T(1,128)} %get-tuple-element.269) | copy-start | bytes 12292
  313.6 113.8 %all-gather.11.cloned.1.call-start = ((), (), s32[]{:S(2)}) async-start(), calls=%async_computation.10 | async-start | bytes 5242880 | tf_op jit(solution)/shard_map/all_gather | solution.py:159
  389.4 38.0 %copy-start.31 = (bf16[256,1024]{1,0:T(8,128)(2,1)S(1)}, bf16[256,1024]{1,0:T(8,128)(2,1)}, u32[]{:S(2)}) copy-start(bf16[256,1024]{1,0:T(8,128)(2,1)} %param.22) | copy-start | bytes 1572868
  389.4 42.5 %copy-start.42 = (f32[512]{0:T(512)}, f32[512]{0:T(512)S(1)}, u32[]{:S(2)}) copy-start(f32[512]{0:T(512)S(1)} %negate_multiply_fusion.2) | copy-start | bytes 6148
  392.8 347.1 %reduce-scatter.11.cloned.1.call-start = ((), (), s32[]{:S(2)}) async-start(), calls=%async_computation.11 | async-start | bytes 5242880 | tf_op jit(solution)/shard_map/reduce_scatter | solution.py:209
  690.0 445.9 %all-reduce.9.cloned.1.call-start = ((), (), s32[]{:S(2)}) async-start(), calls=%async_computation.12 | async-start | bytes 25165824 | tf_op jit(solution)/shard_map/psum | solution.py:205
  715.2 24.8 %copy-start.36 = (f32[512]{0:T(512)S(1)}, f32[512]{0:T(512)}, u32[]{:S(2)}) copy-start(f32[512]{0:T(512)} %copy-done.35) | copy-start | bytes 6148
  715.2 26.6 %copy-start.45 = (f32[512]{0:T(512)S(1)}, f32[512]{0:T(512)}, u32[]{:S(2)}) copy-start(f32[512]{0:T(512)} %copy-done.44) | copy-start | bytes 6148
  715.2 26.6 %copy-start.41 = (f32[512]{0:T(512)S(1)}, f32[512]{0:T(512)}, u32[]{:S(2)}) copy-start(f32[512]{0:T(512)} %copy-done.40) | copy-start | bytes 6148
  715.2 29.1 %copy-start.47 = (f32[1024]{0:T(1024)S(1)}, f32[1024]{0:T(1024)}, u32[]{:S(2)}) copy-start(f32[1024]{0:T(1024)} %get-tuple-element.183) | copy-start | bytes 12292
  715.2 29.1 %copy-start.48 = (f32[1024]{0:T(1024)S(1)}, f32[1024]{0:T(1024)}, u32[]{:S(2)}) copy-start(f32[1024]{0:T(1024)} %get-tuple-element.238) | copy-start | bytes 12292
  715.2 29.1 %copy-start.50 = (f32[1024]{0:T(1024)S(1)}, f32[1024]{0:T(1024)}, u32[]{:S(2)}) copy-start(f32[1024]{0:T(1024)} %get-tuple-element.189) | copy-start | bytes 12292
  715.2 29.1 %copy-start.52 = (f32[1024]{0:T(1024)S(1)}, f32[1024]{0:T(1024)}, u32[]{:S(2)}) copy-start(f32[1024]{0:T(1024)} %get-tuple-element.236) | copy-start | bytes 12292
  715.2 71.1 %copy-start.12 = (f32[512,1024]{1,0:T(8,128)S(1)}, f32[512,1024]{1,0:T(8,128)}, u32[]{:S(2)}) copy-start(f32[512,1024]{1,0:T(8,128)} %copy-done.11) | copy-start | bytes 6291460
  715.3 71.1 %copy-start.39 = (f32[512]{0:T(512)S(1)}, f32[512]{0:T(512)}, u32[]{:S(2)}) copy-start(f32[512]{0:T(512)} %copy-done.38) | copy-start | bytes 6148
  715.3 71.1 %copy-start.43 = (f32[512]{0:T(512)S(1)}, f32[512]{0:T(512)}, u32[]{:S(2)}) copy-start(f32[512]{0:T(512)} %copy-done.42) | copy-start | bytes 6148
  (62 other events, 343.4 us)
Sparse Core Ops, SparseCore 0:
  16.7 37.1 all-gather.4
  136.6 44.5 reduce-scatter.4
  187.2 34.4 all-gather.6
  223.7 34.4 all-gather.8
  294.1 44.5 reduce-scatter.8
  341.1 44.5 reduce-scatter.6
  392.9 34.4 all-gather.10
  690.1 44.5 reduce-scatter.10
  740.1 395.7 all-reduce.8
where the time goes:
time: 1160 us; the launch traced here: 1150 us
  waiting for transfers between devices  585 us (50%)
  matrix products  269 us (23%)
  other arithmetic  125 us (11%)
  local copies, waits for them, and re-layouts  88.7 us (8%)
  blocking collectives  64.1 us (6%)
  between operations  14.9 us (1%)
    psum x1, waiting for transfers between devices, shards(): lax.psum((grad_wqkv, grad_bqkv, grad_wproj, grad_w1, grad_b1, grad_w2), '...  346 us
    dynamic_update_slice x8, local copies, waits for them, and re-layouts, shards(): attended, log_sums = lax.map(attend_block, jnp.arange(nblocks))  46.5 us
    dot_general x4, matrix products, back_block(): jnp.einsum('qhd,khd->hqk', grad_out_blk, value_low, preferred_element_typ...  46 us
    reduce_scatter x1, waiting for transfers between devices, shards(): lax.psum_scatter(rounded(jnp.dot(picked, w_proj, preferred_element_type=f...  44.4 us
    reduce_scatter x1, waiting for transfers between devices, shards(): lax.psum_scatter(rounded(jnp.dot(picked, w_fc2, preferred_element_type=f3...  44.1 us
    convert_element_type x4, other arithmetic, back_block(): grad_scores = (probs * (grad_probs - inner)).astype(bf16)  44.1 us
    psum x1, blocking collectives, shards(): lax.psum((gain_terms, shift_terms), ('dp', 'tensor'))  42 us
    all_gather x1, waiting for transfers between devices, shards(): lax.all_gather(normed_one.astype(bf16), 'tensor', axis=0, tiled=True)  35.5 us
  transfers between devices with their start and end apart: 9, of which 8 were waited for; matrix products, arithmetic and copies ran while one was open for 6% of the time, Pallas kernels for 0%

commit v1 on v0

v1 whole, which is shorter than its diff:
```python
from functools import partial

import jax
import jax.numpy as jnp
from jax import lax
from jax.experimental import pallas as pl
from jax.experimental.pallas import tpu as pltpu
from jax.sharding import PartitionSpec as P

HDIM=64
LOG2E=1.4426950408889634
LN2=0.6931471805599453
f32=jnp.float32; bf16=jnp.bfloat16
BLK=256
VROWS=80
NT=(((1,),(1,)),((),()))

def work(flops):
    return pl.CostEstimate(flops=flops,bytes_accessed=0,transcendentals=0)

def lane_half(shape, which):
    lane=lax.broadcasted_iota(jnp.int32, shape, 1)
    return (lane//HDIM)%2==which

def attn_fwd_kernel(codes, q_ref, k_ref, v_ref, segq_ref, segk_ref, o_ref, lse_ref, vt, qm, m_sc, acc):
    step=pl.program_id(0)
    nkb=k_ref.shape[0]//BLK
    heads=q_ref.shape[1]//HDIM
    @pl.when(step==0)
    def _():
        for blk in range(nkb):
            rows=pl.ds(blk*BLK,BLK)
            vT=v_ref[rows,:].T
            for h in range(heads):
                vt[h*VROWS:h*VROWS+HDIM, rows]=vT[h*HDIM:(h+1)*HDIM,:]
        for h in range(heads):
            vt[h*VROWS+HDIM:(h+1)*VROWS,:]=jnp.ones((VROWS-HDIM,vt.shape[1]),bf16)
    for p in range(heads//2):
        qp=q_ref[:,p*128:(p+1)*128]
        for w in range(2):
            qm[2*p+w]=jnp.where(lane_half(qp.shape,w),qp,jnp.zeros_like(qp))
    m_sc[...]=jnp.full(m_sc.shape,-1e30,f32)
    acc[...]=jnp.zeros(acc.shape,f32)
    scale=HDIM**-0.5*LOG2E

    def tile(kb,masked):
        rows=pl.ds(pl.multiple_of(kb*BLK,BLK),BLK)
        if masked:
            allowed=segk_ref[rows,:][:,0:1]==segq_ref[0:1,:]
        for h in range(heads):
            p=h//2
            s=lax.dot_general(k_ref[rows,p*128:(p+1)*128],qm[h],NT,preferred_element_type=f32)*scale
            if masked: s=jnp.where(allowed,s,-1e30)
            m_prev=m_sc[h:h+1,:]
            m_new=jnp.maximum(m_prev,jnp.max(s,axis=0,keepdims=True))
            alpha=jnp.exp2(m_prev-m_new)
            prob=jnp.exp2(s-m_new).astype(bf16)
            m_sc[h:h+1,:]=m_new
            arows=slice(h*VROWS,(h+1)*VROWS)
            acc[arows,:]=acc[arows,:]*alpha+jnp.dot(vt[arows,rows],prob,preferred_element_type=f32)

    def body(kb,carry):
        code=codes[step,kb]
        @pl.when(code==1)
        def _(): tile(kb,False)
        @pl.when(code==2)
        def _(): tile(kb,True)
        return carry
    lax.fori_loop(0,nkb,body,0)
    outs=[]
    for h in range(heads):
        total=acc[h*VROWS+HDIM:h*VROWS+HDIM+1,:]
        outs.append(acc[h*VROWS:h*VROWS+HDIM,:]/total)
        lse_ref[h:h+1,:]=m_sc[h:h+1,:]+jnp.log2(total)
    for h in range(heads,8):
        lse_ref[h:h+1,:]=jnp.zeros((1,BLK),f32)
    o_ref[...]=jnp.concatenate(outs,axis=0).T.astype(bf16)

def attn_fwd(codes,q,k,v,segq,segk,block0,nblocks):
    rows,cols=k.shape
    heads=cols//HDIM
    full=lambda i,c:(0,0)
    return pl.pallas_call(
        attn_fwd_kernel,
        out_shape=(jax.ShapeDtypeStruct((nblocks*BLK,cols),bf16),jax.ShapeDtypeStruct((8,nblocks*BLK),f32)),
        grid_spec=pltpu.PrefetchScalarGridSpec(num_scalar_prefetch=1,grid=(nblocks,),
            in_specs=[pl.BlockSpec((BLK,cols),lambda i,c:(i+block0,0)),
                      pl.BlockSpec((rows,cols),full),pl.BlockSpec((rows,cols),full),
                      pl.BlockSpec((1,BLK),lambda i,c:(0,i+block0)),
                      pl.BlockSpec((rows,1),full)],
            out_specs=[pl.BlockSpec((BLK,cols),lambda i,c:(i,0)),pl.BlockSpec((8,BLK),lambda i,c:(0,i))],
            scratch_shapes=[pltpu.VMEM((heads*VROWS,rows),bf16),pltpu.VMEM((heads,BLK,128),bf16),
                            pltpu.VMEM((8,BLK),f32),pltpu.VMEM((heads*VROWS,BLK),f32)]),
        compiler_params=pltpu.CompilerParams(dimension_semantics=("arbitrary",)),
        name="attn_fwd",
        cost_estimate=work(64*nblocks*BLK*rows*cols),
    )(codes,q,k,v,segq,segk)

def swap_halves(x):
    n=x.shape[1]
    lane=lax.broadcasted_iota(jnp.int32,x.shape,1)
    up=pltpu.roll(x,n-HDIM//2,1)
    down=pltpu.roll(x,HDIM//2,1)
    return jnp.where(lane%HDIM<HDIM//2,up,down)

def attn_bwd_kernel(last, pair, codes, q_ref,k_ref,v_ref,do_ref,o_ref,lse_ref,segq_ref,segk_ref,cos_ref,sin_ref,cosk_ref,sink_ref,*rest):
    if last:
        dk0_ref,dv0_ref,gq_ref,gk_ref,gv_ref,bsum_ref,kt,qm,dom,delta,dq,dk,dv=rest
    else:
        gq_ref,gk_ref,gv_ref,bsum_ref,kt,qm,dom,delta,dq,dk,dv=rest
    step=pl.program_id(0)
    nkb=pl.num_programs(0)
    nqb=q_ref.shape[0]//BLK
    heads=q_ref.shape[1]//HDIM
    scale=HDIM**-0.5
    def unrotate(x,cos,sin):
        out=[]
        for p in range(heads//2):
            xp=x[:,p*128:(p+1)*128]
            out.append(xp*cos-swap_halves(xp)*sin)
        return jnp.concatenate(out,axis=1)
    @pl.when(step==0)
    def _():
        def prep(blk,carry):
            rows=pl.ds(pl.multiple_of(blk*BLK,BLK),BLK)
            for p in range(heads//2):
                lanes=slice(p*128,(p+1)*128)
                qp=q_ref[rows,lanes]; dp=do_ref[rows,lanes]
                for w in range(2):
                    sel=lane_half(qp.shape,w)
                    qm[2*p+w,rows,:]=jnp.where(sel,qp,jnp.zeros_like(qp))
                    dom[2*p+w,rows,:]=jnp.where(sel,dp,jnp.zeros_like(dp))
            prod=(do_ref[rows,:].astype(f32)*o_ref[rows,:].astype(f32)).T
            for h in range(heads):
                delta[h:h+1,rows]=jnp.sum(prod[h*HDIM:(h+1)*HDIM,:],axis=0,keepdims=True)
            return carry
        lax.fori_loop(0,nqb,prep,0)
        dq[...]=jnp.zeros(dq.shape,f32)
        bsum_ref[...]=jnp.zeros(bsum_ref.shape,f32)
    kt[...]=k_ref[...].T
    if last:
        dk[...]=dk0_ref[...]
        dv[...]=dv0_ref[...]
    else:
        dk[...]=jnp.zeros(dk.shape,f32)
        dv[...]=jnp.zeros(dv.shape,f32)

    def tile(qb,masked):
        rows=pl.ds(pl.multiple_of(qb*BLK,BLK),BLK)
        if masked:
            allowed=segk_ref[:,0:1]==segq_ref[0:1,rows]
        for h in range(heads):
            p=h//2
            lanes=slice(p*128,(p+1)*128)
            hr=slice(h*HDIM,(h+1)*HDIM)
            qh=qm[h,rows,:]; dh=dom[h,rows,:]
            s=lax.dot_general(k_ref[:,lanes],qh,NT,preferred_element_type=f32)*(scale*LOG2E)
            prob=jnp.exp2(s-lse_ref[2*pair+h:2*pair+h+1,rows])
            if masked: prob=jnp.where(allowed,prob,0.0)
            dp=lax.dot_general(v_ref[:,lanes],dh,NT,preferred_element_type=f32)
            ds=(prob*(dp-delta[h:h+1,rows])).astype(bf16)
            dv[:,lanes]+=jnp.dot(prob.astype(bf16),dh,preferred_element_type=f32)
            dk[:,lanes]+=jnp.dot(ds,qh,preferred_element_type=f32)
            dq[hr,rows]+=jnp.dot(kt[hr,:],ds,preferred_element_type=f32)

    def body(qb,carry):
        code=codes[qb,step]
        @pl.when(code==1)
        def _(): tile(qb,False)
        @pl.when(code==2)
        def _(): tile(qb,True)
        return carry
    lax.fori_loop(0,nqb,body,0)

    if last:
        gk=unrotate(dk[...]*scale,cosk_ref[...],sink_ref[...]).astype(bf16)
        gv=dv[...].astype(bf16)
        gk_ref[...]=gk
        gv_ref[...]=gv
        bsum_ref[1:2,:]+=jnp.sum(gk.astype(f32),axis=0,keepdims=True)
        bsum_ref[2:3,:]+=jnp.sum(gv.astype(f32),axis=0,keepdims=True)
    else:
        gk_ref[...]=dk[...]
        gv_ref[...]=dv[...]

    @pl.when(step==nkb-1)
    def _():
        def fin(blk,carry):
            rows=pl.ds(pl.multiple_of(blk*BLK,BLK),BLK)
            gq=unrotate(dq[:,rows].T*scale,cos_ref[rows,:],sin_ref[rows,:]).astype(bf16)
            gq_ref[rows,:]=gq
            bsum_ref[0:1,:]+=jnp.sum(gq.astype(f32),axis=0,keepdims=True)
            return carry
        lax.fori_loop(0,nqb,fin,0)

def attn_bwd(codes,q,k,v,do,o,lse,segq,segk,cos,sin,part,pair,carried):
    rows=k.shape[0]
    cols=2*HDIM
    half=do.shape[0]
    nb=rows//BLK
    last=carried is not None
    here=lambda n: pl.BlockSpec((half,n),lambda i,c:(0,0))
    mine=lambda n,col: pl.BlockSpec((half,n),lambda i,c:(part,col))
    held=pl.BlockSpec((half,cols),lambda i,c:(0,pair))
    blk=lambda n,col: pl.BlockSpec((BLK,n),lambda i,c:(i,col))
    kdtype=bf16 if last else f32
    return pl.pallas_call(
        partial(attn_bwd_kernel,last,pair),
        out_shape=(jax.ShapeDtypeStruct((half,cols),bf16),jax.ShapeDtypeStruct((rows,cols),kdtype),
                   jax.ShapeDtypeStruct((rows,cols),kdtype),jax.ShapeDtypeStruct((8,cols),f32)),
        grid_spec=pltpu.PrefetchScalarGridSpec(num_scalar_prefetch=1,grid=(nb,),
            in_specs=[mine(cols,pair),blk(cols,pair),blk(cols,pair),held,held,pl.BlockSpec((8,half),lambda i,c:(0,0)),
                      pl.BlockSpec((1,half),lambda i,c:(0,part)),blk(1,0),mine(128,0),mine(128,0),blk(128,0),blk(128,0)]
                     +([blk(cols,0),blk(cols,0)] if last else []),
            out_specs=[here(cols),blk(cols,0),blk(cols,0),pl.BlockSpec((8,cols),lambda i,c:(0,0))],
            scratch_shapes=[pltpu.VMEM((cols,BLK),bf16),pltpu.VMEM((2,half,128),bf16),pltpu.VMEM((2,half,128),bf16),
                            pltpu.VMEM((8,half),f32),pltpu.VMEM((cols,half),f32),pltpu.VMEM((BLK,cols),f32),pltpu.VMEM((BLK,cols),f32)]),
        compiler_params=pltpu.CompilerParams(dimension_semantics=("arbitrary",)),
        name="attn_bwd",
        cost_estimate=work(60*half*rows*cols),
    )(codes,q,k,v,do,o,lse,segq,segk,cos,sin,cos,sin,*(carried or ()))

def block_codes(seg,pad_seg,skip_pad):
    sb=seg.reshape(-1,BLK)
    lo=jnp.min(sb,axis=1); hi=jnp.max(sb,axis=1)
    meet=(lo[:,None]<=hi[None,:])&(lo[None,:]<=hi[:,None])
    whole=(lo==hi)
    same=whole[:,None]&whole[None,:]&(lo[:,None]==lo[None,:])
    code=jnp.where(meet,jnp.where(same,1,2),0).astype(jnp.int32)
    if skip_pad:
        alive=lo<pad_seg
        code=jnp.where(alive[:,None]&alive[None,:],code,0)
    return code


def pick(i,n,a_ref,b_ref):
    return jnp.where(i<n,a_ref[...],b_ref[...])


def qkv_kernel(n, xa_ref, xb_ref, w_ref, b_ref, cos_ref, sin_ref, *rest):
    x=pick(pl.program_id(0),n,xa_ref,xb_ref)
    cos=cos_ref[...]; sin=sin_ref[...]
    for c,o_ref in enumerate(rest[-3:]):
        y=jnp.dot(x,w_ref[c],preferred_element_type=f32)+b_ref[c:c+1,:]
        if c<2:
            parts=[]
            for p in range(y.shape[1]//128):
                yp=y[:,p*128:(p+1)*128]
                parts.append(yp*cos+swap_halves(yp)*sin)
            y=jnp.concatenate(parts,axis=1)
        o_ref[...]=y.astype(bf16)


def two(tile,n,width):
    return [pl.BlockSpec((tile,width),lambda i:(jnp.minimum(i,n-1),0)),
            pl.BlockSpec((tile,width),lambda i:(jnp.maximum(i-n,0),0))]


def qkv_rows(xa,xb,w,b,cos,sin,part,full):
    rows,d=xa.shape
    cols=w.shape[2]
    tile=min(512,rows)
    n=rows//tile
    off=part*2*n
    row=lambda m: pl.BlockSpec((tile,m),lambda i:(i+off,0))
    kept=[] if full is None else list(full)
    return pl.pallas_call(
        partial(qkv_kernel,n),
        grid=(2*n,),
        out_shape=[jax.ShapeDtypeStruct((cos.shape[0],cols),bf16)]*3,
        in_specs=two(tile,n,d)+[pl.BlockSpec(w.shape,lambda i:(0,0,0)),pl.BlockSpec(b.shape,lambda i:(0,0)),
                  row(128),row(128)]+[pl.BlockSpec(memory_space=pl.ANY)]*len(kept),
        out_specs=[row(cols)]*3,
        input_output_aliases={6+i:i for i in range(len(kept))},
        compiler_params=pltpu.CompilerParams(dimension_semantics=("arbitrary",)),
        name="qkv",
        cost_estimate=work(20*rows*d*cols*2),
    )(xa,xb,w,b,cos,sin,*kept)


def mlp_kernel(n,xa_ref,xb_ref,ga_ref,gb_ref,w1_ref,b1_ref,w2_ref,*rest):
    hid_ref,gp_ref,na_ref,nb_ref,db_ref=rest[-5:]
    i=pl.program_id(0)
    @pl.when(i==0)
    def _():
        db_ref[...]=jnp.zeros(db_ref.shape,f32)
    pre=jnp.dot(pick(i,n,xa_ref,xb_ref),w1_ref[...],preferred_element_type=f32)+b1_ref[...]
    phi=0.5+0.5*lax.erf(pre*0.7071067811865476)
    hid_ref[...]=(pre*phi).astype(bf16)
    slope=phi+pre*(0.3989422804014327*jnp.exp2(pre*pre*(-0.5*LOG2E)))
    gh=lax.dot_general(pick(i,n,ga_ref,gb_ref),w2_ref[...],NT,preferred_element_type=f32)
    gp=(gh*slope).astype(bf16)
    gp_ref[...]=gp
    db_ref[...]+=jnp.sum(gp.astype(f32),axis=0,keepdims=True)
    gn=lax.dot_general(gp,w1_ref[...],NT,preferred_element_type=f32).astype(bf16)
    @pl.when(i<n)
    def _(): na_ref[...]=gn
    @pl.when(i>=n)
    def _(): nb_ref[...]=gn


def mlp_rows(xs,gs,w1,b1,w2,part,full):
    rows,d=xs[0].shape
    units=w1.shape[1]
    tile=min(256,rows)
    n=rows//tile
    off=part*2*n
    row=lambda m: pl.BlockSpec((tile,m),lambda i:(i+off,0))
    whole=lambda a: pl.BlockSpec(a.shape,lambda i:(0,0))
    kept=[] if full is None else list(full)
    return pl.pallas_call(
        partial(mlp_kernel,n),
        grid=(2*n,),
        out_shape=[jax.ShapeDtypeStruct((rows*4,units),bf16)]*2+[jax.ShapeDtypeStruct((rows,d),bf16)]*2+
                  [jax.ShapeDtypeStruct((1,units),f32)],
        in_specs=two(tile,n,d)+two(tile,n,d)+[whole(w1),whole(b1),whole(w2)]+[pl.BlockSpec(memory_space=pl.ANY)]*len(kept),
        out_specs=[row(units),row(units)]+two(tile,n,d)+[pl.BlockSpec((1,units),lambda i:(0,0))],
        input_output_aliases={7+i:i for i in range(len(kept))},
        compiler_params=pltpu.CompilerParams(dimension_semantics=("arbitrary",)),
        name="mlp",
        cost_estimate=work(12*rows*d*units),
    )(*xs,*gs,w1,b1,w2,*kept)


def back_kernel(n,pairs,*refs):
    i=pl.program_id(0)
    w_ref,oa_ref,ob_ref=refs[-3:]
    y=0.0
    for c in range(3):
        g=jnp.concatenate([refs[c*pairs+p][...] for p in range(pairs)],axis=1)
        y=y+lax.dot_general(g,w_ref[c],NT,preferred_element_type=f32)
    y=y.astype(bf16)
    @pl.when(i<n)
    def _(): oa_ref[...]=y
    @pl.when(i>=n)
    def _(): ob_ref[...]=y


def back_rows(gq,gk,gv,w,part):
    half,cols=gq[0].shape
    rows=half//2
    d=w.shape[1]
    tile=min(512,rows)
    n=rows//tile
    off=part*2*n
    row=pl.BlockSpec((tile,cols),lambda i:(i+off,0))
    pairs=len(gq)
    return pl.pallas_call(
        partial(back_kernel,n,pairs),
        grid=(2*n,),
        out_shape=[jax.ShapeDtypeStruct((rows,d),bf16)]*2,
        in_specs=[pl.BlockSpec((tile,cols),lambda i:(i,0))]*pairs+[row]*(2*pairs)+[pl.BlockSpec(w.shape,lambda i:(0,0,0))],
        out_specs=two(tile,n,d),
        compiler_params=pltpu.CompilerParams(dimension_semantics=("arbitrary",)),
        name="back",
        cost_estimate=work(12*rows*d*cols*pairs),
    )(*gq,*gk,*gv,w)


def norm_rows(values_in, gain_row, shift_row):
    row_mean = jnp.mean(values_in, axis=-1, keepdims=True)
    centred = values_in - row_mean
    variance = jnp.mean(centred * centred, axis=-1, keepdims=True)
    return centred * lax.rsqrt(variance + 1e-06) * gain_row + shift_row


def flip(x,bits):
    n=lax.axis_size("tensor")
    return lax.ppermute(x,"tensor",[(i,i^bits) for i in range(n)])


def pair_sum(mine,other):
    return mine.astype(f32)+flip(other,1).astype(f32)


def dp_flip(x,bit):
    n=lax.axis_size("dp")
    return lax.ppermute(x,"dp",[(i,i^(1<<bit)) for i in range(n)])


class DpSum:
    def __init__(self,x,order):
        self.cur=x
        self.stages=[(bit,True) for bit in order]+[(bit,False) for bit in reversed(order)]
        self.at=0

    def operand(self):
        bit,halving=self.stages[self.at]
        if not halving: return self.cur
        half=self.cur.shape[0]//2
        up=(lax.axis_index("dp")>>bit)&1
        self.kept=lax.dynamic_slice_in_dim(self.cur,up*half,half,0)
        return lax.dynamic_slice_in_dim(self.cur,(1-up)*half,half,0)

    def start(self,operand):
        self.sent=operand
        self.got=dp_flip(operand,self.stages[self.at][0])

    def finish(self,got):
        bit,halving=self.stages[self.at]
        self.at+=1
        if halving:
            self.cur=(self.kept.astype(f32)+got.astype(f32)).astype(bf16)
        else:
            up=((lax.axis_index("dp")>>bit)&1)==1
            self.cur=jnp.concatenate([jnp.where(up,got,self.sent),jnp.where(up,self.sent,got)],axis=0)

    def rest(self):
        while self.at<len(self.stages):
            self.start(self.operand())
            self.finish(self.got)
        return self.cur


def begin(sums,value):
    value,*sends=lax.optimization_barrier((value,*[s.operand() for s in sums]))
    for s,x in zip(sums,sends): s.start(x)
    return value


def settle(sums,value):
    value,*gots=lax.optimization_barrier((value,*[s.got for s in sums]))
    for s,x in zip(sums,gots): s.finish(x)
    return value


def all_sum(x):
    for bits in (1,2):
        x=x+flip(x,bits)
    for bit in range(lax.axis_size("dp").bit_length()-1):
        x=x+dp_flip(x,bit)
    return x


def after(x,*others):
    return lax.optimization_barrier((x,)+others)[0]


def shards(tokens,grad_out,lengths,coords,w_qkv,b_qkv,w_proj,w_fc1,b_fc1,w_fc2,norm_gains,shift_biases):
    tok=tokens.shape[0]
    ranks=lax.axis_size("tensor")
    bits=lax.axis_size("dp").bit_length()-1
    me=lax.axis_index("tensor")
    rows_all=tok*ranks
    half=rows_all//2
    cols=w_qkv.shape[2]
    ends=jnp.cumsum(lengths[0])
    slots=lengths.shape[1]
    rel=jnp.arange(rows_all,dtype=jnp.int32)
    place=((rel//tok)^me)*tok+rel%tok
    seg=jnp.sum((place[:,None]>=ends[None,:]).astype(jnp.int32),axis=1)
    live=(place[:tok]<ends[-1]).astype(f32)[:,None]
    cgrp=jnp.concatenate([lax.dynamic_slice_in_dim(coords,(me^j)*tok,tok,1) for j in range(ranks)],axis=1).astype(f32)
    lane=jnp.arange(128,dtype=jnp.int32)
    pair=lane%(HDIM//2)
    freq=100.0**(-(pair//3).astype(f32)/(HDIM//2//3+1))
    angle=jnp.zeros((rows_all,128),f32)
    for a in range(3):
        angle=angle+cgrp[a][:,None]*jnp.where(pair%3==a,freq,0.0)[None,:]
    cos=jnp.cos(angle)
    sin=jnp.sin(angle)*jnp.where(lane%HDIM<HDIM//2,-1.0,1.0)[None,:]
    gains=norm_gains.astype(f32)
    shifts=shift_biases.astype(f32)
    x_rows=tokens.astype(f32)

    normed_one,norm_one_back=jax.vjp(norm_rows,x_rows,gains[0],shifts[0])
    low_one=normed_one.astype(bf16)
    far=flip(low_one,2)
    near=flip(low_one,1)
    grad_y=grad_out.astype(f32)*live
    grad_mlp=grad_y.astype(bf16)

    bq=b_qkv.astype(f32)
    qkv=qkv_rows(low_one,near,w_qkv,bq,cos,sin,0,None)
    far,*qkv=lax.optimization_barrier((far,*qkv))
    far_pair=flip(far,1)
    q,k,v=qkv_rows(far,far_pair,w_qkv,bq,cos,sin,1,qkv)
    n1=[low_one,near,far,far_pair]
    late,q,k,v=lax.optimization_barrier((grad_mlp,q,k,v))
    gm=[late,flip(late,1),flip(late,2)]
    segq=seg[None,:]; segk=seg[:,None]
    hb=half//BLK
    codes=block_codes(seg,slots,False)
    att_far,lse_far=attn_fwd(codes[hb:],q,k,v,segq,segk,hb,hb)
    proj=lambda a: jnp.dot(a,w_proj,preferred_element_type=f32).astype(bf16)
    across=pair_sum(proj(att_far[tok:]),proj(att_far[:tok])).astype(bf16)
    q_late,across,g2=lax.optimization_barrier((q,across,gm[2]))
    gm=[gm[0],gm[1],g2,flip(g2,1)]
    across=flip(across,3)
    att_near,lse_near=attn_fwd(codes[:hb],q_late,k,v,segq,segk,0,hb)
    across,att_near=lax.optimization_barrier((across,att_near))
    mine=pair_sum(proj(att_near[:tok]),proj(att_near[tok:]))
    resid_one=x_rows+mine+across.astype(f32)+shifts[2]
    normed_two,norm_two_back=jax.vjp(norm_rows,resid_one,gains[1],shifts[1])
    low_two=normed_two.astype(bf16)
    far=flip(low_two,2)
    near=flip(low_two,1)
    b1=b_fc1.astype(f32)[None,:]
    hid,gp,gn0,gn1,db0=mlp_rows((low_two,near),(gm[0],gm[1]),w_fc1,b1,w_fc2,0,None)
    far,hid,gp=lax.optimization_barrier((far,hid,gp))
    far_pair=flip(far,1)
    hid,gp,gn2,gn3,db1=mlp_rows((far,far_pair),(gm[2],gm[3]),w_fc1,b1,w_fc2,1,(hid,gp))
    db=db0+db1
    across=pair_sum(gn3,gn2).astype(bf16)
    hid,gp,across=lax.optimization_barrier((hid,gp,across))
    across=flip(across,3)
    mine=pair_sum(gn0,gn1)
    tn=lambda a,b: lax.dot_general(a,b,(((0,),(0,)),((),())),preferred_element_type=f32)
    grad_w1=tn(jnp.concatenate([low_two,near,far,far_pair],axis=0),gp).astype(bf16)
    grad_w2=tn(hid,jnp.concatenate(gm,axis=0)).astype(bf16)
    across,grad_w1,grad_w2=lax.optimization_barrier((across,grad_w1,grad_w2))
    low_order=tuple(range(bits))
    swapped=(1,0)+tuple(range(2,bits))
    wsums=[DpSum(grad_w1,low_order),DpSum(grad_w2,swapped)]
    grad_resid_two,grad_gain_two,grad_shift_two=norm_two_back(mine+across.astype(f32))

    grad_resid_one=grad_y+grad_resid_two
    grad_attn=grad_resid_one.astype(bf16)
    far=flip(grad_attn,2)
    near=flip(grad_attn,1)
    ghead=lambda a: lax.dot_general(a,w_proj,NT,preferred_element_type=f32).astype(bf16)
    bcodes=block_codes(seg,slots,True)
    do_near=jnp.concatenate([ghead(grad_attn),ghead(near)],axis=0)
    do_near=begin(wsums,do_near)
    bwd_near=lambda pair,do: attn_bwd(bcodes[:hb],q,k,v,do,att_near,lse_near,segq,segk,cos,sin,0,pair,None)
    bwd_far=lambda pair,do,carried: attn_bwd(bcodes[hb:],q,k,v,do,att_far,lse_far,segq,segk,cos,sin,1,pair,carried)
    gq0n,dk,dv,bs0=bwd_near(0,do_near)
    far,dk,dv=lax.optimization_barrier((far,dk,dv))
    dk=settle(wsums,dk)
    far_pair=flip(far,1)
    do_far=jnp.concatenate([ghead(far),ghead(far_pair)],axis=0)
    do_far=begin(wsums,do_far)
    gq0f,gk0,gv0,bs1=bwd_far(0,do_far,(dk,dv))
    gk0=settle(wsums,gk0)
    all1=jnp.concatenate(n1,axis=0)
    wpart=lambda gqn,gqf,gk,gv: tn(all1,jnp.concatenate([jnp.concatenate([gqn,gqf],axis=0),gk,gv],axis=1)).astype(bf16)
    do_near,gk0=lax.optimization_barrier((do_near,gk0))
    do_near=begin(wsums,do_near)
    gq1n,dk,dv,bs2=bwd_near(1,do_near)
    dk=settle(wsums,dk)
    dk=begin(wsums,dk)
    dk,gq0n,alla,atts=lax.optimization_barrier((dk,gq0n,jnp.concatenate([grad_attn,near,far,far_pair],axis=0),
                                                jnp.concatenate([att_near,att_far],axis=0)))
    tail0=[DpSum(wpart(gq0n,gq0f,gk0,gv0),low_order),DpSum(tn(atts,alla).astype(bf16),swapped)]
    dk=begin(tail0,dk)
    gq1f,gk1,gv1,bs3=bwd_far(1,do_far,(dk,dv))
    gk1=settle(wsums+tail0,gk1)
    gk1=begin(wsums+tail0,gk1)
    r2,r3=back_rows([gq0f,gq1f],[gk0,gk1],[gv0,gv1],w_qkv,1)
    across=pair_sum(r3,r2).astype(bf16)
    gq1n,across,hid=lax.optimization_barrier((gq1n,across,hid))
    across=flip(across,3)
    wqkv1=wpart(gq1n,gq1f,gk1,gv1)
    early=jnp.stack([grad_gain_two,grad_shift_two,jnp.sum(grad_attn,axis=0,dtype=f32),jnp.sum(grad_mlp,axis=0,dtype=f32)])
    early=early+flip(early,1)
    early=early+flip(early,2)
    d=tokens.shape[1]
    bsum=jnp.concatenate([(bs0+bs1)[:3],(bs2+bs3)[:3]],axis=1)
    sizes=(3*cols,db.shape[1],early.size)
    width=wqkv1.shape[1]
    pad=(-sum(sizes))%(width*8<<bits)
    small=jnp.concatenate([bsum.reshape(-1),db[0],early.reshape(-1),jnp.zeros((pad,),f32)]).astype(bf16).reshape(-1,width)
    hd=d//2
    tail1=[DpSum(wqkv1[:hd],low_order),DpSum(jnp.concatenate([wqkv1[hd:],small],axis=0),swapped)]
    gq_near=[gq0n,gq1n]
    gq1n_late=begin(tail1,gq1n)
    r0,r1=back_rows([gq0n,gq1n_late],[gk0,gk1],[gv0,gv1],w_qkv,0)
    r0=settle(wsums+tail0,r0)
    r0=begin(wsums+tail0,r0)
    mine=pair_sum(r0,r1)
    across,hid=lax.optimization_barrier((across,hid))
    o=[jnp.dot(hid[j*tok:(j+1)*tok],w_fc2,preferred_element_type=f32).astype(bf16) for j in range(ranks)]
    o_across=flip(pair_sum(o[3],o[2]).astype(bf16),3)
    output=(resid_one+pair_sum(o[0],o[1])+o_across.astype(f32)+shifts[3]).astype(bf16)
    for t in wsums+tail0+tail1:
        if hasattr(t,"got"): t.finish(t.got)
    grad_w1,grad_w2=[t.rest() for t in wsums]
    wqkv0,grad_proj=[t.rest() for t in tail0]
    tail_a,tail_b=[t.rest() for t in tail1]
    wqkv1=jnp.concatenate([tail_a,tail_b[:d-hd]],axis=0)
    spread=lambda w: jnp.stack([w[:,c*width//3:(c+1)*width//3] for c in range(3)])
    grad_wqkv=jnp.concatenate([spread(wqkv0),spread(wqkv1)],axis=2).astype(f32)
    small=tail_b[d-hd:].reshape(-1).astype(f32)
    grad_bqkv=small[:sizes[0]].reshape(3,cols)
    grad_b1=small[sizes[0]:sizes[0]+sizes[1]]
    early=small[sizes[0]+sizes[1]:sum(sizes)].reshape(4,d)
    grad_x_norm,grad_gain_one,grad_shift_one=norm_one_back(mine+across.astype(f32))
    grad_tokens=(grad_resid_one+grad_x_norm).astype(bf16)
    one=all_sum(jnp.stack([grad_gain_one,grad_shift_one]))
    return (output,grad_tokens,grad_wqkv,grad_bqkv,grad_proj.astype(f32),grad_w1.astype(f32),grad_b1,grad_w2.astype(f32),
            jnp.stack([one[0],early[0]]),jnp.stack([one[1],early[1],early[2],early[3]]))


def solution(mesh):
    rows=P(("dp","tensor"),None)
    return jax.shard_map(shards,mesh=mesh,
        in_specs=(rows,rows,P("dp",None),P(None,"dp"),P(None,None,"tensor"),P(None,"tensor"),P("tensor",None),
                  P(None,"tensor"),P("tensor"),P("tensor",None),P(),P()),
        out_specs=(rows,rows,P(None,None,"tensor"),P(None,"tensor"),P("tensor",None),P(None,"tensor"),P("tensor"),
                   P("tensor",None),P(),P()),
        check_vma=False)
```

time: 1160 us -> 646 us (0.56)
  waiting for transfers between devices: 585 us -> 188 us
  matrix products: 269 us -> 41.5 us
  Pallas kernels: 0 us -> 210 us
  starting transfers between devices: 1.09 us -> 78.1 us
  blocking collectives: 64.1 us -> 0 us
  local copies, waits for them, and re-layouts: 88.7 us -> 36.1 us
  other arithmetic: 125 us -> 77.4 us
  between operations: 14.9 us -> 2.61 us
    psum x1 -> x0, waiting for transfers between devices: 346 us -> none  [shards(): lax.psum((grad_wqkv, grad_bqkv, grad_wproj, grad_w1, grad_b1, grad_w2), '...]
    dot_general x40 -> x17, matrix products: 269 us -> 41.5 us  [the longest x5 26.3 us: shards(): lax.dot_general(a, b, (((0,), (0,)), ((), ())), preferred_element_type=f32)]
    pallas_call x0 -> x12, Pallas kernels: none -> 210 us  [the longest x4 88.7 us: attn_bwd(): pl.pallas_call(partial(attn_bwd_kernel, last, pair), out_shape=(jax.Shape...]
    ppermute x0 -> x67, waiting for transfers between devices: none -> 188 us  [the longest x39 113 us: dp_flip(): return lax.ppermute(x, 'dp', [(i, i ^ 1 << bit) for i in range(n)])]
    all_gather x4 -> x0, waiting for transfers between devices: 125 us -> none  [the longest x1 35.5 us: shards(): lax.all_gather(normed_one.astype(bf16), 'tensor', axis=0, tiled=True)]
    reduce_scatter x4 -> x0, waiting for transfers between devices: 114 us -> none  [the longest x1 44.4 us: shards(): lax.psum_scatter(rounded(jnp.dot(picked, w_proj, preferred_element_type=f...]
    ppermute x0 -> x67, starting transfers between devices: none -> 78.1 us  [the longest x39 55.3 us: dp_flip(): return lax.ppermute(x, 'dp', [(i, i ^ 1 << bit) for i in range(n)])]
    psum x2 -> x0, blocking collectives: 64.1 us -> none  [the longest x1 42 us: shards(): lax.psum((gain_terms, shift_terms), ('dp', 'tensor'))]
  transfers between devices with their start and end apart: 9 -> 67, of which waited for: 8 -> 32; matrix products, arithmetic and copies ran while one was open for 6% -> 20% of each run, Pallas kernels for 0% -> 25%
where the time goes in v1:
time: 646 us; the launch traced here: 634 us
  Pallas kernels  210 us (33%)
  waiting for transfers between devices  188 us (29%)
  starting transfers between devices  78.1 us (12%)
  other arithmetic  77.4 us (12%)
  matrix products  41.5 us (6%)
  local copies, waits for them, and re-layouts  36.1 us (6%)
    ppermute x39, waiting for transfers between devices, dp_flip(): return lax.ppermute(x, 'dp', [(i, i ^ 1 << bit) for i in range(n)])  113 us
    pallas_call x4, Pallas kernels, attn_bwd(): pl.pallas_call(partial(attn_bwd_kernel, last, pair), out_shape=(jax.Shape...  88.7 us
    pallas_call x2, Pallas kernels, attn_fwd(): pl.pallas_call(attn_fwd_kernel, out_shape=(jax.ShapeDtypeStruct((nblocks...  75 us
    ppermute x28, waiting for transfers between devices, flip(): return lax.ppermute(x, 'tensor', [(i, i ^ bits) for i in range(n)])  74.8 us
    ppermute x39, starting transfers between devices, dp_flip(): return lax.ppermute(x, 'dp', [(i, i ^ 1 << bit) for i in range(n)])  55.3 us
    dot_general x5, matrix products, shards(): lax.dot_general(a, b, (((0,), (0,)), ((), ())), preferred_element_type=f32)  26.3 us
    pallas_call x2, Pallas kernels, mlp_rows(): pl.pallas_call(partial(mlp_kernel, n), grid=(2 * n,), out_shape=[jax.Shap...  24.4 us
    ppermute x28, starting transfers between devices, flip(): return lax.ppermute(x, 'tensor', [(i, i ^ bits) for i in range(n)])  22.9 us
  transfers between devices with their start and end apart: 67, of which 32 were waited for; matrix products, arithmetic and copies ran while one was open for 20% of the time, Pallas kernels for 25%

profile of v1, /device:TPU:0, one launch (start us, length us, event | category | flops | bytes accessed | tf_op | source)
XLA Modules:
  0.0 634.0 jit_solution(10693705587204996389)
XLA Ops:
  9.4 5.8 sine_multiply_fusion
  15.2 5.5 qkv.2
  20.8 11.3 %collective-permute-done.xa_ref = bf16[512,1024]{1,0:T(8,128)(2,1)} collective-permute-done((bf16[512,1024]{1,0:T(8,128)(2,1)S(1)}, bf16[512,1024]{1,0:T(8,128)(2,1)}, u32[]{:S(2)}, u32[]{:S(2)}) %collective-permute-start) | collective-permute-done | bytes 1048608 | tf_op jit(solution)/shard_map/ppermute | solution.py:369
  37.7 5.5 qkv.3
  43.2 35.1 %attn_fwd.2 = (bf16[1024,256]{1,0:T(8,128)(2,1)}, f32[8,1024]{1,0:T(8,128)}) custom-call(s32[4,8]{1,0:T(4,128)} %get-tuple-element.342.codes, bf16[2048,256]{1,0:T(8,128)(2,1)} %get-tuple-element.149.q_ref, bf16[2048,256]{1,0:T(8,128)(2,1)} %get-tuple-element.144.k_ref, bf16[2048,256]{1,0:T(8,128)(2,1)} %get-tuple-element.145.v_ref, s32[1,2048]{1,0:T(1,128)} %bitcast.63, ...), custom_call_target="tpu_custom_call" | custom-call | flops 34359738368 | tf_op jit(solution)/shard_map/attn_fwd/pallas_call | solution.py:83
  80.1 6.7 %collective-permute-start.4 = (bf16[512,1024]{1,0:T(8,128)(2,1)}, bf16[512,1024]{1,0:T(8,128)(2,1)}, u32[]{:S(2)}, u32[]{:S(2)}) collective-permute-start(bf16[512,1024]{1,0:T(8,128)(2,1)} %get-tuple-element.147.ga_ref), channel_id=1, source_target_pairs={{0,2},{1,3},{2,0},{3,1},{4,6},{5,7},{6,4},{7,5},{8,10},{9,11},{10,... | collective-permute-start | bytes 3145736 | tf_op jit(solution)/shard_map/ppermute | solution.py:369
  88.2 22.3 %collective-permute-done.4.ga_ref = bf16[512,1024]{1,0:T(8,128)(2,1)} collective-permute-done((bf16[512,1024]{1,0:T(8,128)(2,1)}, bf16[512,1024]{1,0:T(8,128)(2,1)}, u32[]{:S(2)}, u32[]{:S(2)}) %collective-permute-start.4) | collective-permute-done | bytes 1048608 | tf_op jit(solution)/shard_map/ppermute | solution.py:369
  111.1 40.0 %attn_fwd.3 = (bf16[1024,256]{1,0:T(8,128)(2,1)}, f32[8,1024]{1,0:T(8,128)}) custom-call(s32[4,8]{1,0:T(4,128)} %get-tuple-element.341.codes, bf16[2048,256]{1,0:T(8,128)(2,1)} %get-tuple-element.149.q_ref, bf16[2048,256]{1,0:T(8,128)(2,1)} %get-tuple-element.144.k_ref, bf16[2048,256]{1,0:T(8,128)(2,1)} %get-tuple-element.145.v_ref, s32[1,2048]{1,0:T(1,128)} %bitcast.64, ...), custom_call_target="tpu_custom_call" | custom-call | flops 34359738368 | tf_op jit(solution)/shard_map/attn_fwd/pallas_call | solution.py:83
  163.2 12.3 %mlp.2 = (bf16[2048,1024]{1,0:T(8,128)(2,1)}, bf16[2048,1024]{1,0:T(8,128)(2,1)}, bf16[512,1024]{1,0:T(8,128)(2,1)}, bf16[512,1024]{1,0:T(8,128)(2,1)}, f32[1,1024]{1,0:T(1,128)}) custom-call(bf16[512,1024]{1,0:T(8,128)(2,1)} %add_convert_fusion.7.xa_ref, bf16[512,1024]{1,0:T(8,128)(2,1)} %collective-permute-done.7.xb_ref, ...), custom_call_target="tpu_custom_call" | custom-call | flops 6442450944 | tf_op jit(solution)/shard_map/mlp/pallas_call | solution.py:311
  175.5 10.6 %collective-permute-done.10.xa_ref = bf16[512,1024]{1,0:T(8,128)(2,1)} collective-permute-done((bf16[512,1024]{1,0:T(8,128)(2,1)}, bf16[512,1024]{1,0:T(8,128)(2,1)}, u32[]{:S(2)}, u32[]{:S(2)}) %collective-permute-start.10) | collective-permute-done | bytes 1048608 | tf_op jit(solution)/shard_map/ppermute | solution.py:369
  189.1 12.1 %mlp.3 = (bf16[2048,1024]{1,0:T(8,128)(2,1)}, bf16[2048,1024]{1,0:T(8,128)(2,1)}, bf16[512,1024]{1,0:T(8,128)(2,1)}, bf16[512,1024]{1,0:T(8,128)(2,1)}, f32[1,1024]{1,0:T(1,128)}) custom-call(bf16[512,1024]{1,0:T(8,128)(2,1)} %collective-permute-done.10.xa_ref, ...), custom_call_target="tpu_custom_call", output_to_operand_aliasing={{0}: (7, {}), {1}: (8, {})} | custom-call | flops 6442450944 | tf_op jit(solution)/shard_map/mlp/pallas_call | solution.py:311
  206.2 8.1 %fusion.30 = bf16[1024,1024]{1,0:T(8,128)(2,1)S(1)} fusion(bf16[2048,1024]{1,0:T(8,128)(2,1)} %get-tuple-element.228, bf16[512,1024]{1,0:T(8,128)(2,1)} %collective-permute-done.12.gb_ref, bf16[512,1024]{1,0:T(8,128)(2,1)} %collective-permute-done.4.ga_ref, bf16[512,1024]{1,0:T(8,128)(2,1)} %collective-permute-done.8.gb_ref, ...), kind=kOutput, calls=%fused_computation.57 | convolution fusion | flops 4312793088 | bytes 10485760 | tf_op jit(solution)/shard_map/dot_general | solution.py:508
  214.4 7.6 %fusion.33 = bf16[1024,1024]{1,0:T(8,128)(2,1)S(1)} fusion(bf16[2048,1024]{1,0:T(8,128)(2,1)S(1)} %copy-done.77, bf16[512,1024]{1,0:T(8,128)(2,1)} %collective-permute-done.11.xb_ref, bf16[512,1024]{1,0:T(8,128)(2,1)} %collective-permute-done.10.xa_ref, bf16[512,1024]{1,0:T(8,128)(2,1)} %collective-permute-done.7.xb_ref, ...), kind=kOutput, calls=%fused_computation.58 | convolution fusion | flops 4312793088 | bytes 10485760 | tf_op jit(solution)/shard_map/dot_general | solution.py:508
  222.0 9.3 %collective-permute-done.14 = bf16[512,1024]{1,0:T(8,128)(2,1)S(1)} collective-permute-done((bf16[512,1024]{1,0:T(8,128)(2,1)S(1)}, bf16[512,1024]{1,0:T(8,128)(2,1)S(1)}, u32[]{:S(2)}, u32[]{:S(2)}) %collective-permute-start.14) | collective-permute-done | bytes 1048608 | tf_op jit(solution)/shard_map/ppermute | solution.py:369
  237.9 13.9 %constant_dynamic-slice_fusion.15 = bf16[512,1024]{1,0:T(8,128)(2,1)} fusion(bf16[1024,1024]{1,0:T(8,128)(2,1)S(1)} %fusion.30, s32[]{:T(128)S(6)} %select_n.449), kind=kLoop, calls=%fused_computation.221 | loop fusion | bytes 2097156 | tf_op jit(solution)/shard_map/dynamic_slice | solution.py:393
  262.4 23.8 %attn_bwd.4 = (bf16[1024,128]{1,0:T(8,128)(2,1)}, f32[2048,128]{1,0:T(8,128)}, f32[2048,128]{1,0:T(8,128)}, f32[8,128]{1,0:T(8,128)}) custom-call(s32[4,8]{1,0:T(4,128)} %get-tuple-element.338.codes, bf16[2048,256]{1,0:T(8,128)(2,1)} %get-tuple-element.149.q_ref, bf16[2048,256]{1,0:T(8,128)(2,1)} %get-tuple-element.144.k_ref, ...), custom_call_target="tpu_custom_call" | custom-call | flops 16106127360 | tf_op jit(solution)/shard_map/attn_bwd/pallas_call | solution.py:207
  297.7 20.6 %attn_bwd.5 = (bf16[1024,128]{1,0:T(8,128)(2,1)}, bf16[2048,128]{1,0:T(8,128)(2,1)}, bf16[2048,128]{1,0:T(8,128)(2,1)}, f32[8,128]{1,0:T(8,128)}) custom-call(s32[4,8]{1,0:T(4,128)} %get-tuple-element.337.codes, bf16[2048,256]{1,0:T(8,128)(2,1)} %get-tuple-element.149.q_ref, bf16[2048,256]{1,0:T(8,128)(2,1)} %get-tuple-element.144.k_ref, ...), custom_call_target="tpu_custom_call" | custom-call | flops 16106127360 | tf_op jit(solution)/shard_map/attn_bwd/pallas_call | solution.py:207
  327.9 23.8 %attn_bwd.6 = (bf16[1024,128]{1,0:T(8,128)(2,1)}, f32[2048,128]{1,0:T(8,128)}, f32[2048,128]{1,0:T(8,128)}, f32[8,128]{1,0:T(8,128)}) custom-call(s32[4,8]{1,0:T(4,128)} %get-tuple-element.338.codes, bf16[2048,256]{1,0:T(8,128)(2,1)} %get-tuple-element.149.q_ref, bf16[2048,256]{1,0:T(8,128)(2,1)} %get-tuple-element.144.k_ref, ...), custom_call_target="tpu_custom_call" | custom-call | flops 16106127360 | tf_op jit(solution)/shard_map/attn_bwd/pallas_call | solution.py:207
  354.4 5.1 fusion.55
  368.1 20.5 %attn_bwd.7 = (bf16[1024,128]{1,0:T(8,128)(2,1)}, bf16[2048,128]{1,0:T(8,128)(2,1)}, bf16[2048,128]{1,0:T(8,128)(2,1)}, f32[8,128]{1,0:T(8,128)}) custom-call(s32[4,8]{1,0:T(4,128)} %get-tuple-element.337.codes, bf16[2048,256]{1,0:T(8,128)(2,1)} %get-tuple-element.149.q_ref, bf16[2048,256]{1,0:T(8,128)(2,1)} %get-tuple-element.144.k_ref, ...), custom_call_target="tpu_custom_call" | custom-call | flops 16106127360 | tf_op jit(solution)/shard_map/attn_bwd/pallas_call | solution.py:207
  398.5 5.5 back.2
  412.2 4.2 fusion.52
  418.1 5.6 back.3
  440.4 26.0 %collective-permute-done.40 = bf16[128,384]{1,0:T(8,128)(2,1)S(1)} collective-permute-done((bf16[128,384]{1,0:T(8,128)(2,1)}, bf16[128,384]{1,0:T(8,128)(2,1)S(1)}, u32[]{:S(2)}, u32[]{:S(2)}) %collective-permute-start.40) | collective-permute-done | bytes 98336 | tf_op jit(solution)/shard_map/ppermute | solution.py:378
  472.5 5.3 collective-permute-done.44
  485.8 21.7 %collective-permute-done.58 = bf16[64,1024]{1,0:T(8,128)(2,1)S(1)} collective-permute-done((bf16[64,1024]{1,0:T(8,128)(2,1)S(1)}, bf16[64,1024]{1,0:T(8,128)(2,1)S(1)}, u32[]{:S(2)}, u32[]{:S(2)}) %collective-permute-start.58) | collective-permute-done | bytes 131104 | tf_op jit(solution)/shard_map/ppermute | solution.py:378
  530.6 4.3 collective-permute-done.42
  551.3 6.6 %collective-permute-done.59 = bf16[128,1024]{1,0:T(8,128)(2,1)S(1)} collective-permute-done((bf16[128,1024]{1,0:T(8,128)(2,1)S(1)}, bf16[128,1024]{1,0:T(8,128)(2,1)S(1)}, u32[]{:S(2)}, u32[]{:S(2)}) %collective-permute-start.59) | collective-permute-done | bytes 262176 | tf_op jit(solution)/shard_map/ppermute | solution.py:378
  564.4 5.1 collective-permute-done.49
  571.1 4.3 collective-permute-done.55
  577.5 6.0 collective-permute-done.43
  618.8 13.0 %collective-permute-done.32 = bf16[512,1024]{1,0:T(8,128)(2,1)S(1)} collective-permute-done((bf16[512,1024]{1,0:T(8,128)(2,1)S(1)}, bf16[512,1024]{1,0:T(8,128)(2,1)S(1)}, u32[]{:S(2)}, u32[]{:S(2)}) %collective-permute-start.32) | collective-permute-done | bytes 1048608 | tf_op jit(solution)/shard_map/ppermute | solution.py:369
  (443 shorter events, 223.8 us)
Async XLA Ops:
  5.7 26.4 %collective-permute-start = (bf16[512,1024]{1,0:T(8,128)(2,1)S(1)}, bf16[512,1024]{1,0:T(8,128)(2,1)}, u32[]{:S(2)}, u32[]{:S(2)}) collective-permute-start(bf16[512,1024]{1,0:T(8,128)(2,1)S(1)} %fusion.23.xa_ref), channel_id=1, source_target_pairs={{0,2},{1,3},{2,0},{3,1},{4,6},{5,7},{6,4},{7,5},{8,10},{9,11},{10,... | collective-permute-start | bytes 3145736 | tf_op jit(solution)/shard_map/ppermute | solution.py:369
  80.1 30.4 %collective-permute-start.4 = (bf16[512,1024]{1,0:T(8,128)(2,1)}, bf16[512,1024]{1,0:T(8,128)(2,1)}, u32[]{:S(2)}, u32[]{:S(2)}) collective-permute-start(bf16[512,1024]{1,0:T(8,128)(2,1)} %get-tuple-element.147.ga_ref), channel_id=1, source_target_pairs={{0,2},{1,3},{2,0},{3,1},{4,6},{5,7},{6,4},{7,5},{8,10},{9,11},{10,... | collective-permute-start | bytes 3145736 | tf_op jit(solution)/shard_map/ppermute | solution.py:369
  110.6 40.5 %collective-permute-start.5 = (bf16[512,1024]{1,0:T(8,128)(2,1)S(1)}, bf16[512,1024]{1,0:T(8,128)(2,1)S(1)}, u32[]{:S(2)}, u32[]{:S(2)}) collective-permute-start(bf16[512,1024]{1,0:T(8,128)(2,1)S(1)} %add_convert_fusion.8), channel_id=1, source_target_pairs={{0,3},{1,2},{2,1},{3,0},{4,7},{5,6},{6,5},{7,4},{8,11},{9,10},{10,... | collective-permute-start | bytes 3145736 | tf_op jit(solution)/shard_map/ppermute | solution.py:369
  160.5 25.5 %collective-permute-start.10 = (bf16[512,1024]{1,0:T(8,128)(2,1)}, bf16[512,1024]{1,0:T(8,128)(2,1)}, u32[]{:S(2)}, u32[]{:S(2)}) collective-permute-start(bf16[512,1024]{1,0:T(8,128)(2,1)} %add_convert_fusion.7.xa_ref), channel_id=1, source_target_pairs={{0,2},{1,3},{2,0},{3,1},{4,6},{5,7},{6,4},{7,5},{8,10},{9,11},{10,... | collective-permute-start | bytes 3145736 | tf_op jit(solution)/shard_map/ppermute | solution.py:369
  161.2 24.9 %collective-permute-start.12 = (bf16[512,1024]{1,0:T(8,128)(2,1)}, bf16[512,1024]{1,0:T(8,128)(2,1)}, u32[]{:S(2)}, u32[]{:S(2)}) collective-permute-start(bf16[512,1024]{1,0:T(8,128)(2,1)} %collective-permute-done.4.ga_ref), channel_id=1, source_target_pairs={{0,1},{1,0},{2,3},{3,2},{4,5},{5,4},{6,7},{7,6},{8,9},{9,8},{10,11... | collective-permute-start | bytes 3145736 | tf_op jit(solution)/shard_map/ppermute | solution.py:369
  201.9 29.5 %collective-permute-start.9 = (bf16[512,1024]{1,0:T(8,128)(2,1)}, bf16[512,1024]{1,0:T(8,128)(2,1)S(1)}, u32[]{:S(2)}, u32[]{:S(2)}) collective-permute-start(bf16[512,1024]{1,0:T(8,128)(2,1)} %get-tuple-element.154), channel_id=1, source_target_pairs={{0,1},{1,0},{2,3},{3,2},{4,5},{5,4},{6,7},{7,6},{8,9},{9,8},{10,11... | collective-permute-start | bytes 3145736 | tf_op jit(solution)/shard_map/ppermute | solution.py:369
  206.2 25.2 %collective-permute-start.14 = (bf16[512,1024]{1,0:T(8,128)(2,1)S(1)}, bf16[512,1024]{1,0:T(8,128)(2,1)S(1)}, u32[]{:S(2)}, u32[]{:S(2)}) collective-permute-start(bf16[512,1024]{1,0:T(8,128)(2,1)S(1)} %add_convert_fusion.6), channel_id=1, source_target_pairs={{0,3},{1,2},{2,1},{3,0},{4,7},{5,6},{6,5},{7,4},{8,11},{9,10},{10,... | collective-permute-start | bytes 3145736 | tf_op jit(solution)/shard_map/ppermute | solution.py:369
  235.2 21.8 %collective-permute-start.15 = (bf16[512,1024]{1,0:T(8,128)(2,1)}, bf16[512,1024]{1,0:T(8,128)(2,1)S(1)}, u32[]{:S(2)}, u32[]{:S(2)}) collective-permute-start(bf16[512,1024]{1,0:T(8,128)(2,1)} %get-tuple-element.267), channel_id=1, source_target_pairs={{0,1},{1,0},{2,3},{3,2},{4,5},{5,4},{6,7},{7,6},{8,9},{9,8},{10,11... | collective-permute-start | bytes 3145736 | tf_op jit(solution)/shard_map/ppermute | solution.py:369
  237.5 48.7 %collective-permute-start.16 = (bf16[512,1024]{1,0:T(8,128)(2,1)}, bf16[512,1024]{1,0:T(8,128)(2,1)}, u32[]{:S(2)}, u32[]{:S(2)}) collective-permute-start(bf16[512,1024]{1,0:T(8,128)(2,1)} %get-tuple-element.267), channel_id=1, source_target_pairs={{0,2},{1,3},{2,0},{3,1},{4,6},{5,7},{6,4},{7,5},{8,10},{9,11},{10,... | collective-permute-start | bytes 3145736 | tf_op jit(solution)/shard_map/ppermute | solution.py:369
  255.2 148.9 %collective-permute-start.34 = (f32[4,1024]{1,0:T(4,128)}, f32[4,1024]{1,0:T(4,128)}, u32[]{:S(2)}, u32[]{:S(2)}) collective-permute-start(f32[4,1024]{1,0:T(4,128)} %fusion.96), channel_id=1, source_target_pairs={{0,2},{1,3},{2,0},{3,1},{4,6},{5,7},{6,4},{7,5},{8,10},{9,11},{10,... | collective-permute-start | bytes 49160 | tf_op jit(solution)/shard_map/ppermute | solution.py:369
  259.3 29.3 %collective-permute-start.18 = (bf16[512,1024]{1,0:T(8,128)(2,1)}, bf16[512,1024]{1,0:T(8,128)(2,1)}, u32[]{:S(2)}, u32[]{:S(2)}) collective-permute-start(bf16[512,1024]{1,0:T(8,128)(2,1)} %constant_dynamic-slice_fusion.16), channel_id=1, source_target_pairs={{0,4},{4,0},{8,12},{12,8},{16,20},{20,16},{24,28},{28,24},{1,5},{5... | collective-permute-start | bytes 3145736 | tf_op jit(solution)/shard_map/ppermute | solution.py:378
  260.8 27.8 %collective-permute-start.19 = (bf16[512,1024]{1,0:T(8,128)(2,1)}, bf16[512,1024]{1,0:T(8,128)(2,1)}, u32[]{:S(2)}, u32[]{:S(2)}) collective-permute-start(bf16[512,1024]{1,0:T(8,128)(2,1)} %constant_dynamic-slice_fusion.15), channel_id=1, source_target_pairs={{0,8},{4,12},{8,0},{12,4},{16,24},{20,28},{24,16},{28,20},{1,9},{5... | collective-permute-start | bytes 3145736 | tf_op jit(solution)/shard_map/ppermute | solution.py:378
  296.8 25.3 %collective-permute-start.20 = (bf16[256,1024]{1,0:T(8,128)(2,1)}, bf16[256,1024]{1,0:T(8,128)(2,1)S(1)}, u32[]{:S(2)}, u32[]{:S(2)}) collective-permute-start(bf16[256,1024]{1,0:T(8,128)(2,1)} %constant_dynamic-slice_fusion.14), channel_id=1, source_target_pairs={{0,8},{4,12},{8,0},{12,4},{16,24},{20,28},{24,16},{28,20},{1,9},{5... | collective-permute-start | bytes 1572872 | tf_op jit(solution)/shard_map/ppermute | solution.py:378
  297.2 24.9 %collective-permute-start.21 = (bf16[256,1024]{1,0:T(8,128)(2,1)}, bf16[256,1024]{1,0:T(8,128)(2,1)S(1)}, u32[]{:S(2)}, u32[]{:S(2)}) collective-permute-start(bf16[256,1024]{1,0:T(8,128)(2,1)} %constant_dynamic-slice_fusion.13), channel_id=1, source_target_pairs={{0,4},{4,0},{8,12},{12,8},{16,20},{20,16},{24,28},{28,24},{1,5},{5... | collective-permute-start | bytes 1572872 | tf_op jit(solution)/shard_map/ppermute | solution.py:378
  325.0 26.7 %collective-permute-start.22 = (bf16[128,1024]{1,0:T(8,128)(2,1)}, bf16[128,1024]{1,0:T(8,128)(2,1)}, u32[]{:S(2)}, u32[]{:S(2)}) collective-permute-start(bf16[128,1024]{1,0:T(8,128)(2,1)} %constant_dynamic-slice_fusion.12), channel_id=1, source_target_pairs={{0,16},{4,20},{8,24},{12,28},{16,0},{20,4},{24,8},{28,12},{1,17},{... | collective-permute-start | bytes 786440 | tf_op jit(solution)/shard_map/ppermute | solution.py:378
  325.0 26.7 %collective-permute-start.23 = (bf16[128,1024]{1,0:T(8,128)(2,1)S(1)}, bf16[128,1024]{1,0:T(8,128)(2,1)}, u32[]{:S(2)}, u32[]{:S(2)}) collective-permute-start(bf16[128,1024]{1,0:T(8,128)(2,1)S(1)} %constant_dynamic-slice_fusion.11), channel_id=1, source_target_pairs={{0,16},{4,20},{8,24},{12,28},{16,0},{20,4},{24,8},{28,12},{1,17},{... | collective-permute-start | bytes 786440 | tf_op jit(solution)/shard_map/ppermute | solution.py:378
  361.7 29.4 %collective-permute-start.26 = (bf16[512,384]{1,0:T(8,128)(2,1)S(1)}, bf16[512,384]{1,0:T(8,128)(2,1)}, u32[]{:S(2)}, u32[]{:S(2)}) collective-permute-start(bf16[512,384]{1,0:T(8,128)(2,1)S(1)} %constant_dynamic-slice_fusion.10), channel_id=1, source_target_pairs={{0,4},{4,0},{8,12},{12,8},{16,20},{20,16},{24,28},{28,24},{1,5},{5... | collective-permute-start | bytes 1179656 | tf_op jit(solution)/shard_map/ppermute | solution.py:378
  363.2 25.4 %collective-permute-start.27 = (bf16[128,1024]{1,0:T(8,128)(2,1)}, bf16[128,1024]{1,0:T(8,128)(2,1)}, u32[]{:S(2)}, u32[]{:S(2)}) collective-permute-start(bf16[128,1024]{1,0:T(8,128)(2,1)} %constant_dynamic-slice_fusion.9), channel_id=1, source_target_pairs={{0,8},{4,12},{8,0},{12,4},{16,24},{20,28},{24,16},{28,20},{1,9},{5... | collective-permute-start | bytes 786440 | tf_op jit(solution)/shard_map/ppermute | solution.py:378
  365.1 23.5 %collective-permute-start.24 = (bf16[128,1024]{1,0:T(8,128)(2,1)S(1)}, bf16[128,1024]{1,0:T(8,128)(2,1)}, u32[]{:S(2)}, u32[]{:S(2)}) collective-permute-start(bf16[128,1024]{1,0:T(8,128)(2,1)S(1)} %add_convert_fusion.14), channel_id=1, source_target_pairs={{0,16},{4,20},{8,24},{12,28},{16,0},{20,4},{24,8},{28,12},{1,17},{... | collective-permute-start | bytes 786440 | tf_op jit(solution)/shard_map/ppermute | solution.py:378
  365.1 25.9 %collective-permute-start.25 = (bf16[128,1024]{1,0:T(8,128)(2,1)}, bf16[128,1024]{1,0:T(8,128)(2,1)}, u32[]{:S(2)}, u32[]{:S(2)}) collective-permute-start(bf16[128,1024]{1,0:T(8,128)(2,1)} %add_convert_fusion.13), channel_id=1, source_target_pairs={{0,16},{4,20},{8,24},{12,28},{16,0},{20,4},{24,8},{28,12},{1,17},{... | collective-permute-start | bytes 786440 | tf_op jit(solution)/shard_map/ppermute | solution.py:378
  405.2 18.7 %collective-permute-start.35 = (bf16[256,1024]{1,0:T(8,128)(2,1)S(1)}, bf16[256,1024]{1,0:T(8,128)(2,1)}, u32[]{:S(2)}, u32[]{:S(2)}) collective-permute-start(bf16[256,1024]{1,0:T(8,128)(2,1)S(1)} %pad_maximum_fusion.10), channel_id=1, source_target_pairs={{0,8},{4,12},{8,0},{12,4},{16,24},{20,28},{24,16},{28,20},{1,9},{5... | collective-permute-start | bytes 1572872 | tf_op jit(solution)/shard_map/ppermute | solution.py:378
  405.2 18.6 %collective-permute-start.36 = (bf16[256,1024]{1,0:T(8,128)(2,1)}, bf16[256,1024]{1,0:T(8,128)(2,1)}, u32[]{:S(2)}, u32[]{:S(2)}) collective-permute-start(bf16[256,1024]{1,0:T(8,128)(2,1)} %pad_maximum_fusion.11), channel_id=1, source_target_pairs={{0,4},{4,0},{8,12},{12,8},{16,20},{20,16},{24,28},{28,24},{1,5},{5... | collective-permute-start | bytes 1572872 | tf_op jit(solution)/shard_map/ppermute | solution.py:378
  406.8 17.0 %collective-permute-start.37 = (bf16[256,384]{1,0:T(8,128)(2,1)}, bf16[256,384]{1,0:T(8,128)(2,1)}, u32[]{:S(2)}, u32[]{:S(2)}) collective-permute-start(bf16[256,384]{1,0:T(8,128)(2,1)} %constant_dynamic-slice_fusion.8), channel_id=1, source_target_pairs={{0,8},{4,12},{8,0},{12,4},{16,24},{20,28},{24,16},{28,20},{1,9},{5... | collective-permute-start | bytes 589832 | tf_op jit(solution)/shard_map/ppermute | solution.py:378
  431.9 159.4 %collective-permute-start.39 = (bf16[512,1024]{1,0:T(8,128)(2,1)}, bf16[512,1024]{1,0:T(8,128)(2,1)}, u32[]{:S(2)}, u32[]{:S(2)}) collective-permute-start(bf16[512,1024]{1,0:T(8,128)(2,1)} %get-tuple-element.248), channel_id=1, source_target_pairs={{0,1},{1,0},{2,3},{3,2},{4,5},{5,4},{6,7},{7,6},{8,9},{9,8},{10,11... | collective-permute-start | bytes 3145736 | tf_op jit(solution)/shard_map/ppermute | solution.py:369
  431.9 154.8 %collective-permute-start.29 = (bf16[512,1024]{1,0:T(8,128)(2,1)}, bf16[512,1024]{1,0:T(8,128)(2,1)}, u32[]{:S(2)}, u32[]{:S(2)}) collective-permute-start(bf16[512,1024]{1,0:T(8,128)(2,1)} %add_convert_fusion.3), channel_id=1, source_target_pairs={{0,3},{1,2},{2,1},{3,0},{4,7},{5,6},{6,5},{7,4},{8,11},{9,10},{10,... | collective-permute-start | bytes 3145736 | tf_op jit(solution)/shard_map/ppermute | solution.py:369
  435.7 48.2 %collective-permute-start.50 = (bf16[288,384]{1,0:T(8,128)(2,1)S(1)}, bf16[288,384]{1,0:T(8,128)(2,1)S(1)}, u32[]{:S(2)}, u32[]{:S(2)}) collective-permute-start(bf16[288,384]{1,0:T(8,128)(2,1)S(1)} %copy-done.39), channel_id=1, source_target_pairs={{0,8},{4,12},{8,0},{12,4},{16,24},{20,28},{24,16},{28,20},{1,9},{5... | collective-permute-start | bytes 663560 | tf_op jit(solution)/shard_map/ppermute | solution.py:378
  436.9 165.5 %collective-permute-start.61 = (bf16[512,1024]{1,0:T(8,128)(2,1)}, bf16[512,1024]{1,0:T(8,128)(2,1)}, u32[]{:S(2)}, u32[]{:S(2)}) collective-permute-start(bf16[512,1024]{1,0:T(8,128)(2,1)} %pad_maximum_fusion.4), channel_id=1, source_target_pairs={{0,8},{4,12},{8,0},{12,4},{16,24},{20,28},{24,16},{28,20},{1,9},{5... | collective-permute-start | bytes 3145736 | tf_op jit(solution)/shard_map/ppermute | solution.py:378
  437.9 28.5 %collective-permute-start.40 = (bf16[128,384]{1,0:T(8,128)(2,1)}, bf16[128,384]{1,0:T(8,128)(2,1)S(1)}, u32[]{:S(2)}, u32[]{:S(2)}) collective-permute-start(bf16[128,384]{1,0:T(8,128)(2,1)} %constant_dynamic-slice_fusion.5), channel_id=1, source_target_pairs={{0,16},{4,20},{8,24},{12,28},{16,0},{20,4},{24,8},{28,12},{1,17},{... | collective-permute-start | bytes 294920 | tf_op jit(solution)/shard_map/ppermute | solution.py:378
  483.4 123.1 %collective-permute-start.60 = (bf16[512,1024]{1,0:T(8,128)(2,1)}, bf16[512,1024]{1,0:T(8,128)(2,1)}, u32[]{:S(2)}, u32[]{:S(2)}) collective-permute-start(bf16[512,1024]{1,0:T(8,128)(2,1)} %pad_maximum_fusion.3), channel_id=1, source_target_pairs={{0,4},{4,0},{8,12},{12,8},{16,20},{20,16},{24,28},{28,24},{1,5},{5... | collective-permute-start | bytes 3145736 | tf_op jit(solution)/shard_map/ppermute | solution.py:378
  484.0 23.5 %collective-permute-start.58 = (bf16[64,1024]{1,0:T(8,128)(2,1)S(1)}, bf16[64,1024]{1,0:T(8,128)(2,1)S(1)}, u32[]{:S(2)}, u32[]{:S(2)}) collective-permute-start(bf16[64,1024]{1,0:T(8,128)(2,1)S(1)} %pad_maximum_fusion.18), channel_id=1, source_target_pairs={{0,4},{4,0},{8,12},{12,8},{16,20},{20,16},{24,28},{28,24},{1,5},{5... | collective-permute-start | bytes 393224 | tf_op jit(solution)/shard_map/ppermute | solution.py:378
  597.8 21.0 %collective-permute-start.30 = (bf16[512,1024]{1,0:T(8,128)(2,1)S(1)}, bf16[512,1024]{1,0:T(8,128)(2,1)S(1)}, u32[]{:S(2)}, u32[]{:S(2)}) collective-permute-start(bf16[512,1024]{1,0:T(8,128)(2,1)S(1)} %convolution_convert_fusion.2), channel_id=1, source_target_pairs={{0,1},{1,0},{2,3},{3,2},{4,5},{5,4},{6,7},{7,6},{8,9},{9,8},{10,11... | collective-permute-start | bytes 3145736 | tf_op jit(solution)/shard_map/ppermute | solution.py:369
  606.3 25.5 %collective-permute-start.32 = (bf16[512,1024]{1,0:T(8,128)(2,1)S(1)}, bf16[512,1024]{1,0:T(8,128)(2,1)S(1)}, u32[]{:S(2)}, u32[]{:S(2)}) collective-permute-start(bf16[512,1024]{1,0:T(8,128)(2,1)S(1)} %add_convert_fusion.2), channel_id=1, source_target_pairs={{0,3},{1,2},{2,1},{3,0},{4,7},{5,6},{6,5},{7,4},{8,11},{9,10},{10,... | collective-permute-start | bytes 3145736 | tf_op jit(solution)/shard_map/ppermute | solution.py:369
  (115 other events, 985.8 us)

commit v2 on v1

--- a/solution.py
+++ b/solution.py
@@ -103,7 +103,7 @@
     down=pltpu.roll(x,HDIM//2,1)
     return jnp.where(lane%HDIM<HDIM//2,up,down)
 
-def attn_bwd_kernel(last, pair, codes, q_ref,k_ref,v_ref,do_ref,o_ref,lse_ref,segq_ref,segk_ref,cos_ref,sin_ref,cosk_ref,sink_ref,*rest):
+def attn_bwd_kernel(last, codes, q_ref,k_ref,v_ref,do_ref,o_ref,lse_ref,segq_ref,segk_ref,cos_ref,sin_ref,cosk_ref,sink_ref,*rest):
     if last:
         dk0_ref,dv0_ref,gq_ref,gk_ref,gv_ref,bsum_ref,kt,qm,dom,delta,dq,dk,dv=rest
     else:
@@ -155,7 +155,7 @@
             hr=slice(h*HDIM,(h+1)*HDIM)
             qh=qm[h,rows,:]; dh=dom[h,rows,:]
             s=lax.dot_general(k_ref[:,lanes],qh,NT,preferred_element_type=f32)*(scale*LOG2E)
-            prob=jnp.exp2(s-lse_ref[2*pair+h:2*pair+h+1,rows])
+            prob=jnp.exp2(s-lse_ref[h:h+1,rows])
             if masked: prob=jnp.where(allowed,prob,0.0)
             dp=lax.dot_general(v_ref[:,lanes],dh,NT,preferred_element_type=f32)
             ds=(prob*(dp-delta[h:h+1,rows])).astype(bf16)
@@ -193,31 +193,30 @@
             return carry
         lax.fori_loop(0,nqb,fin,0)
 
-def attn_bwd(codes,q,k,v,do,o,lse,segq,segk,cos,sin,part,pair,carried):
-    rows=k.shape[0]
-    cols=2*HDIM
+def attn_bwd(codes,q,k,v,do,o,lse,segq,segk,cos,sin,part,carried):
+    rows,cols=k.shape
     half=do.shape[0]
+    heads=cols//HDIM
     nb=rows//BLK
     last=carried is not None
+    mine=lambda n: pl.BlockSpec((half,n),lambda i,c:(part,0))
     here=lambda n: pl.BlockSpec((half,n),lambda i,c:(0,0))
-    mine=lambda n,col: pl.BlockSpec((half,n),lambda i,c:(part,col))
-    held=pl.BlockSpec((half,cols),lambda i,c:(0,pair))
-    blk=lambda n,col: pl.BlockSpec((BLK,n),lambda i,c:(i,col))
+    blk=lambda n: pl.BlockSpec((BLK,n),lambda i,c:(i,0))
     kdtype=bf16 if last else f32
     return pl.pallas_call(
-        partial(attn_bwd_kernel,last,pair),
+        partial(attn_bwd_kernel,last),
         out_shape=(jax.ShapeDtypeStruct((half,cols),bf16),jax.ShapeDtypeStruct((rows,cols),kdtype),
                    jax.ShapeDtypeStruct((rows,cols),kdtype),jax.ShapeDtypeStruct((8,cols),f32)),
         grid_spec=pltpu.PrefetchScalarGridSpec(num_scalar_prefetch=1,grid=(nb,),
-            in_specs=[mine(cols,pair),blk(cols,pair),blk(cols,pair),held,held,pl.BlockSpec((8,half),lambda i,c:(0,0)),
-                      pl.BlockSpec((1,half),lambda i,c:(0,part)),blk(1,0),mine(128,0),mine(128,0),blk(128,0),blk(128,0)]
-                     +([blk(cols,0),blk(cols,0)] if last else []),
-            out_specs=[here(cols),blk(cols,0),blk(cols,0),pl.BlockSpec((8,cols),lambda i,c:(0,0))],
-            scratch_shapes=[pltpu.VMEM((cols,BLK),bf16),pltpu.VMEM((2,half,128),bf16),pltpu.VMEM((2,half,128),bf16),
+            in_specs=[mine(cols),blk(cols),blk(cols),here(cols),here(cols),pl.BlockSpec((8,half),lambda i,c:(0,0)),
+                      pl.BlockSpec((1,half),lambda i,c:(0,part)),blk(1),mine(128),mine(128),blk(128),blk(128)]
+                     +([blk(cols),blk(cols)] if last else []),
+            out_specs=[here(cols),blk(cols),blk(cols),pl.BlockSpec((8,cols),lambda i,c:(0,0))],
+            scratch_shapes=[pltpu.VMEM((cols,BLK),bf16),pltpu.VMEM((heads,half,128),bf16),pltpu.VMEM((heads,half,128),bf16),
                             pltpu.VMEM((8,half),f32),pltpu.VMEM((cols,half),f32),pltpu.VMEM((BLK,cols),f32),pltpu.VMEM((BLK,cols),f32)]),
         compiler_params=pltpu.CompilerParams(dimension_semantics=("arbitrary",)),
         name="attn_bwd",
-        cost_estimate=work(60*half*rows*cols),
+        cost_estimate=work(1),
     )(codes,q,k,v,do,o,lse,segq,segk,cos,sin,cos,sin,*(carried or ()))
 
 def block_codes(seg,pad_seg,skip_pad):
@@ -322,14 +321,11 @@
     )(*xs,*gs,w1,b1,w2,*kept)
 
 
-def back_kernel(n,pairs,*refs):
+def back_kernel(n,gq_ref,gk_ref,gv_ref,w_ref,oa_ref,ob_ref):
     i=pl.program_id(0)
-    w_ref,oa_ref,ob_ref=refs[-3:]
-    y=0.0
-    for c in range(3):
-        g=jnp.concatenate([refs[c*pairs+p][...] for p in range(pairs)],axis=1)
-        y=y+lax.dot_general(g,w_ref[c],NT,preferred_element_type=f32)
-    y=y.astype(bf16)
+    y=lax.dot_general(gq_ref[...],w_ref[0],NT,preferred_element_type=f32)
+    y=y+lax.dot_general(gk_ref[...],w_ref[1],NT,preferred_element_type=f32)
+    y=(y+lax.dot_general(gv_ref[...],w_ref[2],NT,preferred_element_type=f32)).astype(bf16)
     @pl.when(i<n)
     def _(): oa_ref[...]=y
     @pl.when(i>=n)
@@ -337,24 +333,23 @@
 
 
 def back_rows(gq,gk,gv,w,part):
-    half,cols=gq[0].shape
+    half,cols=gq.shape
     rows=half//2
     d=w.shape[1]
     tile=min(512,rows)
     n=rows//tile
     off=part*2*n
     row=pl.BlockSpec((tile,cols),lambda i:(i+off,0))
-    pairs=len(gq)
     return pl.pallas_call(
-        partial(back_kernel,n,pairs),
+        partial(back_kernel,n),
         grid=(2*n,),
         out_shape=[jax.ShapeDtypeStruct((rows,d),bf16)]*2,
-        in_specs=[pl.BlockSpec((tile,cols),lambda i:(i,0))]*pairs+[row]*(2*pairs)+[pl.BlockSpec(w.shape,lambda i:(0,0,0))],
+        in_specs=[pl.BlockSpec((tile,cols),lambda i:(i,0)),row,row,pl.BlockSpec(w.shape,lambda i:(0,0,0))],
         out_specs=two(tile,n,d),
         compiler_params=pltpu.CompilerParams(dimension_semantics=("arbitrary",)),
         name="back",
-        cost_estimate=work(12*rows*d*cols*pairs),
-    )(*gq,*gk,*gv,w)
+        cost_estimate=work(1),
+    )(gq,gk,gv,w)
 
 
 def norm_rows(values_in, gain_row, shift_row):
@@ -387,10 +382,10 @@
     def operand(self):
         bit,halving=self.stages[self.at]
         if not halving: return self.cur
-        half=self.cur.shape[0]//2
         up=(lax.axis_index("dp")>>bit)&1
-        self.kept=lax.dynamic_slice_in_dim(self.cur,up*half,half,0)
-        return lax.dynamic_slice_in_dim(self.cur,(1-up)*half,half,0)
+        halves=self.cur.reshape(2,-1,self.cur.shape[1])
+        self.kept=lax.dynamic_index_in_dim(halves,up,0,False)
+        return lax.dynamic_index_in_dim(halves,1-up,0,False)
 
     def start(self,operand):
         self.sent=operand
@@ -509,9 +504,7 @@
     grad_w1=tn(jnp.concatenate([low_two,near,far,far_pair],axis=0),gp).astype(bf16)
     grad_w2=tn(hid,jnp.concatenate(gm,axis=0)).astype(bf16)
     across,grad_w1,grad_w2=lax.optimization_barrier((across,grad_w1,grad_w2))
-    low_order=tuple(range(bits))
-    swapped=(1,0)+tuple(range(2,bits))
-    wsums=[DpSum(grad_w1,low_order),DpSum(grad_w2,swapped)]
+    wsum=lax.psum_scatter(jnp.concatenate([grad_w1,grad_w2],axis=0),"dp",scatter_dimension=0,tiled=True)
     grad_resid_two,grad_gain_two,grad_shift_two=norm_two_back(mine+across.astype(f32))
 
     grad_resid_one=grad_y+grad_resid_two
@@ -521,73 +514,53 @@
     ghead=lambda a: lax.dot_general(a,w_proj,NT,preferred_element_type=f32).astype(bf16)
     bcodes=block_codes(seg,slots,True)
     do_near=jnp.concatenate([ghead(grad_attn),ghead(near)],axis=0)
-    do_near=begin(wsums,do_near)
-    bwd_near=lambda pair,do: attn_bwd(bcodes[:hb],q,k,v,do,att_near,lse_near,segq,segk,cos,sin,0,pair,None)
-    bwd_far=lambda pair,do,carried: attn_bwd(bcodes[hb:],q,k,v,do,att_far,lse_far,segq,segk,cos,sin,1,pair,carried)
-    gq0n,dk,dv,bs0=bwd_near(0,do_near)
-    far,dk,dv=lax.optimization_barrier((far,dk,dv))
-    dk=settle(wsums,dk)
-    far_pair=flip(far,1)
-    do_far=jnp.concatenate([ghead(far),ghead(far_pair)],axis=0)
-    do_far=begin(wsums,do_far)
-    gq0f,gk0,gv0,bs1=bwd_far(0,do_far,(dk,dv))
-    gk0=settle(wsums,gk0)
-    all1=jnp.concatenate(n1,axis=0)
-    wpart=lambda gqn,gqf,gk,gv: tn(all1,jnp.concatenate([jnp.concatenate([gqn,gqf],axis=0),gk,gv],axis=1)).astype(bf16)
-    do_near,gk0=lax.optimization_barrier((do_near,gk0))
-    do_near=begin(wsums,do_near)
-    gq1n,dk,dv,bs2=bwd_near(1,do_near)
-    dk=settle(wsums,dk)
-    dk=begin(wsums,dk)
-    dk,gq0n,alla,atts=lax.optimization_barrier((dk,gq0n,jnp.concatenate([grad_attn,near,far,far_pair],axis=0),
-                                                jnp.concatenate([att_near,att_far],axis=0)))
-    tail0=[DpSum(wpart(gq0n,gq0f,gk0,gv0),low_order),DpSum(tn(atts,alla).astype(bf16),swapped)]
-    dk=begin(tail0,dk)
-    gq1f,gk1,gv1,bs3=bwd_far(1,do_far,(dk,dv))
-    gk1=settle(wsums+tail0,gk1)
-    gk1=begin(wsums+tail0,gk1)
-    r2,r3=back_rows([gq0f,gq1f],[gk0,gk1],[gv0,gv1],w_qkv,1)
-    across=pair_sum(r3,r2).astype(bf16)
-    gq1n,across,hid=lax.optimization_barrier((gq1n,across,hid))
-    across=flip(across,3)
-    wqkv1=wpart(gq1n,gq1f,gk1,gv1)
     early=jnp.stack([grad_gain_two,grad_shift_two,jnp.sum(grad_attn,axis=0,dtype=f32),jnp.sum(grad_mlp,axis=0,dtype=f32)])
     early=early+flip(early,1)
     early=early+flip(early,2)
+    do_near,early=lax.optimization_barrier((do_near,early))
+    gq_near,dk,dv,bs0=attn_bwd(bcodes[:hb],q,k,v,do_near,att_near,lse_near,segq,segk,cos,sin,0,None)
+    far,dk,dv=lax.optimization_barrier((far,dk,dv))
+    far_pair=flip(far,1)
+    do_far=jnp.concatenate([ghead(far),ghead(far_pair)],axis=0)
+    alla=jnp.concatenate([grad_attn,near,far,far_pair],axis=0)
+    grad_proj=tn(jnp.concatenate([att_near,att_far],axis=0),alla).astype(bf16)
+    do_far,grad_proj=lax.optimization_barrier((do_far,grad_proj))
+    gq_far,gk,gv,bs1=attn_bwd(bcodes[hb:],q,k,v,do_far,att_far,lse_far,segq,segk,cos,sin,1,(dk,dv))
+    gk,wsum=lax.optimization_barrier((gk,wsum))
+    wsum=lax.all_gather(wsum,"dp",axis=0,tiled=True)
+    grad_w1,grad_w2=wsum[:tokens.shape[1]],wsum[tokens.shape[1]:]
+    r2,r3=back_rows(gq_far,gk,gv,w_qkv,1)
+    across=pair_sum(r3,r2).astype(bf16)
+    gq_near,gk,gv,across,early=lax.optimization_barrier((gq_near,gk,gv,across,early))
+    across=flip(across,3)
+    g_all=jnp.concatenate([jnp.concatenate([gq_near,gq_far],axis=0),gk,gv],axis=1)
+    grad_wqkv=tn(jnp.concatenate(n1,axis=0),g_all).astype(bf16)
     d=tokens.shape[1]
-    bsum=jnp.concatenate([(bs0+bs1)[:3],(bs2+bs3)[:3]],axis=1)
     sizes=(3*cols,db.shape[1],early.size)
-    width=wqkv1.shape[1]
-    pad=(-sum(sizes))%(width*8<<bits)
-    small=jnp.concatenate([bsum.reshape(-1),db[0],early.reshape(-1),jnp.zeros((pad,),f32)]).astype(bf16).reshape(-1,width)
-    hd=d//2
-    tail1=[DpSum(wqkv1[:hd],low_order),DpSum(jnp.concatenate([wqkv1[hd:],small],axis=0),swapped)]
-    gq_near=[gq0n,gq1n]
-    gq1n_late=begin(tail1,gq1n)
-    r0,r1=back_rows([gq0n,gq1n_late],[gk0,gk1],[gv0,gv1],w_qkv,0)
-    r0=settle(wsums+tail0,r0)
-    r0=begin(wsums+tail0,r0)
+    pad=(-sum(sizes))%(8*cols<<bits)
+    small=jnp.concatenate([(bs0+bs1)[:3].reshape(-1),db[0],early.reshape(-1),jnp.zeros((pad,),f32)]).astype(bf16).reshape(-1,cols)
+    tail_a=DpSum(jnp.concatenate([grad_wqkv[:,:cols],grad_wqkv[:,cols:2*cols]],axis=0),tuple(range(bits)))
+    tail_b=DpSum(jnp.concatenate([grad_wqkv[:,2*cols:],grad_proj.reshape(-1,cols),small],axis=0),(1,0)+tuple(range(2,bits)))
+    tails=(tail_a,tail_b)
+    for t in tails: t.start(t.operand())
+    *gots,hid,gq_near=lax.optimization_barrier((tail_a.got,tail_b.got,hid,gq_near))
+    for t,got in zip(tails,gots): t.finish(got)
+    tail_a,tail_b=[t.rest() for t in tails]
+    r0,r1=back_rows(gq_near,gk,gv,w_qkv,0)
     mine=pair_sum(r0,r1)
-    across,hid=lax.optimization_barrier((across,hid))
     o=[jnp.dot(hid[j*tok:(j+1)*tok],w_fc2,preferred_element_type=f32).astype(bf16) for j in range(ranks)]
     o_across=flip(pair_sum(o[3],o[2]).astype(bf16),3)
     output=(resid_one+pair_sum(o[0],o[1])+o_across.astype(f32)+shifts[3]).astype(bf16)
-    for t in wsums+tail0+tail1:
-        if hasattr(t,"got"): t.finish(t.got)
-    grad_w1,grad_w2=[t.rest() for t in wsums]
-    wqkv0,grad_proj=[t.rest() for t in tail0]
-    tail_a,tail_b=[t.rest() for t in tail1]
-    wqkv1=jnp.concatenate([tail_a,tail_b[:d-hd]],axis=0)
-    spread=lambda w: jnp.stack([w[:,c*width//3:(c+1)*width//3] for c in range(3)])
-    grad_wqkv=jnp.concatenate([spread(wqkv0),spread(wqkv1)],axis=2).astype(f32)
-    small=tail_b[d-hd:].reshape(-1).astype(f32)
+    grad_wqkv=jnp.stack([tail_a[:d],tail_a[d:],tail_b[:d]]).astype(f32)
+    grad_wproj=tail_b[d:2*d].reshape(cols,d).astype(f32)
+    small=tail_b[2*d:].reshape(-1).astype(f32)
     grad_bqkv=small[:sizes[0]].reshape(3,cols)
     grad_b1=small[sizes[0]:sizes[0]+sizes[1]]
     early=small[sizes[0]+sizes[1]:sum(sizes)].reshape(4,d)
     grad_x_norm,grad_gain_one,grad_shift_one=norm_one_back(mine+across.astype(f32))
     grad_tokens=(grad_resid_one+grad_x_norm).astype(bf16)
     one=all_sum(jnp.stack([grad_gain_one,grad_shift_one]))
-    return (output,grad_tokens,grad_wqkv,grad_bqkv,grad_proj.astype(f32),grad_w1.astype(f32),grad_b1,grad_w2.astype(f32),
+    return (output,grad_tokens,grad_wqkv,grad_bqkv,grad_wproj,grad_w1.astype(f32),grad_b1,grad_w2.astype(f32),
             jnp.stack([one[0],early[0]]),jnp.stack([one[1],early[1],early[2],early[3]]))
 
 

time: 646 us -> 574 us (0.89)
  starting transfers between devices: 78.1 us -> 29.5 us
  local copies, waits for them, and re-layouts: 36.1 us -> 13.6 us
  other arithmetic: 77.4 us -> 60.1 us
  Pallas kernels: 210 us -> 194 us
  waiting for transfers between devices: 188 us -> 201 us
  between operations: 2.61 us -> 15.5 us
  matrix products: 41.5 us -> 50 us
    ppermute x39 -> x15, starting transfers between devices: 55.3 us -> 11 us  [dp_flip(): return lax.ppermute(x, 'dp', [(i, i ^ 1 << bit) for i in range(n)])]
    ppermute x28, waiting for transfers between devices: 74.8 us -> 101 us  [flip(): return lax.ppermute(x, 'tensor', [(i, i ^ bits) for i in range(n)])]
    dynamic_slice x17 -> x0, local copies, waits for them, and re-layouts: 22 us -> none  [operand(): return lax.dynamic_slice_in_dim(self.cur, (1 - up) * half, half, 0)]
    pallas_call x6 -> x4, Pallas kernels: 99.8 us -> 83.3 us  [the longest x2 72.1 us: attn_bwd(): pl.pallas_call(partial(attn_bwd_kernel, last), out_shape=(jax.ShapeDtypeS...]
    ppermute x39 -> x15, waiting for transfers between devices: 113 us -> 99.8 us  [dp_flip(): return lax.ppermute(x, 'dp', [(i, i ^ 1 << bit) for i in range(n)])]
    dot_general x4, matrix products: 5.03 us -> 14.7 us  [shards(): jnp.dot(hid[j * tok:(j + 1) * tok], w_fc2, preferred_element_type=f32)]
    convert_element_type x18 -> x6, other arithmetic: 11.6 us -> 2.75 us  [finish(): self.cur = (self.kept.astype(f32) + got.astype(f32)).astype(bf16)]
    select_n x18 -> x4, other arithmetic: 8.86 us -> 0.26 us  [finish(): jnp.where(up, got, self.sent)]
  transfers between devices with their start and end apart: 67 -> 45, of which waited for: 32 -> 26; matrix products, arithmetic and copies ran while one was open for 20% -> 16% of each run, Pallas kernels for 25% -> 24%
where the time goes in v2:
time: 574 us; the launch traced here: 563 us
  waiting for transfers between devices  201 us (35%)
  Pallas kernels  194 us (34%)
  other arithmetic  60.1 us (10%)
  matrix products  50 us (9%)
  starting transfers between devices  29.5 us (5%)
  between operations  15.5 us (3%)
  local copies, waits for them, and re-layouts  13.6 us (2%)
    ppermute x28, waiting for transfers between devices, flip(): return lax.ppermute(x, 'tensor', [(i, i ^ bits) for i in range(n)])  101 us
    ppermute x15, waiting for transfers between devices, dp_flip(): return lax.ppermute(x, 'dp', [(i, i ^ 1 << bit) for i in range(n)])  99.8 us
    pallas_call x2, Pallas kernels, attn_fwd(): pl.pallas_call(attn_fwd_kernel, out_shape=(jax.ShapeDtypeStruct((nblocks...  75 us
    pallas_call x2, Pallas kernels, attn_bwd(): pl.pallas_call(partial(attn_bwd_kernel, last), out_shape=(jax.ShapeDtypeS...  72.1 us
    dot_general x4, matrix products, shards(): lax.dot_general(a, b, (((0,), (0,)), ((), ())), preferred_element_type=f32)  25.1 us
    pallas_call x2, Pallas kernels, mlp_rows(): pl.pallas_call(partial(mlp_kernel, n), grid=(2 * n,), out_shape=[jax.Shap...  24.5 us
    ppermute x28, starting transfers between devices, flip(): return lax.ppermute(x, 'tensor', [(i, i ^ bits) for i in range(n)])  18.2 us
    dot_general x4, matrix products, shards(): jnp.dot(hid[j * tok:(j + 1) * tok], w_fc2, preferred_element_type=f32)  14.7 us
  transfers between devices with their start and end apart: 45, of which 26 were waited for; matrix products, arithmetic and copies ran while one was open for 16% of the time, Pallas kernels for 24%

profile of v2, /device:TPU:0, one launch (start us, length us, event | category | flops | bytes accessed | tf_op | source)
XLA Modules:
  0.0 563.2 jit_solution(8118475353275454536)
XLA Ops:
  16.0 5.8 %sine_multiply_fusion = (f32[2048,128]{1,0:T(8,128)}, f32[2048,128]{1,0:T(8,128)}) fusion(f32[128]{0:T(128)S(1)} %get-tuple-element.221, f32[128]{0:T(128)S(1)} %get-tuple-element.222, f32[2048]{0:T(1024)S(1)} %bitcast.149, f32[128]{0:T(128)S(1)} %get-tuple-element.223, f32[2048]{0:T(1024)S(1)} %bitcast.148, f32[128]{0:T(128)S(1)} %get-tuple-element.224, ...), kind=kLoop, calls=%fused_computation.108 | loop fusion | flops 1572864 | bytes 2123776 | tf_op jit(solution)/shard_map/mul | solution.py:456
  22.8 5.6 qkv.2
  28.3 10.3 %collective-permute-done.xa_ref = bf16[512,1024]{1,0:T(8,128)(2,1)} collective-permute-done((bf16[512,1024]{1,0:T(8,128)(2,1)S(1)}, bf16[512,1024]{1,0:T(8,128)(2,1)}, u32[]{:S(2)}, u32[]{:S(2)}) %collective-permute-start) | collective-permute-done | bytes 1048608 | tf_op jit(solution)/shard_map/ppermute | solution.py:364
  44.3 5.5 qkv.3
  49.7 35.1 %attn_fwd.2 = (bf16[1024,256]{1,0:T(8,128)(2,1)}, f32[8,1024]{1,0:T(8,128)}) custom-call(s32[4,8]{1,0:T(4,128)} %get-tuple-element.216.codes, bf16[2048,256]{1,0:T(8,128)(2,1)} %get-tuple-element.98.q_ref, bf16[2048,256]{1,0:T(8,128)(2,1)} %get-tuple-element.93.k_ref, bf16[2048,256]{1,0:T(8,128)(2,1)} %get-tuple-element.94.v_ref, s32[1,2048]{1,0:T(1,128)} %bitcast.119, ...), custom_call_target="tpu_custom_call" | custom-call | flops 34359738368 | tf_op jit(solution)/shard_map/attn_fwd/pallas_call | solution.py:83
  86.7 6.7 %collective-permute-start.4 = (bf16[512,1024]{1,0:T(8,128)(2,1)}, bf16[512,1024]{1,0:T(8,128)(2,1)}, u32[]{:S(2)}, u32[]{:S(2)}) collective-permute-start(bf16[512,1024]{1,0:T(8,128)(2,1)} %get-tuple-element.96.ga_ref), channel_id=1, source_target_pairs={{0,2},{1,3},{2,0},{3,1},{4,6},{5,7},{6,4},{7,5},{8,10},{9,11},{10,... | collective-permute-start | bytes 3145736 | tf_op jit(solution)/shard_map/ppermute | solution.py:364
  94.8 22.3 %collective-permute-done.4.ga_ref = bf16[512,1024]{1,0:T(8,128)(2,1)} collective-permute-done((bf16[512,1024]{1,0:T(8,128)(2,1)}, bf16[512,1024]{1,0:T(8,128)(2,1)}, u32[]{:S(2)}, u32[]{:S(2)}) %collective-permute-start.4) | collective-permute-done | bytes 1048608 | tf_op jit(solution)/shard_map/ppermute | solution.py:364
  117.7 39.9 %attn_fwd.3 = (bf16[1024,256]{1,0:T(8,128)(2,1)}, f32[8,1024]{1,0:T(8,128)}) custom-call(s32[4,8]{1,0:T(4,128)} %get-tuple-element.215.codes, bf16[2048,256]{1,0:T(8,128)(2,1)} %get-tuple-element.98.q_ref, bf16[2048,256]{1,0:T(8,128)(2,1)} %get-tuple-element.93.k_ref, bf16[2048,256]{1,0:T(8,128)(2,1)} %get-tuple-element.94.v_ref, s32[1,2048]{1,0:T(1,128)} %bitcast.120, ...), custom_call_target="tpu_custom_call" | custom-call | flops 34359738368 | tf_op jit(solution)/shard_map/attn_fwd/pallas_call | solution.py:83
  169.7 12.4 %mlp.2 = (bf16[2048,1024]{1,0:T(8,128)(2,1)}, bf16[2048,1024]{1,0:T(8,128)(2,1)}, bf16[512,1024]{1,0:T(8,128)(2,1)}, bf16[512,1024]{1,0:T(8,128)(2,1)}, f32[1,1024]{1,0:T(1,128)}) custom-call(bf16[512,1024]{1,0:T(8,128)(2,1)} %add_convert_fusion.5.xa_ref, bf16[512,1024]{1,0:T(8,128)(2,1)} %collective-permute-done.7.xb_ref, ...), custom_call_target="tpu_custom_call" | custom-call | flops 6442450944 | tf_op jit(solution)/shard_map/mlp/pallas_call | solution.py:310
  182.1 10.5 %collective-permute-done.10.xa_ref = bf16[512,1024]{1,0:T(8,128)(2,1)} collective-permute-done((bf16[512,1024]{1,0:T(8,128)(2,1)}, bf16[512,1024]{1,0:T(8,128)(2,1)}, u32[]{:S(2)}, u32[]{:S(2)}) %collective-permute-start.10) | collective-permute-done | bytes 1048608 | tf_op jit(solution)/shard_map/ppermute | solution.py:364
  195.6 12.1 %mlp.3 = (bf16[2048,1024]{1,0:T(8,128)(2,1)}, bf16[2048,1024]{1,0:T(8,128)(2,1)}, bf16[512,1024]{1,0:T(8,128)(2,1)}, bf16[512,1024]{1,0:T(8,128)(2,1)}, f32[1,1024]{1,0:T(1,128)}) custom-call(bf16[512,1024]{1,0:T(8,128)(2,1)} %collective-permute-done.10.xa_ref, ...), custom_call_target="tpu_custom_call", output_to_operand_aliasing={{0}: (7, {}), {1}: (8, {})} | custom-call | flops 6442450944 | tf_op jit(solution)/shard_map/mlp/pallas_call | solution.py:310
  212.4 8.1 %fusion.53 = bf16[1024,1024]{1,0:T(8,128)(2,1)S(1)} fusion(bf16[2048,1024]{1,0:T(8,128)(2,1)} %get-tuple-element.146, bf16[512,1024]{1,0:T(8,128)(2,1)} %collective-permute-done.12.gb_ref, bf16[512,1024]{1,0:T(8,128)(2,1)} %collective-permute-done.4.ga_ref, bf16[512,1024]{1,0:T(8,128)(2,1)} %collective-permute-done.8.gb_ref, ...), kind=kOutput, calls=%fused_computation.77 | convolution fusion | flops 4312793088 | bytes 10485760 | tf_op jit(solution)/shard_map/dot_general | solution.py:503
  220.5 6.8 %fusion.56 = bf16[1024,1024]{1,0:T(8,128)(2,1)S(1)} fusion(bf16[2048,1024]{1,0:T(8,128)(2,1)S(1)} %copy-done.46, bf16[512,1024]{1,0:T(8,128)(2,1)} %collective-permute-done.11.xb_ref, bf16[512,1024]{1,0:T(8,128)(2,1)} %collective-permute-done.10.xa_ref, bf16[512,1024]{1,0:T(8,128)(2,1)} %collective-permute-done.7.xb_ref, ...), kind=kOutput, calls=%fused_computation.78 | convolution fusion | flops 4312793088 | bytes 10485760 | tf_op jit(solution)/shard_map/dot_general | solution.py:503
  227.3 10.3 %collective-permute-done.14 = bf16[512,1024]{1,0:T(8,128)(2,1)} collective-permute-done((bf16[512,1024]{1,0:T(8,128)(2,1)S(1)}, bf16[512,1024]{1,0:T(8,128)(2,1)}, u32[]{:S(2)}, u32[]{:S(2)}) %collective-permute-start.14) | collective-permute-done | bytes 1048608 | tf_op jit(solution)/shard_map/ppermute | solution.py:364
  255.3 22.0 %collective-permute-done.17 = f32[4,1024]{1,0:T(4,128)S(1)} collective-permute-done((f32[4,1024]{1,0:T(4,128)S(1)}, f32[4,1024]{1,0:T(4,128)S(1)}, u32[]{:S(2)}, u32[]{:S(2)}) %collective-permute-start.17) | collective-permute-done | bytes 16416 | tf_op jit(solution)/shard_map/ppermute | solution.py:364
  278.7 39.1 %attn_bwd.2 = (bf16[1024,256]{1,0:T(8,128)(2,1)}, f32[2048,256]{1,0:T(8,128)}, f32[2048,256]{1,0:T(8,128)}, f32[8,256]{1,0:T(8,128)}) custom-call(s32[4,8]{1,0:T(4,128)} %get-tuple-element.212.codes, bf16[2048,256]{1,0:T(8,128)(2,1)} %get-tuple-element.98.q_ref, bf16[2048,256]{1,0:T(8,128)(2,1)} %get-tuple-element.93.k_ref, ...), custom_call_target="tpu_custom_call" | custom-call | flops 1 | tf_op jit(solution)/shard_map/attn_bwd/pallas_call | solution.py:206
  326.1 32.9 %attn_bwd.3 = (bf16[1024,256]{1,0:T(8,128)(2,1)}, bf16[2048,256]{1,0:T(8,128)(2,1)}, bf16[2048,256]{1,0:T(8,128)(2,1)}, f32[8,256]{1,0:T(8,128)}) custom-call(s32[4,8]{1,0:T(4,128)} %get-tuple-element.211.codes, bf16[2048,256]{1,0:T(8,128)(2,1)} %get-tuple-element.98.q_ref, bf16[2048,256]{1,0:T(8,128)(2,1)} %get-tuple-element.93.k_ref, ...), custom_call_target="tpu_custom_call" | custom-call | flops 1 | tf_op jit(solution)/shard_map/attn_bwd/pallas_call | solution.py:206
  359.1 5.6 back.2
  371.6 6.6 %fusion.59 = bf16[1024,768]{1,0:T(8,128)(2,1)S(1)} fusion(bf16[2048,256]{1,0:T(8,128)(2,1)} %get-tuple-element.139.gv_ref, bf16[2048,256]{1,0:T(8,128)(2,1)} %get-tuple-element.138.gk_ref, bf16[1024,256]{1,0:T(8,128)(2,1)} %get-tuple-element.133.gq_ref, bf16[1024,256]{1,0:T(8,128)(2,1)} %get-tuple-element.147.gq_ref, bf16[512,1024]{1,0:T(8,128)(2,1)} %copy-done.41, ...), kind=kOutput, calls=%fused_computation.79 | convolution fusion | flops 3251372032 | bytes 8912896 | tf_op jit(solution)/shard_map/dot_general | solution.py:503
  379.3 3.9 collective-permute-start.22
  385.7 19.3 %collective-permute-done.21 = bf16[1024,256]{1,0:T(8,128)(2,1)} collective-permute-done((bf16[1024,256]{1,0:T(8,128)(2,1)}, bf16[1024,256]{1,0:T(8,128)(2,1)}, u32[]{:S(2)}, u32[]{:S(2)}) %collective-permute-start.21) | collective-permute-done | bytes 524320 | tf_op jit(solution)/shard_map/ppermute | solution.py:373
  405.0 4.2 convolution_convert_fusion
  412.7 5.6 %back.3 = (bf16[512,1024]{1,0:T(8,128)(2,1)}, bf16[512,1024]{1,0:T(8,128)(2,1)}) custom-call(bf16[1024,256]{1,0:T(8,128)(2,1)} %get-tuple-element.147.gq_ref, bf16[2048,256]{1,0:T(8,128)(2,1)} %get-tuple-element.138.gk_ref, bf16[2048,256]{1,0:T(8,128)(2,1)} %get-tuple-element.139.gv_ref, bf16[3,1024,256]{2,1,0:T(8,128)(2,1)} %w_ref.7), custom_call_target="tpu_custom_call" | custom-call | flops 1 | tf_op jit(solution)/shard_map/back/pallas_call | solution.py:343
  425.2 17.8 %collective-permute-done.28 = bf16[512,256]{1,0:T(8,128)(2,1)S(1)} collective-permute-done((bf16[512,256]{1,0:T(8,128)(2,1)S(1)}, bf16[512,256]{1,0:T(8,128)(2,1)S(1)}, u32[]{:S(2)}, u32[]{:S(2)}) %collective-permute-start.28) | collective-permute-done | bytes 262176 | tf_op jit(solution)/shard_map/ppermute | solution.py:373
  443.5 17.3 %collective-permute-done.29 = bf16[256,256]{1,0:T(8,128)(2,1)S(1)} collective-permute-done((bf16[256,256]{1,0:T(8,128)(2,1)S(1)}, bf16[256,256]{1,0:T(8,128)(2,1)S(1)}, u32[]{:S(2)}, u32[]{:S(2)}) %collective-permute-start.29) | collective-permute-done | bytes 131104 | tf_op jit(solution)/shard_map/ppermute | solution.py:373
  460.9 9.9 %collective-permute-done.34 = bf16[264,256]{1,0:T(8,128)(2,1)S(1)} collective-permute-done((bf16[264,256]{1,0:T(8,128)(2,1)S(1)}, bf16[264,256]{1,0:T(8,128)(2,1)S(1)}, u32[]{:S(2)}, u32[]{:S(2)}) %collective-permute-start.34) | collective-permute-done | bytes 135200 | tf_op jit(solution)/shard_map/ppermute | solution.py:373
  470.9 8.1 %collective-permute-done.30 = bf16[256,256]{1,0:T(8,128)(2,1)S(1)} collective-permute-done((bf16[256,256]{1,0:T(8,128)(2,1)S(1)}, bf16[256,256]{1,0:T(8,128)(2,1)S(1)}, u32[]{:S(2)}, u32[]{:S(2)}) %collective-permute-start.30) | collective-permute-done | bytes 131104 | tf_op jit(solution)/shard_map/ppermute | solution.py:373
  479.0 8.9 %collective-permute-done.35 = bf16[264,256]{1,0:T(8,128)(2,1)S(1)} collective-permute-done((bf16[264,256]{1,0:T(8,128)(2,1)S(1)}, bf16[264,256]{1,0:T(8,128)(2,1)S(1)}, u32[]{:S(2)}, u32[]{:S(2)}) %collective-permute-start.35) | collective-permute-done | bytes 135200 | tf_op jit(solution)/shard_map/ppermute | solution.py:373
  488.0 8.1 %collective-permute-done.31 = bf16[512,256]{1,0:T(8,128)(2,1)S(1)} collective-permute-done((bf16[512,256]{1,0:T(8,128)(2,1)S(1)}, bf16[512,256]{1,0:T(8,128)(2,1)S(1)}, u32[]{:S(2)}, u32[]{:S(2)}) %collective-permute-start.31) | collective-permute-done | bytes 262176 | tf_op jit(solution)/shard_map/ppermute | solution.py:373
  497.1 6.6 %collective-permute-done.36 = bf16[528,256]{1,0:T(8,128)(2,1)S(1)} collective-permute-done((bf16[528,256]{1,0:T(8,128)(2,1)S(1)}, bf16[528,256]{1,0:T(8,128)(2,1)S(1)}, u32[]{:S(2)}, u32[]{:S(2)}) %collective-permute-start.36) | collective-permute-done | bytes 270368 | tf_op jit(solution)/shard_map/ppermute | solution.py:373
  538.2 7.8 %collective-permute-done.25 = bf16[512,1024]{1,0:T(8,128)(2,1)} collective-permute-done((bf16[512,1024]{1,0:T(8,128)(2,1)}, bf16[512,1024]{1,0:T(8,128)(2,1)}, u32[]{:S(2)}, u32[]{:S(2)}) %collective-permute-start.25) | collective-permute-done | bytes 1048608 | tf_op jit(solution)/shard_map/ppermute | solution.py:364
  549.3 6.7 %slice_convert_fusion = (f32[1024,1024]{1,0:T(8,128)}, f32[1024,1024]{1,0:T(8,128)}) fusion(bf16[2048,1024]{1,0:T(8,128)(2,1)} %all-gather.2.cloned.1.call-done), kind=kLoop, calls=%fused_computation.58 | loop fusion | flops 2097152 | bytes 12582912 | tf_op jit(solution)/shard_map/convert_element_type | solution.py:563
  (285 shorter events, 126.1 us)
Async XLA Ops:
  7.3 351.8 %reduce-scatter.2.cloned.1.call-start = ((), (), s32[]{:S(2)}) async-start(), calls=%async_computation.1 | async-start | bytes 4718592 | tf_op jit(solution)/shard_map/reduce_scatter | solution.py:507
  11.7 10.0 %collective-permute-start.1 = (bf16[512,1024]{1,0:T(8,128)(2,1)S(1)}, bf16[512,1024]{1,0:T(8,128)(2,1)S(1)}, u32[]{:S(2)}, u32[]{:S(2)}) collective-permute-start(bf16[512,1024]{1,0:T(8,128)(2,1)S(1)} %fusion.46.xa_ref), channel_id=1, source_target_pairs={{0,1},{1,0},{2,3},{3,2},{4,5},{5,4},{6,7},{7,6},{8,9},{9,8},{10,11... | collective-permute-start | bytes 3145736 | tf_op jit(solution)/shard_map/ppermute | solution.py:364
  12.2 26.4 %collective-permute-start = (bf16[512,1024]{1,0:T(8,128)(2,1)S(1)}, bf16[512,1024]{1,0:T(8,128)(2,1)}, u32[]{:S(2)}, u32[]{:S(2)}) collective-permute-start(bf16[512,1024]{1,0:T(8,128)(2,1)S(1)} %fusion.46.xa_ref), channel_id=1, source_target_pairs={{0,2},{1,3},{2,0},{3,1},{4,6},{5,7},{6,4},{7,5},{8,10},{9,11},{10,... | collective-permute-start | bytes 3145736 | tf_op jit(solution)/shard_map/ppermute | solution.py:364
  38.6 4.7 collective-permute-start.2
  86.2 7.2 %collective-permute-start.3 = (bf16[512,1024]{1,0:T(8,128)(2,1)S(1)}, bf16[512,1024]{1,0:T(8,128)(2,1)S(1)}, u32[]{:S(2)}, u32[]{:S(2)}) collective-permute-start(bf16[512,1024]{1,0:T(8,128)(2,1)S(1)} %convolution_convert_fusion.6), channel_id=1, source_target_pairs={{0,1},{1,0},{2,3},{3,2},{4,5},{5,4},{6,7},{7,6},{8,9},{9,8},{10,11... | collective-permute-start | bytes 3145736 | tf_op jit(solution)/shard_map/ppermute | solution.py:364
  86.7 30.4 %collective-permute-start.4 = (bf16[512,1024]{1,0:T(8,128)(2,1)}, bf16[512,1024]{1,0:T(8,128)(2,1)}, u32[]{:S(2)}, u32[]{:S(2)}) collective-permute-start(bf16[512,1024]{1,0:T(8,128)(2,1)} %get-tuple-element.96.ga_ref), channel_id=1, source_target_pairs={{0,2},{1,3},{2,0},{3,1},{4,6},{5,7},{6,4},{7,5},{8,10},{9,11},{10,... | collective-permute-start | bytes 3145736 | tf_op jit(solution)/shard_map/ppermute | solution.py:364
  117.2 40.5 %collective-permute-start.5 = (bf16[512,1024]{1,0:T(8,128)(2,1)S(1)}, bf16[512,1024]{1,0:T(8,128)(2,1)S(1)}, u32[]{:S(2)}, u32[]{:S(2)}) collective-permute-start(bf16[512,1024]{1,0:T(8,128)(2,1)S(1)} %add_convert_fusion.6), channel_id=1, source_target_pairs={{0,3},{1,2},{2,1},{3,0},{4,7},{5,6},{6,5},{7,4},{8,11},{9,10},{10,... | collective-permute-start | bytes 3145736 | tf_op jit(solution)/shard_map/ppermute | solution.py:364
  160.7 7.1 %collective-permute-start.8 = (bf16[512,1024]{1,0:T(8,128)(2,1)}, bf16[512,1024]{1,0:T(8,128)(2,1)}, u32[]{:S(2)}, u32[]{:S(2)}) collective-permute-start(bf16[512,1024]{1,0:T(8,128)(2,1)} %get-tuple-element.96.ga_ref), channel_id=1, source_target_pairs={{0,1},{1,0},{2,3},{3,2},{4,5},{5,4},{6,7},{7,6},{8,9},{9,8},{10,11... | collective-permute-start | bytes 3145736 | tf_op jit(solution)/shard_map/ppermute | solution.py:364
  167.1 25.5 %collective-permute-start.10 = (bf16[512,1024]{1,0:T(8,128)(2,1)}, bf16[512,1024]{1,0:T(8,128)(2,1)}, u32[]{:S(2)}, u32[]{:S(2)}) collective-permute-start(bf16[512,1024]{1,0:T(8,128)(2,1)} %add_convert_fusion.5.xa_ref), channel_id=1, source_target_pairs={{0,2},{1,3},{2,0},{3,1},{4,6},{5,7},{6,4},{7,5},{8,10},{9,11},{10,... | collective-permute-start | bytes 3145736 | tf_op jit(solution)/shard_map/ppermute | solution.py:364
  167.7 24.9 %collective-permute-start.12 = (bf16[512,1024]{1,0:T(8,128)(2,1)}, bf16[512,1024]{1,0:T(8,128)(2,1)}, u32[]{:S(2)}, u32[]{:S(2)}) collective-permute-start(bf16[512,1024]{1,0:T(8,128)(2,1)} %collective-permute-done.4.ga_ref), channel_id=1, source_target_pairs={{0,1},{1,0},{2,3},{3,2},{4,5},{5,4},{6,7},{7,6},{8,9},{9,8},{10,11... | collective-permute-start | bytes 3145736 | tf_op jit(solution)/shard_map/ppermute | solution.py:364
  212.3 25.3 %collective-permute-start.14 = (bf16[512,1024]{1,0:T(8,128)(2,1)S(1)}, bf16[512,1024]{1,0:T(8,128)(2,1)}, u32[]{:S(2)}, u32[]{:S(2)}) collective-permute-start(bf16[512,1024]{1,0:T(8,128)(2,1)S(1)} %add_convert_fusion.4), channel_id=1, source_target_pairs={{0,3},{1,2},{2,1},{3,0},{4,7},{5,6},{6,5},{7,4},{8,11},{9,10},{10,... | collective-permute-start | bytes 3145736 | tf_op jit(solution)/shard_map/ppermute | solution.py:364
  240.1 309.2 %all-gather.2.cloned.1.call-start = ((), (), s32[]{:S(2)}) async-start(), calls=%async_computation.2 | async-start | bytes 4718592 | tf_op jit(solution)/shard_map/all_gather | solution.py:530
  250.3 27.1 %collective-permute-start.15 = (bf16[512,1024]{1,0:T(8,128)(2,1)}, bf16[512,1024]{1,0:T(8,128)(2,1)S(1)}, u32[]{:S(2)}, u32[]{:S(2)}) collective-permute-start(bf16[512,1024]{1,0:T(8,128)(2,1)} %get-tuple-element.165), channel_id=1, source_target_pairs={{0,1},{1,0},{2,3},{3,2},{4,5},{5,4},{6,7},{7,6},{8,9},{9,8},{10,11... | collective-permute-start | bytes 3145736 | tf_op jit(solution)/shard_map/ppermute | solution.py:364
  251.5 66.4 %collective-permute-start.18 = (bf16[512,1024]{1,0:T(8,128)(2,1)}, bf16[512,1024]{1,0:T(8,128)(2,1)}, u32[]{:S(2)}, u32[]{:S(2)}) collective-permute-start(bf16[512,1024]{1,0:T(8,128)(2,1)} %get-tuple-element.165), channel_id=1, source_target_pairs={{0,2},{1,3},{2,0},{3,1},{4,6},{5,7},{6,4},{7,5},{8,10},{9,11},{10,... | collective-permute-start | bytes 3145736 | tf_op jit(solution)/shard_map/ppermute | solution.py:364
  253.2 24.1 %collective-permute-start.17 = (f32[4,1024]{1,0:T(4,128)S(1)}, f32[4,1024]{1,0:T(4,128)S(1)}, u32[]{:S(2)}, u32[]{:S(2)}) collective-permute-start(f32[4,1024]{1,0:T(4,128)S(1)} %fusion.107), channel_id=1, source_target_pairs={{0,2},{1,3},{2,0},{3,1},{4,6},{5,7},{6,4},{7,5},{8,10},{9,11},{10,... | collective-permute-start | bytes 49160 | tf_op jit(solution)/shard_map/ppermute | solution.py:364
  379.3 25.7 %collective-permute-start.22 = (bf16[1056,256]{1,0:T(8,128)(2,1)}, bf16[1056,256]{1,0:T(8,128)(2,1)S(1)}, u32[]{:S(2)}, u32[]{:S(2)}) collective-permute-start(bf16[1056,256]{1,0:T(8,128)(2,1)} %dynamic-slice_bitcast_fusion), channel_id=1, source_target_pairs={{0,8},{4,12},{8,0},{12,4},{16,24},{20,28},{24,16},{28,20},{1,9},{5... | collective-permute-start | bytes 1622024 | tf_op jit(solution)/shard_map/ppermute | solution.py:373
  385.2 19.9 %collective-permute-start.21 = (bf16[1024,256]{1,0:T(8,128)(2,1)}, bf16[1024,256]{1,0:T(8,128)(2,1)}, u32[]{:S(2)}, u32[]{:S(2)}) collective-permute-start(bf16[1024,256]{1,0:T(8,128)(2,1)} %dynamic-slice_bitcast_fusion.1), channel_id=1, source_target_pairs={{0,4},{4,0},{8,12},{12,8},{16,20},{20,16},{24,28},{28,24},{1,5},{5... | collective-permute-start | bytes 1572872 | tf_op jit(solution)/shard_map/ppermute | solution.py:373
  385.2 119.5 %collective-permute-start.27 = (bf16[512,1024]{1,0:T(8,128)(2,1)}, bf16[512,1024]{1,0:T(8,128)(2,1)}, u32[]{:S(2)}, u32[]{:S(2)}) collective-permute-start(bf16[512,1024]{1,0:T(8,128)(2,1)} %add_convert_fusion.3), channel_id=1, source_target_pairs={{0,3},{1,2},{2,1},{3,0},{4,7},{5,6},{6,5},{7,4},{8,11},{9,10},{10,... | collective-permute-start | bytes 3145736 | tf_op jit(solution)/shard_map/ppermute | solution.py:364
  418.4 86.9 %collective-permute-start.26 = (bf16[512,1024]{1,0:T(8,128)(2,1)}, bf16[512,1024]{1,0:T(8,128)(2,1)S(1)}, u32[]{:S(2)}, u32[]{:S(2)}) collective-permute-start(bf16[512,1024]{1,0:T(8,128)(2,1)} %get-tuple-element.149), channel_id=1, source_target_pairs={{0,1},{1,0},{2,3},{3,2},{4,5},{5,4},{6,7},{7,6},{8,9},{9,8},{10,11... | collective-permute-start | bytes 3145736 | tf_op jit(solution)/shard_map/ppermute | solution.py:364
  419.8 23.5 %collective-permute-start.33 = (bf16[528,256]{1,0:T(8,128)(2,1)S(1)}, bf16[528,256]{1,0:T(8,128)(2,1)S(1)}, u32[]{:S(2)}, u32[]{:S(2)}) collective-permute-start(bf16[528,256]{1,0:T(8,128)(2,1)S(1)} %dynamic-slice_bitcast_fusion.2), channel_id=1, source_target_pairs={{0,4},{4,0},{8,12},{12,8},{16,20},{20,16},{24,28},{28,24},{1,5},{5... | collective-permute-start | bytes 811016 | tf_op jit(solution)/shard_map/ppermute | solution.py:373
  421.5 21.5 %collective-permute-start.28 = (bf16[512,256]{1,0:T(8,128)(2,1)S(1)}, bf16[512,256]{1,0:T(8,128)(2,1)S(1)}, u32[]{:S(2)}, u32[]{:S(2)}) collective-permute-start(bf16[512,256]{1,0:T(8,128)(2,1)S(1)} %dynamic-slice_bitcast_fusion.3), channel_id=1, source_target_pairs={{0,8},{4,12},{8,0},{12,4},{16,24},{20,28},{24,16},{28,20},{1,9},{5... | collective-permute-start | bytes 786440 | tf_op jit(solution)/shard_map/ppermute | solution.py:373
  421.6 86.3 %collective-permute-start.24 = (bf16[512,1024]{1,0:T(8,128)(2,1)S(1)}, bf16[512,1024]{1,0:T(8,128)(2,1)S(1)}, u32[]{:S(2)}, u32[]{:S(2)}) collective-permute-start(bf16[512,1024]{1,0:T(8,128)(2,1)S(1)} %copy-done.42), channel_id=1, source_target_pairs={{0,1},{1,0},{2,3},{3,2},{4,5},{5,4},{6,7},{7,6},{8,9},{9,8},{10,11... | collective-permute-start | bytes 3145736 | tf_op jit(solution)/shard_map/ppermute | solution.py:364
  443.0 95.2 %collective-permute-start.23 = (bf16[512,1024]{1,0:T(8,128)(2,1)}, bf16[512,1024]{1,0:T(8,128)(2,1)}, u32[]{:S(2)}, u32[]{:S(2)}) collective-permute-start(bf16[512,1024]{1,0:T(8,128)(2,1)} %convolution_convert_fusion.2), channel_id=1, source_target_pairs={{0,1},{1,0},{2,3},{3,2},{4,5},{5,4},{6,7},{7,6},{8,9},{9,8},{10,11... | collective-permute-start | bytes 3145736 | tf_op jit(solution)/shard_map/ppermute | solution.py:364
  443.3 17.5 %collective-permute-start.29 = (bf16[256,256]{1,0:T(8,128)(2,1)S(1)}, bf16[256,256]{1,0:T(8,128)(2,1)S(1)}, u32[]{:S(2)}, u32[]{:S(2)}) collective-permute-start(bf16[256,256]{1,0:T(8,128)(2,1)S(1)} %dynamic-slice_bitcast_fusion.5), channel_id=1, source_target_pairs={{0,16},{4,20},{8,24},{12,28},{16,0},{20,4},{24,8},{28,12},{1,17},{... | collective-permute-start | bytes 393224 | tf_op jit(solution)/shard_map/ppermute | solution.py:373
  460.9 10.0 %collective-permute-start.34 = (bf16[264,256]{1,0:T(8,128)(2,1)S(1)}, bf16[264,256]{1,0:T(8,128)(2,1)S(1)}, u32[]{:S(2)}, u32[]{:S(2)}) collective-permute-start(bf16[264,256]{1,0:T(8,128)(2,1)S(1)} %dynamic-slice_bitcast_fusion.4), channel_id=1, source_target_pairs={{0,16},{4,20},{8,24},{12,28},{16,0},{20,4},{24,8},{28,12},{1,17},{... | collective-permute-start | bytes 405512 | tf_op jit(solution)/shard_map/ppermute | solution.py:373
  470.8 8.1 %collective-permute-start.30 = (bf16[256,256]{1,0:T(8,128)(2,1)S(1)}, bf16[256,256]{1,0:T(8,128)(2,1)S(1)}, u32[]{:S(2)}, u32[]{:S(2)}) collective-permute-start(bf16[256,256]{1,0:T(8,128)(2,1)S(1)} %fusion.82), channel_id=1, source_target_pairs={{0,16},{4,20},{8,24},{12,28},{16,0},{20,4},{24,8},{28,12},{1,17},{... | collective-permute-start | bytes 393224 | tf_op jit(solution)/shard_map/ppermute | solution.py:373
  478.9 9.0 %collective-permute-start.35 = (bf16[264,256]{1,0:T(8,128)(2,1)S(1)}, bf16[264,256]{1,0:T(8,128)(2,1)S(1)}, u32[]{:S(2)}, u32[]{:S(2)}) collective-permute-start(bf16[264,256]{1,0:T(8,128)(2,1)S(1)} %fusion.81), channel_id=1, source_target_pairs={{0,16},{4,20},{8,24},{12,28},{16,0},{20,4},{24,8},{28,12},{1,17},{... | collective-permute-start | bytes 405512 | tf_op jit(solution)/shard_map/ppermute | solution.py:373
  487.9 8.2 %collective-permute-start.31 = (bf16[512,256]{1,0:T(8,128)(2,1)S(1)}, bf16[512,256]{1,0:T(8,128)(2,1)S(1)}, u32[]{:S(2)}, u32[]{:S(2)}) collective-permute-start(bf16[512,256]{1,0:T(8,128)(2,1)S(1)} %pad_maximum_fusion.9), channel_id=1, source_target_pairs={{0,8},{4,12},{8,0},{12,4},{16,24},{20,28},{24,16},{28,20},{1,9},{5... | collective-permute-start | bytes 786440 | tf_op jit(solution)/shard_map/ppermute | solution.py:373
  496.1 7.6 %collective-permute-start.36 = (bf16[528,256]{1,0:T(8,128)(2,1)S(1)}, bf16[528,256]{1,0:T(8,128)(2,1)S(1)}, u32[]{:S(2)}, u32[]{:S(2)}) collective-permute-start(bf16[528,256]{1,0:T(8,128)(2,1)S(1)} %pad_maximum_fusion.8), channel_id=1, source_target_pairs={{0,4},{4,0},{8,12},{12,8},{16,20},{20,16},{24,28},{28,24},{1,5},{5... | collective-permute-start | bytes 811016 | tf_op jit(solution)/shard_map/ppermute | solution.py:373
  503.7 23.5 %collective-permute-start.32 = (bf16[1024,256]{1,0:T(8,128)(2,1)S(1)}, bf16[1024,256]{1,0:T(8,128)(2,1)S(1)}, u32[]{:S(2)}, u32[]{:S(2)}) collective-permute-start(bf16[1024,256]{1,0:T(8,128)(2,1)S(1)} %pad_maximum_fusion.7), channel_id=1, source_target_pairs={{0,4},{4,0},{8,12},{12,8},{16,20},{20,16},{24,28},{28,24},{1,5},{5... | collective-permute-start | bytes 1572872 | tf_op jit(solution)/shard_map/ppermute | solution.py:373
  504.7 23.7 %collective-permute-start.37 = (bf16[1056,256]{1,0:T(8,128)(2,1)S(1)}, bf16[1056,256]{1,0:T(8,128)(2,1)S(1)}, u32[]{:S(2)}, u32[]{:S(2)}) collective-permute-start(bf16[1056,256]{1,0:T(8,128)(2,1)S(1)} %pad_maximum_fusion.3), channel_id=1, source_target_pairs={{0,8},{4,12},{8,0},{12,4},{16,24},{20,28},{24,16},{28,20},{1,9},{5... | collective-permute-start | bytes 1622024 | tf_op jit(solution)/shard_map/ppermute | solution.py:373
  520.4 25.6 %collective-permute-start.25 = (bf16[512,1024]{1,0:T(8,128)(2,1)}, bf16[512,1024]{1,0:T(8,128)(2,1)}, u32[]{:S(2)}, u32[]{:S(2)}) collective-permute-start(bf16[512,1024]{1,0:T(8,128)(2,1)} %add_convert_fusion.2), channel_id=1, source_target_pairs={{0,3},{1,2},{2,1},{3,0},{4,7},{5,6},{6,5},{7,4},{8,11},{9,10},{10,... | collective-permute-start | bytes 3145736 | tf_op jit(solution)/shard_map/ppermute | solution.py:364
  (60 other events, 469.7 us)
Sparse Core Ops, SparseCore 0:
  240.2 87.7 reduce-scatter.1
  385.3 84.5 all-gather.1

commit v3 on v2

--- a/solution.py
+++ b/solution.py
@@ -477,9 +477,10 @@
     hb=half//BLK
     codes=block_codes(seg,slots,False)
     att_far,lse_far=attn_fwd(codes[hb:],q,k,v,segq,segk,hb,hb)
+    att_far,g2=lax.optimization_barrier((att_far,gm[2]))
     proj=lambda a: jnp.dot(a,w_proj,preferred_element_type=f32).astype(bf16)
     across=pair_sum(proj(att_far[tok:]),proj(att_far[:tok])).astype(bf16)
-    q_late,across,g2=lax.optimization_barrier((q,across,gm[2]))
+    q_late,across=lax.optimization_barrier((q,across))
     gm=[gm[0],gm[1],g2,flip(g2,1)]
     across=flip(across,3)
     att_near,lse_near=attn_fwd(codes[:hb],q_late,k,v,segq,segk,0,hb)
@@ -514,27 +515,26 @@
     ghead=lambda a: lax.dot_general(a,w_proj,NT,preferred_element_type=f32).astype(bf16)
     bcodes=block_codes(seg,slots,True)
     do_near=jnp.concatenate([ghead(grad_attn),ghead(near)],axis=0)
+    gq_near,dk,dv,bs0=attn_bwd(bcodes[:hb],q,k,v,do_near,att_near,lse_near,segq,segk,cos,sin,0,None)
     early=jnp.stack([grad_gain_two,grad_shift_two,jnp.sum(grad_attn,axis=0,dtype=f32),jnp.sum(grad_mlp,axis=0,dtype=f32)])
+    far,dk,dv,early=lax.optimization_barrier((far,dk,dv,early))
     early=early+flip(early,1)
     early=early+flip(early,2)
-    do_near,early=lax.optimization_barrier((do_near,early))
-    gq_near,dk,dv,bs0=attn_bwd(bcodes[:hb],q,k,v,do_near,att_near,lse_near,segq,segk,cos,sin,0,None)
-    far,dk,dv=lax.optimization_barrier((far,dk,dv))
     far_pair=flip(far,1)
     do_far=jnp.concatenate([ghead(far),ghead(far_pair)],axis=0)
     alla=jnp.concatenate([grad_attn,near,far,far_pair],axis=0)
     grad_proj=tn(jnp.concatenate([att_near,att_far],axis=0),alla).astype(bf16)
-    do_far,grad_proj=lax.optimization_barrier((do_far,grad_proj))
+    do_far,grad_proj,early=lax.optimization_barrier((do_far,grad_proj,early))
     gq_far,gk,gv,bs1=attn_bwd(bcodes[hb:],q,k,v,do_far,att_far,lse_far,segq,segk,cos,sin,1,(dk,dv))
     gk,wsum=lax.optimization_barrier((gk,wsum))
     wsum=lax.all_gather(wsum,"dp",axis=0,tiled=True)
-    grad_w1,grad_w2=wsum[:tokens.shape[1]],wsum[tokens.shape[1]:]
     r2,r3=back_rows(gq_far,gk,gv,w_qkv,1)
     across=pair_sum(r3,r2).astype(bf16)
     gq_near,gk,gv,across,early=lax.optimization_barrier((gq_near,gk,gv,across,early))
     across=flip(across,3)
     g_all=jnp.concatenate([jnp.concatenate([gq_near,gq_far],axis=0),gk,gv],axis=1)
     grad_wqkv=tn(jnp.concatenate(n1,axis=0),g_all).astype(bf16)
+    grad_wqkv,hid,gq_near=lax.optimization_barrier((grad_wqkv,hid,gq_near))
     d=tokens.shape[1]
     sizes=(3*cols,db.shape[1],early.size)
     pad=(-sum(sizes))%(8*cols<<bits)
@@ -543,23 +543,41 @@
     tail_b=DpSum(jnp.concatenate([grad_wqkv[:,2*cols:],grad_proj.reshape(-1,cols),small],axis=0),(1,0)+tuple(range(2,bits)))
     tails=(tail_a,tail_b)
     for t in tails: t.start(t.operand())
-    *gots,hid,gq_near=lax.optimization_barrier((tail_a.got,tail_b.got,hid,gq_near))
+    *gots,across=lax.optimization_barrier((tail_a.got,tail_b.got,across))
     for t,got in zip(tails,gots): t.finish(got)
-    tail_a,tail_b=[t.rest() for t in tails]
     r0,r1=back_rows(gq_near,gk,gv,w_qkv,0)
     mine=pair_sum(r0,r1)
+    grad_x_norm,grad_gain_one,grad_shift_one=norm_one_back(mine+across.astype(f32))
+    one=jnp.stack([grad_gain_one,grad_shift_one])
     o=[jnp.dot(hid[j*tok:(j+1)*tok],w_fc2,preferred_element_type=f32).astype(bf16) for j in range(ranks)]
     o_across=flip(pair_sum(o[3],o[2]).astype(bf16),3)
+    for t in tails: t.start(t.operand())
+    one,*gots=lax.optimization_barrier((one,tail_a.got,tail_b.got))
+    for t,got in zip(tails,gots): t.finish(got)
+    hops=[partial(dp_flip,bit=bit) for bit in range(bits)]+[partial(flip,bits=1),partial(flip,bits=2)]
+    while hops or tail_a.at<len(tail_a.stages):
+        busy=[t for t in tails if t.at<len(t.stages)]
+        for t in busy: t.start(t.operand())
+        hop=hops.pop(0) if hops else None
+        other=hop(one) if hop else one
+        third=bool(busy) and busy[0].at==bits-1
+        gots=[t.got for t in busy]
+        if third:
+            other,o_across,wsum,*gots=lax.optimization_barrier((other,o_across,wsum,*gots))
+        else:
+            other,*gots=lax.optimization_barrier((other,*gots))
+        for t,got in zip(busy,gots): t.finish(got)
+        one=one+other if hop else one
+    tail_a,tail_b=tail_a.cur,tail_b.cur
     output=(resid_one+pair_sum(o[0],o[1])+o_across.astype(f32)+shifts[3]).astype(bf16)
+    grad_w1,grad_w2=wsum[:d],wsum[d:]
     grad_wqkv=jnp.stack([tail_a[:d],tail_a[d:],tail_b[:d]]).astype(f32)
     grad_wproj=tail_b[d:2*d].reshape(cols,d).astype(f32)
     small=tail_b[2*d:].reshape(-1).astype(f32)
     grad_bqkv=small[:sizes[0]].reshape(3,cols)
     grad_b1=small[sizes[0]:sizes[0]+sizes[1]]
     early=small[sizes[0]+sizes[1]:sum(sizes)].reshape(4,d)
-    grad_x_norm,grad_gain_one,grad_shift_one=norm_one_back(mine+across.astype(f32))
     grad_tokens=(grad_resid_one+grad_x_norm).astype(bf16)
-    one=all_sum(jnp.stack([grad_gain_one,grad_shift_one]))
     return (output,grad_tokens,grad_wqkv,grad_bqkv,grad_wproj,grad_w1.astype(f32),grad_b1,grad_w2.astype(f32),
             jnp.stack([one[0],early[0]]),jnp.stack([one[1],early[1],early[2],early[3]]))
 

time: 574 us -> 492 us (0.86)
  waiting for transfers between devices: 201 us -> 115 us
  starting transfers between devices: 29.5 us -> 40.1 us
    ppermute x28, waiting for transfers between devices: 101 us -> 52.2 us  [flip(): return lax.ppermute(x, 'tensor', [(i, i ^ bits) for i in range(n)])]
    ppermute x15, waiting for transfers between devices: 99.8 us -> 61.8 us  [dp_flip(): return lax.ppermute(x, 'dp', [(i, i ^ 1 << bit) for i in range(n)])]
    ppermute x28, starting transfers between devices: 18.2 us -> 25.3 us  [flip(): return lax.ppermute(x, 'tensor', [(i, i ^ bits) for i in range(n)])]
  transfers between devices with their start and end apart: 45 -> 45, of which waited for: 26 -> 22; matrix products, arithmetic and copies ran while one was open for 16% -> 20% of each run, Pallas kernels for 24% -> 36%
where the time goes in v3:
time: 492 us; the launch traced here: 482 us
  Pallas kernels  197 us (40%)
  waiting for transfers between devices  115 us (23%)
  other arithmetic  57.3 us (12%)
  matrix products  45.3 us (9%)
  starting transfers between devices  40.1 us (8%)
  between operations  15.5 us (3%)
  local copies, waits for them, and re-layouts  11.3 us (2%)
    pallas_call x2, Pallas kernels, attn_bwd(): pl.pallas_call(partial(attn_bwd_kernel, last), out_shape=(jax.ShapeDtypeS...  75.6 us
    pallas_call x2, Pallas kernels, attn_fwd(): pl.pallas_call(attn_fwd_kernel, out_shape=(jax.ShapeDtypeStruct((nblocks...  75 us
    ppermute x15, waiting for transfers between devices, dp_flip(): return lax.ppermute(x, 'dp', [(i, i ^ 1 << bit) for i in range(n)])  61.8 us
    ppermute x28, waiting for transfers between devices, flip(): return lax.ppermute(x, 'tensor', [(i, i ^ bits) for i in range(n)])  52.2 us
    ppermute x28, starting transfers between devices, flip(): return lax.ppermute(x, 'tensor', [(i, i ^ bits) for i in range(n)])  25.3 us
    dot_general x4, matrix products, shards(): lax.dot_general(a, b, (((0,), (0,)), ((), ())), preferred_element_type=f32)  25.1 us
    pallas_call x2, Pallas kernels, mlp_rows(): pl.pallas_call(partial(mlp_kernel, n), grid=(2 * n,), out_shape=[jax.Shap...  24.5 us
    ppermute x15, starting transfers between devices, dp_flip(): return lax.ppermute(x, 'dp', [(i, i ^ 1 << bit) for i in range(n)])  14.5 us
  transfers between devices with their start and end apart: 45, of which 22 were waited for; matrix products, arithmetic and copies ran while one was open for 20% of the time, Pallas kernels for 36%

profile of v3, /device:TPU:0, one launch (start us, length us, event | category | flops | bytes accessed | tf_op | source)
XLA Modules:
  0.0 482.0 jit_solution(8651291016929549424)
XLA Ops:
  16.0 5.8 %sine_multiply_fusion = (f32[2048,128]{1,0:T(8,128)}, f32[2048,128]{1,0:T(8,128)}) fusion(f32[128]{0:T(128)S(1)} %get-tuple-element.261, f32[128]{0:T(128)S(1)} %get-tuple-element.262, f32[2048]{0:T(1024)S(1)} %bitcast.131, f32[128]{0:T(128)S(1)} %get-tuple-element.263, f32[2048]{0:T(1024)S(1)} %bitcast.130, f32[128]{0:T(128)S(1)} %get-tuple-element.264, ...), kind=kLoop, calls=%fused_computation.108 | loop fusion | flops 1572864 | bytes 2123776 | tf_op jit(solution)/shard_map/mul | solution.py:456
  22.7 5.5 %qkv.2 = (bf16[2048,256]{1,0:T(8,128)(2,1)}, bf16[2048,256]{1,0:T(8,128)(2,1)}, bf16[2048,256]{1,0:T(8,128)(2,1)}) custom-call(bf16[512,1024]{1,0:T(8,128)(2,1)} %copy-done.17, bf16[512,1024]{1,0:T(8,128)(2,1)} %copy-done.40, bf16[3,1024,256]{2,1,0:T(8,128)(2,1)} %w_ref.7, f32[3,256]{1,0:T(4,128)} %convert_element_type.290.b_ref, ...), custom_call_target="tpu_custom_call" | custom-call | flops 5368709120 | tf_op jit(solution)/shard_map/qkv/pallas_call | solution.py:266
  28.3 10.4 %collective-permute-done.xa_ref = bf16[512,1024]{1,0:T(8,128)(2,1)} collective-permute-done((bf16[512,1024]{1,0:T(8,128)(2,1)S(1)}, bf16[512,1024]{1,0:T(8,128)(2,1)}, u32[]{:S(2)}, u32[]{:S(2)}) %collective-permute-start) | collective-permute-done | bytes 1048608 | tf_op jit(solution)/shard_map/ppermute | solution.py:364
  44.2 5.5 %qkv.3 = (bf16[2048,256]{1,0:T(8,128)(2,1)}, bf16[2048,256]{1,0:T(8,128)(2,1)}, bf16[2048,256]{1,0:T(8,128)(2,1)}) custom-call(bf16[512,1024]{1,0:T(8,128)(2,1)} %collective-permute-done.xa_ref, bf16[512,1024]{1,0:T(8,128)(2,1)} %copy-done.41, bf16[3,1024,256]{2,1,0:T(8,128)(2,1)} %w_ref.7, ...), custom_call_target="tpu_custom_call", output_to_operand_aliasing={{0}: (6, {}), {1}: (7, {}), {2}: (8, {})} | custom-call | flops 5368709120 | tf_op jit(solution)/shard_map/qkv/pallas_call | solution.py:266
  51.4 35.1 %attn_fwd.2 = (bf16[1024,256]{1,0:T(8,128)(2,1)}, f32[8,1024]{1,0:T(8,128)}) custom-call(s32[4,8]{1,0:T(4,128)} %get-tuple-element.256.codes, bf16[2048,256]{1,0:T(8,128)(2,1)} %get-tuple-element.119.q_ref, bf16[2048,256]{1,0:T(8,128)(2,1)} %get-tuple-element.113.k_ref, bf16[2048,256]{1,0:T(8,128)(2,1)} %get-tuple-element.114.v_ref, s32[1,2048]{1,0:T(1,128)} %bitcast.119, ...), custom_call_target="tpu_custom_call" | custom-call | flops 34359738368 | tf_op jit(solution)/shard_map/attn_fwd/pallas_call | solution.py:83
  92.0 5.1 %collective-permute-start.5 = (bf16[512,1024]{1,0:T(8,128)(2,1)S(1)}, bf16[512,1024]{1,0:T(8,128)(2,1)S(1)}, u32[]{:S(2)}, u32[]{:S(2)}) collective-permute-start(bf16[512,1024]{1,0:T(8,128)(2,1)S(1)} %add_convert_fusion.6), channel_id=1, source_target_pairs={{0,3},{1,2},{2,1},{3,0},{4,7},{5,6},{6,5},{7,4},{8,11},{9,10},{10,... | collective-permute-start | bytes 3145736 | tf_op jit(solution)/shard_map/ppermute | solution.py:364
  97.1 39.9 %attn_fwd.3 = (bf16[1024,256]{1,0:T(8,128)(2,1)}, f32[8,1024]{1,0:T(8,128)}) custom-call(s32[4,8]{1,0:T(4,128)} %get-tuple-element.255.codes, bf16[2048,256]{1,0:T(8,128)(2,1)} %get-tuple-element.119.q_ref, bf16[2048,256]{1,0:T(8,128)(2,1)} %get-tuple-element.113.k_ref, bf16[2048,256]{1,0:T(8,128)(2,1)} %get-tuple-element.114.v_ref, s32[1,2048]{1,0:T(1,128)} %bitcast.120, ...), custom_call_target="tpu_custom_call" | custom-call | flops 34359738368 | tf_op jit(solution)/shard_map/attn_fwd/pallas_call | solution.py:83
  148.2 12.4 %mlp.2 = (bf16[2048,1024]{1,0:T(8,128)(2,1)}, bf16[2048,1024]{1,0:T(8,128)(2,1)}, bf16[512,1024]{1,0:T(8,128)(2,1)}, bf16[512,1024]{1,0:T(8,128)(2,1)}, f32[1,1024]{1,0:T(1,128)}) custom-call(bf16[512,1024]{1,0:T(8,128)(2,1)} %add_convert_fusion.5.xa_ref, bf16[512,1024]{1,0:T(8,128)(2,1)} %collective-permute-done.7.xb_ref, ...), custom_call_target="tpu_custom_call" | custom-call | flops 6442450944 | tf_op jit(solution)/shard_map/mlp/pallas_call | solution.py:310
  160.6 10.5 %collective-permute-done.10.xa_ref = bf16[512,1024]{1,0:T(8,128)(2,1)} collective-permute-done((bf16[512,1024]{1,0:T(8,128)(2,1)}, bf16[512,1024]{1,0:T(8,128)(2,1)}, u32[]{:S(2)}, u32[]{:S(2)}) %collective-permute-start.10) | collective-permute-done | bytes 1048608 | tf_op jit(solution)/shard_map/ppermute | solution.py:364
  174.1 12.1 %mlp.3 = (bf16[2048,1024]{1,0:T(8,128)(2,1)}, bf16[2048,1024]{1,0:T(8,128)(2,1)}, bf16[512,1024]{1,0:T(8,128)(2,1)}, bf16[512,1024]{1,0:T(8,128)(2,1)}, f32[1,1024]{1,0:T(1,128)}) custom-call(bf16[512,1024]{1,0:T(8,128)(2,1)} %collective-permute-done.10.xa_ref, ...), custom_call_target="tpu_custom_call", output_to_operand_aliasing={{0}: (7, {}), {1}: (8, {})} | custom-call | flops 6442450944 | tf_op jit(solution)/shard_map/mlp/pallas_call | solution.py:310
  190.9 8.1 %fusion.53 = bf16[1024,1024]{1,0:T(8,128)(2,1)S(1)} fusion(bf16[2048,1024]{1,0:T(8,128)(2,1)} %get-tuple-element.161, bf16[512,1024]{1,0:T(8,128)(2,1)} %collective-permute-done.12.gb_ref, bf16[512,1024]{1,0:T(8,128)(2,1)} %collective-permute-done.3.ga_ref, bf16[512,1024]{1,0:T(8,128)(2,1)} %collective-permute-done.8.gb_ref, ...), kind=kOutput, calls=%fused_computation.77 | convolution fusion | flops 4312793088 | bytes 10485760 | tf_op jit(solution)/shard_map/dot_general | solution.py:504
  199.0 6.8 %fusion.56 = bf16[1024,1024]{1,0:T(8,128)(2,1)S(1)} fusion(bf16[2048,1024]{1,0:T(8,128)(2,1)S(1)} %copy-done.46, bf16[512,1024]{1,0:T(8,128)(2,1)} %collective-permute-done.11.xb_ref, bf16[512,1024]{1,0:T(8,128)(2,1)} %collective-permute-done.10.xa_ref, bf16[512,1024]{1,0:T(8,128)(2,1)} %collective-permute-done.7.xb_ref, ...), kind=kOutput, calls=%fused_computation.78 | convolution fusion | flops 4312793088 | bytes 10485760 | tf_op jit(solution)/shard_map/dot_general | solution.py:504
  205.8 10.3 %collective-permute-done.14 = bf16[512,1024]{1,0:T(8,128)(2,1)} collective-permute-done((bf16[512,1024]{1,0:T(8,128)(2,1)S(1)}, bf16[512,1024]{1,0:T(8,128)(2,1)}, u32[]{:S(2)}, u32[]{:S(2)}) %collective-permute-start.14) | collective-permute-done | bytes 1048608 | tf_op jit(solution)/shard_map/ppermute | solution.py:364
  233.0 39.1 %attn_bwd.2 = (bf16[1024,256]{1,0:T(8,128)(2,1)}, f32[2048,256]{1,0:T(8,128)}, f32[2048,256]{1,0:T(8,128)}, f32[8,256]{1,0:T(8,128)}) custom-call(s32[4,8]{1,0:T(4,128)} %get-tuple-element.252.codes, bf16[2048,256]{1,0:T(8,128)(2,1)} %get-tuple-element.119.q_ref, bf16[2048,256]{1,0:T(8,128)(2,1)} %get-tuple-element.113.k_ref, ...), custom_call_target="tpu_custom_call" | custom-call | flops 1 | tf_op jit(solution)/shard_map/attn_bwd/pallas_call | solution.py:206
  281.3 3.6 fusion.64
  284.9 36.5 %attn_bwd.3 = (bf16[1024,256]{1,0:T(8,128)(2,1)}, bf16[2048,256]{1,0:T(8,128)(2,1)}, bf16[2048,256]{1,0:T(8,128)(2,1)}, f32[8,256]{1,0:T(8,128)}) custom-call(s32[4,8]{1,0:T(4,128)} %get-tuple-element.251.codes, bf16[2048,256]{1,0:T(8,128)(2,1)} %get-tuple-element.119.q_ref, bf16[2048,256]{1,0:T(8,128)(2,1)} %get-tuple-element.113.k_ref, ...), custom_call_target="tpu_custom_call" | custom-call | flops 1 | tf_op jit(solution)/shard_map/attn_bwd/pallas_call | solution.py:206
  321.4 5.6 %back.2 = (bf16[512,1024]{1,0:T(8,128)(2,1)}, bf16[512,1024]{1,0:T(8,128)(2,1)}) custom-call(bf16[1024,256]{1,0:T(8,128)(2,1)} %get-tuple-element.154.gq_ref, bf16[2048,256]{1,0:T(8,128)(2,1)} %get-tuple-element.159.gk_ref, bf16[2048,256]{1,0:T(8,128)(2,1)} %get-tuple-element.160.gv_ref, bf16[3,1024,256]{2,1,0:T(8,128)(2,1)} %w_ref.7), custom_call_target="tpu_custom_call" | custom-call | flops 1 | tf_op jit(solution)/shard_map/back/pallas_call | solution.py:343
  333.1 6.6 %fusion.59 = bf16[1024,768]{1,0:T(8,128)(2,1)S(1)} fusion(bf16[2048,256]{1,0:T(8,128)(2,1)} %get-tuple-element.160.gv_ref, bf16[2048,256]{1,0:T(8,128)(2,1)} %get-tuple-element.159.gk_ref, bf16[1024,256]{1,0:T(8,128)(2,1)} %get-tuple-element.154.gq_ref, bf16[1024,256]{1,0:T(8,128)(2,1)} %get-tuple-element.162.gq_ref, bf16[512,1024]{1,0:T(8,128)(2,1)} %copy-done.41, ...), kind=kOutput, calls=%fused_computation.79 | convolution fusion | flops 3251372032 | bytes 8912896 | tf_op jit(solution)/shard_map/dot_general | solution.py:504
  341.7 6.9 %collective-permute-start.25 = (bf16[512,1024]{1,0:T(8,128)(2,1)}, bf16[512,1024]{1,0:T(8,128)(2,1)}, u32[]{:S(2)}, u32[]{:S(2)}) collective-permute-start(bf16[512,1024]{1,0:T(8,128)(2,1)} %add_convert_fusion.3), channel_id=1, source_target_pairs={{0,3},{1,2},{2,1},{3,0},{4,7},{5,6},{6,5},{7,4},{8,11},{9,10},{10,... | collective-permute-start | bytes 3145736 | tf_op jit(solution)/shard_map/ppermute | solution.py:364
  356.1 5.6 %back.3 = (bf16[512,1024]{1,0:T(8,128)(2,1)}, bf16[512,1024]{1,0:T(8,128)(2,1)}) custom-call(bf16[1024,256]{1,0:T(8,128)(2,1)} %get-tuple-element.162.gq_ref, bf16[2048,256]{1,0:T(8,128)(2,1)} %get-tuple-element.159.gk_ref, bf16[2048,256]{1,0:T(8,128)(2,1)} %get-tuple-element.160.gv_ref, bf16[3,1024,256]{2,1,0:T(8,128)(2,1)} %w_ref.7), custom_call_target="tpu_custom_call" | custom-call | flops 1 | tf_op jit(solution)/shard_map/back/pallas_call | solution.py:343
  362.3 9.0 %collective-permute-done.24 = bf16[1056,256]{1,0:T(8,128)(2,1)S(1)} collective-permute-done((bf16[1056,256]{1,0:T(8,128)(2,1)}, bf16[1056,256]{1,0:T(8,128)(2,1)S(1)}, u32[]{:S(2)}, u32[]{:S(2)}) %collective-permute-start.24) | collective-permute-done | bytes 540704 | tf_op jit(solution)/shard_map/ppermute | solution.py:373
  377.1 3.1 add_convert_fusion.2
  384.4 16.2 %collective-permute-done.26 = bf16[512,256]{1,0:T(8,128)(2,1)S(1)} collective-permute-done((bf16[512,256]{1,0:T(8,128)(2,1)S(1)}, bf16[512,256]{1,0:T(8,128)(2,1)S(1)}, u32[]{:S(2)}, u32[]{:S(2)}) %collective-permute-start.26) | collective-permute-done | bytes 262176 | tf_op jit(solution)/shard_map/ppermute | solution.py:373
  404.1 3.6 fusion.109
  407.7 20.8 %collective-permute-done.31 = bf16[256,256]{1,0:T(8,128)(2,1)S(1)} collective-permute-done((bf16[256,256]{1,0:T(8,128)(2,1)S(1)}, bf16[256,256]{1,0:T(8,128)(2,1)S(1)}, u32[]{:S(2)}, u32[]{:S(2)}) %collective-permute-start.31) | collective-permute-done | bytes 131104 | tf_op jit(solution)/shard_map/ppermute | solution.py:373
  433.0 3.6 collective-permute-done.33
  436.6 6.0 %collective-permute-done.34 = bf16[256,256]{1,0:T(8,128)(2,1)S(1)} collective-permute-done((bf16[256,256]{1,0:T(8,128)(2,1)S(1)}, bf16[256,256]{1,0:T(8,128)(2,1)S(1)}, u32[]{:S(2)}, u32[]{:S(2)}) %collective-permute-start.34) | collective-permute-done | bytes 131104 | tf_op jit(solution)/shard_map/ppermute | solution.py:373
  444.2 3.0 collective-permute-start.36
  447.2 3.3 add_convert_fusion
  454.3 4.4 slice_convert_fusion
  458.8 3.3 add_convert_fusion.1
  462.1 4.3 collective-permute-done.40
  (285 shorter events, 114.3 us)
Async XLA Ops:
  7.3 314.1 %reduce-scatter.2.cloned.1.call-start = ((), (), s32[]{:S(2)}) async-start(), calls=%async_computation.1 | async-start | bytes 4718592 | tf_op jit(solution)/shard_map/reduce_scatter | solution.py:508
  11.7 10.0 %collective-permute-start.1 = (bf16[512,1024]{1,0:T(8,128)(2,1)S(1)}, bf16[512,1024]{1,0:T(8,128)(2,1)S(1)}, u32[]{:S(2)}, u32[]{:S(2)}) collective-permute-start(bf16[512,1024]{1,0:T(8,128)(2,1)S(1)} %fusion.46.xa_ref), channel_id=1, source_target_pairs={{0,1},{1,0},{2,3},{3,2},{4,5},{5,4},{6,7},{7,6},{8,9},{9,8},{10,11... | collective-permute-start | bytes 3145736 | tf_op jit(solution)/shard_map/ppermute | solution.py:364
  12.2 26.4 %collective-permute-start = (bf16[512,1024]{1,0:T(8,128)(2,1)S(1)}, bf16[512,1024]{1,0:T(8,128)(2,1)}, u32[]{:S(2)}, u32[]{:S(2)}) collective-permute-start(bf16[512,1024]{1,0:T(8,128)(2,1)S(1)} %fusion.46.xa_ref), channel_id=1, source_target_pairs={{0,2},{1,3},{2,0},{3,1},{4,6},{5,7},{6,4},{7,5},{8,10},{9,11},{10,... | collective-permute-start | bytes 3145736 | tf_op jit(solution)/shard_map/ppermute | solution.py:364
  38.6 4.6 collective-permute-start.2
  49.7 36.8 %collective-permute-start.3 = (bf16[512,1024]{1,0:T(8,128)(2,1)}, bf16[512,1024]{1,0:T(8,128)(2,1)}, u32[]{:S(2)}, u32[]{:S(2)}) collective-permute-start(bf16[512,1024]{1,0:T(8,128)(2,1)} %get-tuple-element.116.ga_ref), channel_id=1, source_target_pairs={{0,2},{1,3},{2,0},{3,1},{4,6},{5,7},{6,4},{7,5},{8,10},{9,11},{10,... | collective-permute-start | bytes 3145736 | tf_op jit(solution)/shard_map/ppermute | solution.py:364
  92.0 45.0 %collective-permute-start.5 = (bf16[512,1024]{1,0:T(8,128)(2,1)S(1)}, bf16[512,1024]{1,0:T(8,128)(2,1)S(1)}, u32[]{:S(2)}, u32[]{:S(2)}) collective-permute-start(bf16[512,1024]{1,0:T(8,128)(2,1)S(1)} %add_convert_fusion.6), channel_id=1, source_target_pairs={{0,3},{1,2},{2,1},{3,0},{4,7},{5,6},{6,5},{7,4},{8,11},{9,10},{10,... | collective-permute-start | bytes 3145736 | tf_op jit(solution)/shard_map/ppermute | solution.py:364
  139.1 7.2 %collective-permute-start.8 = (bf16[512,1024]{1,0:T(8,128)(2,1)}, bf16[512,1024]{1,0:T(8,128)(2,1)}, u32[]{:S(2)}, u32[]{:S(2)}) collective-permute-start(bf16[512,1024]{1,0:T(8,128)(2,1)} %get-tuple-element.116.ga_ref), channel_id=1, source_target_pairs={{0,1},{1,0},{2,3},{3,2},{4,5},{5,4},{6,7},{7,6},{8,9},{9,8},{10,11... | collective-permute-start | bytes 3145736 | tf_op jit(solution)/shard_map/ppermute | solution.py:364
  145.5 25.6 %collective-permute-start.10 = (bf16[512,1024]{1,0:T(8,128)(2,1)}, bf16[512,1024]{1,0:T(8,128)(2,1)}, u32[]{:S(2)}, u32[]{:S(2)}) collective-permute-start(bf16[512,1024]{1,0:T(8,128)(2,1)} %add_convert_fusion.5.xa_ref), channel_id=1, source_target_pairs={{0,2},{1,3},{2,0},{3,1},{4,6},{5,7},{6,4},{7,5},{8,10},{9,11},{10,... | collective-permute-start | bytes 3145736 | tf_op jit(solution)/shard_map/ppermute | solution.py:364
  146.1 25.0 %collective-permute-start.12 = (bf16[512,1024]{1,0:T(8,128)(2,1)}, bf16[512,1024]{1,0:T(8,128)(2,1)}, u32[]{:S(2)}, u32[]{:S(2)}) collective-permute-start(bf16[512,1024]{1,0:T(8,128)(2,1)} %collective-permute-done.3.ga_ref), channel_id=1, source_target_pairs={{0,1},{1,0},{2,3},{3,2},{4,5},{5,4},{6,7},{7,6},{8,9},{9,8},{10,11... | collective-permute-start | bytes 3145736 | tf_op jit(solution)/shard_map/ppermute | solution.py:364
  190.8 25.3 %collective-permute-start.14 = (bf16[512,1024]{1,0:T(8,128)(2,1)S(1)}, bf16[512,1024]{1,0:T(8,128)(2,1)}, u32[]{:S(2)}, u32[]{:S(2)}) collective-permute-start(bf16[512,1024]{1,0:T(8,128)(2,1)S(1)} %add_convert_fusion.4), channel_id=1, source_target_pairs={{0,3},{1,2},{2,1},{3,0},{4,7},{5,6},{6,5},{7,4},{8,11},{9,10},{10,... | collective-permute-start | bytes 3145736 | tf_op jit(solution)/shard_map/ppermute | solution.py:364
  218.6 211.2 %all-gather.2.cloned.1.call-start = ((), (), s32[]{:S(2)}) async-start(), calls=%async_computation.2 | async-start | bytes 4718592 | tf_op jit(solution)/shard_map/all_gather | solution.py:530
  228.9 43.2 %collective-permute-start.16 = (bf16[512,1024]{1,0:T(8,128)(2,1)}, bf16[512,1024]{1,0:T(8,128)(2,1)}, u32[]{:S(2)}, u32[]{:S(2)}) collective-permute-start(bf16[512,1024]{1,0:T(8,128)(2,1)} %get-tuple-element.205), channel_id=1, source_target_pairs={{0,2},{1,3},{2,0},{3,1},{4,6},{5,7},{6,4},{7,5},{8,10},{9,11},{10,... | collective-permute-start | bytes 3145736 | tf_op jit(solution)/shard_map/ppermute | solution.py:364
  272.1 7.8 %collective-permute-start.17 = (bf16[512,1024]{1,0:T(8,128)(2,1)}, bf16[512,1024]{1,0:T(8,128)(2,1)S(1)}, u32[]{:S(2)}, u32[]{:S(2)}) collective-permute-start(bf16[512,1024]{1,0:T(8,128)(2,1)} %collective-permute-done.16), channel_id=1, source_target_pairs={{0,1},{1,0},{2,3},{3,2},{4,5},{5,4},{6,7},{7,6},{8,9},{9,8},{10,11... | collective-permute-start | bytes 3145736 | tf_op jit(solution)/shard_map/ppermute | solution.py:364
  340.8 30.6 %collective-permute-start.24 = (bf16[1056,256]{1,0:T(8,128)(2,1)}, bf16[1056,256]{1,0:T(8,128)(2,1)S(1)}, u32[]{:S(2)}, u32[]{:S(2)}) collective-permute-start(bf16[1056,256]{1,0:T(8,128)(2,1)} %dynamic-slice_bitcast_fusion), channel_id=1, source_target_pairs={{0,8},{4,12},{8,0},{12,4},{16,24},{20,28},{24,16},{28,20},{1,9},{5... | collective-permute-start | bytes 1622024 | tf_op jit(solution)/shard_map/ppermute | solution.py:373
  341.7 20.1 %collective-permute-start.23 = (bf16[1024,256]{1,0:T(8,128)(2,1)}, bf16[1024,256]{1,0:T(8,128)(2,1)}, u32[]{:S(2)}, u32[]{:S(2)}) collective-permute-start(bf16[1024,256]{1,0:T(8,128)(2,1)} %dynamic-slice_bitcast_fusion.1), channel_id=1, source_target_pairs={{0,4},{4,0},{8,12},{12,8},{16,20},{20,16},{24,28},{28,24},{1,5},{5... | collective-permute-start | bytes 1572872 | tf_op jit(solution)/shard_map/ppermute | solution.py:373
  341.7 30.8 %collective-permute-start.25 = (bf16[512,1024]{1,0:T(8,128)(2,1)}, bf16[512,1024]{1,0:T(8,128)(2,1)}, u32[]{:S(2)}, u32[]{:S(2)}) collective-permute-start(bf16[512,1024]{1,0:T(8,128)(2,1)} %add_convert_fusion.3), channel_id=1, source_target_pairs={{0,3},{1,2},{2,1},{3,0},{4,7},{5,6},{6,5},{7,4},{8,11},{9,10},{10,... | collective-permute-start | bytes 3145736 | tf_op jit(solution)/shard_map/ppermute | solution.py:364
  353.1 23.9 %collective-permute-start.29 = (bf16[512,1024]{1,0:T(8,128)(2,1)}, bf16[512,1024]{1,0:T(8,128)(2,1)}, u32[]{:S(2)}, u32[]{:S(2)}) collective-permute-start(bf16[512,1024]{1,0:T(8,128)(2,1)} %convolution_convert_fusion), channel_id=1, source_target_pairs={{0,1},{1,0},{2,3},{3,2},{4,5},{5,4},{6,7},{7,6},{8,9},{9,8},{10,11... | collective-permute-start | bytes 3145736 | tf_op jit(solution)/shard_map/ppermute | solution.py:364
  361.7 20.1 %collective-permute-start.22 = (bf16[512,1024]{1,0:T(8,128)(2,1)}, bf16[512,1024]{1,0:T(8,128)(2,1)S(1)}, u32[]{:S(2)}, u32[]{:S(2)}) collective-permute-start(bf16[512,1024]{1,0:T(8,128)(2,1)} %get-tuple-element.164), channel_id=1, source_target_pairs={{0,1},{1,0},{2,3},{3,2},{4,5},{5,4},{6,7},{7,6},{8,9},{9,8},{10,11... | collective-permute-start | bytes 3145736 | tf_op jit(solution)/shard_map/ppermute | solution.py:364
  361.8 97.0 %collective-permute-start.21 = (bf16[512,1024]{1,0:T(8,128)(2,1)}, bf16[512,1024]{1,0:T(8,128)(2,1)}, u32[]{:S(2)}, u32[]{:S(2)}) collective-permute-start(bf16[512,1024]{1,0:T(8,128)(2,1)} %convolution_convert_fusion.2), channel_id=1, source_target_pairs={{0,1},{1,0},{2,3},{3,2},{4,5},{5,4},{6,7},{7,6},{8,9},{9,8},{10,11... | collective-permute-start | bytes 3145736 | tf_op jit(solution)/shard_map/ppermute | solution.py:364
  373.7 26.9 %collective-permute-start.27 = (bf16[528,256]{1,0:T(8,128)(2,1)S(1)}, bf16[528,256]{1,0:T(8,128)(2,1)S(1)}, u32[]{:S(2)}, u32[]{:S(2)}) collective-permute-start(bf16[528,256]{1,0:T(8,128)(2,1)S(1)} %dynamic-slice_bitcast_fusion.2), channel_id=1, source_target_pairs={{0,4},{4,0},{8,12},{12,8},{16,20},{20,16},{24,28},{28,24},{1,5},{5... | collective-permute-start | bytes 811016 | tf_op jit(solution)/shard_map/ppermute | solution.py:373
  376.6 24.0 %collective-permute-start.26 = (bf16[512,256]{1,0:T(8,128)(2,1)S(1)}, bf16[512,256]{1,0:T(8,128)(2,1)S(1)}, u32[]{:S(2)}, u32[]{:S(2)}) collective-permute-start(bf16[512,256]{1,0:T(8,128)(2,1)S(1)} %dynamic-slice_bitcast_fusion.3), channel_id=1, source_target_pairs={{0,8},{4,12},{8,0},{12,4},{16,24},{20,28},{24,16},{28,20},{1,9},{5... | collective-permute-start | bytes 786440 | tf_op jit(solution)/shard_map/ppermute | solution.py:373
  380.2 48.3 %collective-permute-start.30 = (bf16[512,1024]{1,0:T(8,128)(2,1)S(1)}, bf16[512,1024]{1,0:T(8,128)(2,1)}, u32[]{:S(2)}, u32[]{:S(2)}) collective-permute-start(bf16[512,1024]{1,0:T(8,128)(2,1)S(1)} %add_convert_fusion.2), channel_id=1, source_target_pairs={{0,3},{1,2},{2,1},{3,0},{4,7},{5,6},{6,5},{7,4},{8,11},{9,10},{10,... | collective-permute-start | bytes 3145736 | tf_op jit(solution)/shard_map/ppermute | solution.py:364
  400.7 27.8 %collective-permute-start.32 = (bf16[264,256]{1,0:T(8,128)(2,1)S(1)}, bf16[264,256]{1,0:T(8,128)(2,1)S(1)}, u32[]{:S(2)}, u32[]{:S(2)}) collective-permute-start(bf16[264,256]{1,0:T(8,128)(2,1)S(1)} %dynamic-slice_bitcast_fusion.4), channel_id=1, source_target_pairs={{0,16},{4,20},{8,24},{12,28},{16,0},{20,4},{24,8},{28,12},{1,17},{... | collective-permute-start | bytes 405512 | tf_op jit(solution)/shard_map/ppermute | solution.py:373
  401.3 27.2 %collective-permute-start.31 = (bf16[256,256]{1,0:T(8,128)(2,1)S(1)}, bf16[256,256]{1,0:T(8,128)(2,1)S(1)}, u32[]{:S(2)}, u32[]{:S(2)}) collective-permute-start(bf16[256,256]{1,0:T(8,128)(2,1)S(1)} %dynamic-slice_bitcast_fusion.5), channel_id=1, source_target_pairs={{0,16},{4,20},{8,24},{12,28},{16,0},{20,4},{24,8},{28,12},{1,17},{... | collective-permute-start | bytes 393224 | tf_op jit(solution)/shard_map/ppermute | solution.py:373
  429.8 12.8 %collective-permute-start.35 = (bf16[264,256]{1,0:T(8,128)(2,1)S(1)}, bf16[264,256]{1,0:T(8,128)(2,1)S(1)}, u32[]{:S(2)}, u32[]{:S(2)}) collective-permute-start(bf16[264,256]{1,0:T(8,128)(2,1)S(1)} %fusion.81), channel_id=1, source_target_pairs={{0,16},{4,20},{8,24},{12,28},{16,0},{20,4},{24,8},{28,12},{1,17},{... | collective-permute-start | bytes 405512 | tf_op jit(solution)/shard_map/ppermute | solution.py:373
  430.0 12.7 %collective-permute-start.34 = (bf16[256,256]{1,0:T(8,128)(2,1)S(1)}, bf16[256,256]{1,0:T(8,128)(2,1)S(1)}, u32[]{:S(2)}, u32[]{:S(2)}) collective-permute-start(bf16[256,256]{1,0:T(8,128)(2,1)S(1)} %fusion.82), channel_id=1, source_target_pairs={{0,16},{4,20},{8,24},{12,28},{16,0},{20,4},{24,8},{28,12},{1,17},{... | collective-permute-start | bytes 393224 | tf_op jit(solution)/shard_map/ppermute | solution.py:373
  442.7 9.6 %collective-permute-start.38 = (bf16[528,256]{1,0:T(8,128)(2,1)S(1)}, bf16[528,256]{1,0:T(8,128)(2,1)S(1)}, u32[]{:S(2)}, u32[]{:S(2)}) collective-permute-start(bf16[528,256]{1,0:T(8,128)(2,1)S(1)} %pad_maximum_fusion.8), channel_id=1, source_target_pairs={{0,4},{4,0},{8,12},{12,8},{16,20},{20,16},{24,28},{28,24},{1,5},{5... | collective-permute-start | bytes 811016 | tf_op jit(solution)/shard_map/ppermute | solution.py:373
  444.1 8.2 %collective-permute-start.37 = (bf16[512,256]{1,0:T(8,128)(2,1)S(1)}, bf16[512,256]{1,0:T(8,128)(2,1)S(1)}, u32[]{:S(2)}, u32[]{:S(2)}) collective-permute-start(bf16[512,256]{1,0:T(8,128)(2,1)S(1)} %pad_maximum_fusion.9), channel_id=1, source_target_pairs={{0,8},{4,12},{8,0},{12,4},{16,24},{20,28},{24,16},{28,20},{1,9},{5... | collective-permute-start | bytes 786440 | tf_op jit(solution)/shard_map/ppermute | solution.py:373
  444.2 6.4 %collective-permute-start.36 = (f32[2,1024]{1,0:T(2,128)S(1)}, f32[2,1024]{1,0:T(2,128)S(1)}, u32[]{:S(2)}, u32[]{:S(2)}) collective-permute-start(f32[2,1024]{1,0:T(2,128)S(1)} %add.347), channel_id=1, source_target_pairs={{0,16},{4,20},{8,24},{12,28},{16,0},{20,4},{24,8},{28,12},{1,17},{... | collective-permute-start | bytes 24584 | tf_op jit(solution)/shard_map/ppermute | solution.py:373
  452.4 14.0 %collective-permute-start.41 = (bf16[1056,256]{1,0:T(8,128)(2,1)S(1)}, bf16[1056,256]{1,0:T(8,128)(2,1)S(1)}, u32[]{:S(2)}, u32[]{:S(2)}) collective-permute-start(bf16[1056,256]{1,0:T(8,128)(2,1)S(1)} %pad_maximum_fusion.3), channel_id=1, source_target_pairs={{0,8},{4,12},{8,0},{12,4},{16,24},{20,28},{24,16},{28,20},{1,9},{5... | collective-permute-start | bytes 1622024 | tf_op jit(solution)/shard_map/ppermute | solution.py:373
  454.0 12.5 %collective-permute-start.40 = (bf16[1024,256]{1,0:T(8,128)(2,1)S(1)}, bf16[1024,256]{1,0:T(8,128)(2,1)S(1)}, u32[]{:S(2)}, u32[]{:S(2)}) collective-permute-start(bf16[1024,256]{1,0:T(8,128)(2,1)S(1)} %pad_maximum_fusion.7), channel_id=1, source_target_pairs={{0,4},{4,0},{8,12},{12,8},{16,20},{20,16},{24,28},{28,24},{1,5},{5... | collective-permute-start | bytes 1572872 | tf_op jit(solution)/shard_map/ppermute | solution.py:373
  467.3 6.2 %collective-permute-start.42 = (f32[2,1024]{1,0:T(2,128)S(1)}, f32[2,1024]{1,0:T(2,128)S(1)}, u32[]{:S(2)}, u32[]{:S(2)}) collective-permute-start(f32[2,1024]{1,0:T(2,128)S(1)} %add.349), channel_id=1, source_target_pairs={{0,2},{1,3},{2,0},{3,1},{4,6},{5,7},{6,4},{7,5},{8,10},{9,11},{10,... | collective-permute-start | bytes 24584 | tf_op jit(solution)/shard_map/ppermute | solution.py:364
  (60 other events, 407.8 us)
Sparse Core Ops, SparseCore 0:
  218.7 87.8 reduce-scatter.1
  327.3 102.4 all-gather.1
